TPU v7x, 256 devices: a whole 4x4x8 slice. The times are simulated.
256 devices in a mesh: dp: 64 (over z_hi, x, y, core), mp: 4 (over z_lo).
Axes of the slice: x: 4, y: 4, z: 8 (z_hi: 2, z_lo: 4; z = z_hi * 4 + z_lo), core: 2. Of those that a mesh axis runs over, the one named last changes fastest.
Arguments:
- hidden_acts: bfloat16 [98304, 1024], P('dp'), may hold values from -7168 to 7168
- out_grads: bfloat16 [98304, 8192], P('dp', 'mp'), may hold values from -6 to 6
- token_counts: int32 [64], P('dp'), may hold values from 1 to 1536, as said below
- down_weight: bfloat16 [1024, 8192], P(None, 'mp'), may hold values from -0.0625 to 0.0625
- owner_map: int32 [64], replicated, may hold values from 0 to 63, each once
- master: float32 [1024, 8192], P('dp', 'mp'), may hold values from -0.046875 to 0.046875
- moment1: float32 [1024, 8192], P('dp', 'mp'), may hold values from -6 to 6
- moment2: bfloat16 [1024, 8192], P('dp', 'mp'), may hold values from 0.099609375 to 10
Outputs:
- master_new: float32 [1024, 8192], P('dp', 'mp')
- moment1_new: float32 [1024, 8192], P('dp', 'mp')
- moment2_new: bfloat16 [1024, 8192], P('dp', 'mp')
- weights_new: bfloat16 [1024, 8192], P(None, 'mp')
- input_grads: bfloat16 [98304, 1024], P('dp', 'mp')
Inputs may be any that keep to these rules, and one draw needn't show every extreme that they name: `token_counts`: the last worker is always full; the others hold from about a third to all of their 1536 slots, rising along the workers.
All inputs are finite; a program needn't handle non-finite values.
Results may differ from a plain program's by a relative error of at most 0.0026.
Values may be sent and summed in bfloat16 or wider, within the bound.
No kernel may reach another device: no remote copies, remote signals or barrier semaphores. Data moves between devices by JAX's collectives and lax.ppermute only.
A program may use at most 128 MiB of HBM per device.

v0:
```python
import jax
import jax.numpy as jnp
from jax import lax
from jax.experimental import pallas as pl
from jax.experimental.pallas import tpu as pltpu
from jax.sharding import PartitionSpec as P


beta_one = 0.9
beta_two = 0.95
learn_rate = 0.0003
epsilon = 1e-08
correct_one = 1.0 - 0.9**50
correct_two = 1.0 - 0.95**50


ZH, X, Y, CORE = 2, 4, 4, 2
f32, bf16, i16 = jnp.float32, jnp.bfloat16, jnp.int16
DIGITS = 6
EXTRA = 128
GROUP = 32


def index_of(zh, x, y, core):
    return ((zh * X + x) * Y + y) * CORE + core


def move(value, to):
    pairs = [
        (index_of(z, x, y, c), index_of(*to(z, x, y, c)))
        for z in range(ZH)
        for x in range(X)
        for y in range(Y)
        for c in range(CORE)
    ]
    return lax.ppermute(value, "dp", pairs)


def to_core(value):
    return move(value, lambda z, x, y, c: (z, x, y, 1 - c))


def to_zh(value):
    return move(value, lambda z, x, y, c: (1 - z, x, y, c))


def shift(value, ring, by):
    if ring == "x":
        return move(value, lambda z, x, y, c: (z, (x + by) % X, y, c))
    return move(value, lambda z, x, y, c: (z, x, (y + by) % Y, c))


def relative_slot(position, me):
    core, zh, first, second = position // 32, (position // 16) % 2, (position // 4) % 4, position % 4
    far_x, far_y = (second, first) if zh else (first, second)
    x = lax.rem(lax.div(me, 8) + far_x, 4)
    y = lax.rem(lax.div(me, 2) + far_y, 4)
    my_zh, my_core = lax.div(me, 32), lax.rem(me, 2)
    return index_of(1 - my_zh if zh else my_zh, x, y, 1 - my_core if core else my_core)


def weight_partials(acts, grads, count, owner_map, me, interpret=False):
    tokens, hidden = acts.shape
    columns = grads.shape[1]
    blocks = owner_map.shape[0]
    height = hidden // blocks
    wide = 512
    steps = columns // wide
    near = blocks // 2
    chunk = 512
    parts = tokens // chunk

    def kernel(count_ref, map_ref, me_ref, acts_ref, grads_ref, keep_ref, send_ref, raw, turned, part, sems):
        step = pl.program_id(0)

        def put():
            for p in range(blocks):
                start = pl.multiple_of(map_ref[relative_slot(p, me_ref[0])] * height, height)
                out = keep_ref if p < near else send_ref
                out[p % near] = part[pl.ds(start, height), :].astype(bf16)

        @pl.when(step == 0)
        def _():
            loads = [
                pltpu.make_async_copy(
                    acts_ref.at[pl.ds(i * chunk, chunk)], raw.at[pl.ds(i * chunk, chunk)], sems.at[i]
                )
                for i in range(parts)
            ]
            for load in loads:
                load.start()
            for i, load in enumerate(loads):
                rows = pl.ds(i * chunk, chunk)
                load.wait()
                live = lax.broadcasted_iota(jnp.int32, (1, chunk), 1) + i * chunk < count_ref[0]
                flipped = raw[rows, :].T * jnp.where(live, 1.0, 0.0).astype(bf16)
                turned[:, rows] = flipped
                value = jnp.dot(flipped, grads_ref[rows, :], preferred_element_type=f32)
                if i == 0:
                    part[...] = value
                else:
                    part[...] += value
            put()

        @pl.when((step > 0) & (step < steps))
        def _():
            part[...] = jnp.dot(turned[...], grads_ref[...], preferred_element_type=f32)
            put()

        @pl.when(step == steps)
        def _():
            lane = lax.broadcasted_iota(jnp.int32, (near, height, EXTRA), 2)
            digit = (count_ref[0] >> jnp.minimum(2 * lane, 30)) & 3
            value = digit.astype(f32).astype(bf16)
            keep_ref[:, :, :EXTRA] = value
            send_ref[:, :, :EXTRA] = value

    out = jax.ShapeDtypeStruct((near, height, columns + EXTRA), bf16)
    spec = pl.BlockSpec((near, height, wide), lambda n: (0, 0, n))
    return pl.pallas_call(
        kernel,
        grid=(steps + 1,),
        out_shape=(out, out),
        in_specs=[pl.BlockSpec(memory_space=pltpu.SMEM)] * 3
        + [
            pl.BlockSpec(memory_space=pl.ANY),
            pl.BlockSpec((tokens, wide), lambda n: (0, jnp.minimum(n, steps - 1))),
        ],
        out_specs=(spec, spec),
        scratch_shapes=[
            pltpu.VMEM((tokens, hidden), bf16),
            pltpu.VMEM((hidden, tokens), bf16),
            pltpu.VMEM((hidden, wide), f32),
            pltpu.SemaphoreType.DMA((parts,)),
        ],
        compiler_params=pltpu.CompilerParams(vmem_limit_bytes=60 * 2**20),
        interpret=interpret,
    )(count, owner_map, me, acts, grads)


def input_shares(grads, weight, count, mine, ways, interpret=False):
    tokens, columns = grads.shape
    hidden = weight.shape[0]
    width = hidden // ways
    tall = 256
    groups = tall // GROUP
    extra = 16

    def kernel(count_ref, mine_ref, grads_ref, weight_ref, own_ref, *refs):
        coded, held, sems = refs[:-2], refs[-2], refs[-1]
        step = pl.program_id(0)
        live = lax.broadcasted_iota(jnp.int32, (tall, width), 0) + step * tall < count_ref[0]
        order = (*range(1, ways), 0)

        def load(offset):
            at = lax.rem(mine_ref[0] + offset, ways) * width
            return pltpu.make_async_copy(
                weight_ref.at[pl.ds(pl.multiple_of(at, width), width)], held.at[offset], sems.at[offset]
            )

        @pl.when(step == 0)
        def _():
            for offset in order:
                load(offset).start()

        for offset in order:

            @pl.when(step == 0)
            def _(offset=offset):
                load(offset).wait()

            share = lax.dot_general(
                grads_ref[...], held[offset], (((1,), (1,)), ((), ())), preferred_element_type=f32
            )
            share = jnp.where(live, share, 0.0)
            if offset == 0:
                own_ref[...] = share
                continue
            out = coded[offset - 1]
            largest = jnp.max(jnp.abs(share).reshape(groups, GROUP, width), axis=1)
            largest = jnp.max(largest, axis=1, keepdims=True)
            power = jnp.floor(jnp.log2(32000.0 / jnp.maximum(largest, 1e-25)))
            power = jnp.broadcast_to(jnp.minimum(power, 90.0), (groups, width))
            factor = jnp.exp2(power)
            for g in range(groups):
                code = jnp.round(share[g * GROUP : (g + 1) * GROUP] * factor[g : g + 1])
                out[0, g * GROUP : (g + 1) * GROUP, :] = code.astype(jnp.int32).astype(i16)
            power = jnp.concatenate([power] * (extra // groups), axis=0)
            out[0, tall : tall + extra, :] = power.astype(jnp.int32).astype(i16)

    code = jax.ShapeDtypeStruct((tokens // tall, tall + extra, width), i16)
    return pl.pallas_call(
        kernel,
        grid=(tokens // tall,),
        out_shape=(jax.ShapeDtypeStruct((tokens, width), f32),) + (code,) * (ways - 1),
        in_specs=[pl.BlockSpec(memory_space=pltpu.SMEM)] * 2
        + [
            pl.BlockSpec((tall, columns), lambda n: (n, 0)),
            pl.BlockSpec(memory_space=pl.ANY),
        ],
        out_specs=(pl.BlockSpec((tall, width), lambda n: (n, 0)),)
        + (pl.BlockSpec((1, tall + extra, width), lambda n: (n, 0, 0)),) * (ways - 1),
        scratch_shapes=[pltpu.VMEM((ways, width, columns), bf16), pltpu.SemaphoreType.DMA((ways,))],
        compiler_params=pltpu.CompilerParams(vmem_limit_bytes=60 * 2**20),
        interpret=interpret,
    )(count, mine, grads, weight)


def add_shares(own, coded, interpret=False):
    tokens, width = own.shape
    steps, padded, _ = coded[0].shape
    tall = tokens // steps
    groups = tall // GROUP

    def kernel(own_ref, *refs):
        out = refs[-1]

        def add(step, carry):
            base = pl.multiple_of(step * tall, tall)
            factors = [
                jnp.exp2(-ref[step, tall:padded, :].astype(jnp.int32).astype(f32))
                for ref in refs[:-1]
            ]
            for g in range(groups):
                rows = pl.ds(base + g * GROUP, GROUP)
                value = own_ref[rows, :]
                for ref, factor in zip(refs[:-1], factors):
                    code = ref[step, g * GROUP : (g + 1) * GROUP, :]
                    value += code.astype(jnp.int32).astype(f32) * factor[g : g + 1]
                out[rows, :] = value.astype(bf16)
            return carry

        lax.fori_loop(0, steps, add, 0)

    whole = pl.BlockSpec(memory_space=pltpu.VMEM)
    return pl.pallas_call(
        kernel,
        out_shape=jax.ShapeDtypeStruct((tokens, width), bf16),
        in_specs=[whole] * (1 + len(coded)),
        out_specs=whole,
        compiler_params=pltpu.CompilerParams(vmem_limit_bytes=12 * 2**20),
        interpret=interpret,
    )(own, *coded)


def place_blocks(pieces, owner_map, me, interpret=False):
    counts = [piece.shape[0] for piece in pieces]
    shape = (sum(counts), *pieces[0].shape[1:])

    def source_slot(position, me):
        core, zh, second, first = position // 32, (position // 16) % 2, (position // 4) % 4, position % 4
        far_x, far_y = (second, first) if zh else (first, second)
        x = lax.rem(lax.div(me, 8) + 4 - far_x, 4)
        y = lax.rem(lax.div(me, 2) + 4 - far_y, 4)
        my_zh, my_core = lax.div(me, 32), lax.rem(me, 2)
        return index_of(1 - my_zh if zh else my_zh, x, y, 1 - my_core if core else my_core)

    def kernel(map_ref, me_ref, *refs):
        sources, out, sent = refs[: len(pieces)], *refs[len(pieces) :]
        at = 0
        for source, count in zip(sources, counts):
            for b in range(count):
                row = map_ref[source_slot(at + b, me_ref[0])]
                pltpu.make_async_copy(source.at[b], out.at[row], sent).start()
            at += count
        pltpu.make_async_copy(out, out, sent).wait()

    return pl.pallas_call(
        kernel,
        out_shape=jax.ShapeDtypeStruct(shape, bf16),
        in_specs=[pl.BlockSpec(memory_space=pltpu.SMEM)] * 2
        + [pl.BlockSpec(memory_space=pltpu.VMEM)] * len(pieces),
        out_specs=pl.BlockSpec(memory_space=pl.ANY),
        scratch_shapes=[pltpu.SemaphoreType.DMA],
        compiler_params=pltpu.CompilerParams(vmem_limit_bytes=12 * 2**20),
        interpret=interpret,
    )(owner_map, me, *pieces)


def per_device(
    hidden_acts, out_grads, token_counts, down_weight, owner_map, master, moment1, moment2
):
    columns = out_grads.shape[1]
    hidden = hidden_acts.shape[1]
    me = lax.axis_index("dp").astype(jnp.int32).reshape(1)
    my_mp = lax.axis_index("mp").astype(jnp.int32).reshape(1)
    ways = lax.axis_size("mp")
    rings = (("x", "y"), ("y", "x"))

    def pass_share(coded, offset):
        ring = [(source, (source + offset) % ways) for source in range(ways)]
        return lax.ppermute(coded[offset - 1], "mp", ring)

    keep, send = weight_partials(hidden_acts, out_grads, token_counts, owner_map, me)
    arrived = to_core(send)
    out_grads, keep = lax.optimization_barrier((out_grads, keep))
    own, *coded = input_shares(out_grads, down_weight, token_counts, my_mp, ways)
    arrived, own = lax.optimization_barrier((arrived, own))
    shares = [pass_share(coded, 1), pass_share(coded, 3)]

    pair = [
        (keep[4 * i : 4 * i + 4].astype(f32) + arrived[4 * i : 4 * i + 4].astype(f32)).astype(bf16)
        for i in range(8)
    ]
    got = [
        [shift(pair[4 * colour + d], first, d) for d in (2, 1, 3)]
        for colour, (first, _) in enumerate(rings)
    ]
    got = lax.optimization_barrier(got)
    lines = [
        [
            sum((g[e].astype(f32) for g in got[colour]), pair[4 * colour][e].astype(f32)).astype(bf16)
            for e in range(4)
        ]
        for colour in range(2)
    ]
    got = [
        [shift(line[d], second, d) for d in (2, 1, 3)] for line, (_, second) in zip(lines, rings)
    ]
    got = lax.optimization_barrier(got)
    sums = [
        sum((g.astype(f32) for g in group), line[0].astype(f32)) for group, line in zip(got, lines)
    ]
    summed = sums[0] + to_zh(sums[1])

    digits = summed[0, columns : columns + DIGITS]
    total = jnp.sum(digits * (4.0 ** jnp.arange(DIGITS, dtype=f32)))
    grad = summed[:, :columns] / total
    moment1_new = beta_one * moment1 + (1.0 - beta_one) * grad
    second = beta_two * moment2.astype(f32) + (1.0 - beta_two) * grad * grad
    moment2_new = second.astype(bf16)
    master_new = master - learn_rate * (moment1_new / correct_one) / (
        jnp.sqrt(second / correct_two) + epsilon
    )

    weights = master_new.astype(bf16)[None]
    other = to_zh(weights)
    shares.append(pass_share(coded, 2))
    pieces = []
    for part, (first, second) in zip((weights, other), rings):
        line = jnp.concatenate([part] + [shift(part, first, d) for d in (1, 2, 3)])
        pieces += [line] + [shift(line, second, d) for d in (1, 2, 3)]
    pieces += [to_core(piece) for piece in pieces]
    input_grads = add_shares(own, shares)
    weights_new = place_blocks(pieces, owner_map, me).reshape(hidden, columns)
    return (master_new, moment1_new, moment2_new, weights_new, input_grads)


def solution(mesh):
    in_specs = (
        P("dp", None),
        P("dp", "mp"),
        P("dp"),
        P(None, "mp"),
        P(),
        P("dp", "mp"),
        P("dp", "mp"),
        P("dp", "mp"),
    )
    out_specs = (P("dp", "mp"), P("dp", "mp"), P("dp", "mp"), P(None, "mp"), P("dp", "mp"))
    return jax.shard_map(per_device, mesh=mesh, in_specs=in_specs, out_specs=out_specs, check_vma=False)
```

profile of v0, /device:TPU:1, one launch (start us, length us, event | category | flops | bytes accessed | tf_op | source)
XLA Modules:
  0.0 189.2 jit_solution(7844067408213943362)
XLA Ops:
  1.3 12.3 %shard_map.119 = (bf16[32,16,2176]{2,1,0:T(8,128)(2,1)}, bf16[32,16,2176]{2,1,0:T(8,128)(2,1)}) custom-call(s32[1]{0:T(128)S(6)} %copy.16.count_ref, s32[64]{0:T(128)} %map_ref.3, s32[1]{0:T(128)} %bitcast.me_ref, bf16[1536,1024]{1,0:T(8,128)(2,1)} %acts_ref.1, bf16[1536,2048]{1,0:T(8,128)(2,1)} %grads_ref.2), custom_call_target="tpu_custom_call" | custom-call | tf_op jit(solution)/shard_map/pallas_call | solution.py:120
  13.6 3.3 %collective-permute-start = (bf16[32,16,2176]{2,1,0:T(8,128)(2,1)}, bf16[32,16,2176]{2,1,0:T(8,128)(2,1)}, u32[]{:S(2)}, u32[]{:S(2)}) collective-permute-start(bf16[32,16,2176]{2,1,0:T(8,128)(2,1)} %get-tuple-element.29), channel_id=1, source_target_pairs={{0,4},{4,0},{8,12},{12,8},{16,20},{20,16},{24,28},{28,24},{32,36},... | collective-permute-start | bytes 6684680 | tf_op jit(solution)/shard_map/ppermute | solution.py:36
  16.9 23.3 %shard_map.120 = (f32[1536,256]{1,0:T(8,128)}, s16[6,272,256]{2,1,0:T(8,128)(2,1)}, s16[6,272,256]{2,1,0:T(8,128)(2,1)}, s16[6,272,256]{2,1,0:T(8,128)(2,1)}) custom-call(s32[1]{0:T(128)S(6)} %copy.16.count_ref, s32[1]{0:T(128)} %bitcast.1.mine_ref, bf16[1536,2048]{1,0:T(8,128)(2,1)} %grads_ref.2, bf16[1024,2048]{1,0:T(8,128)(2,1)} %weight_ref.1), custom_call_target="tpu_custom_call" | custom-call | tf_op jit(solution)/shard_map/pallas_call | solution.py:192
  40.3 2.1 %add_convert_fusion = (bf16[4,16,2176]{2,1,0:T(8,128)(2,1)S(1)}, bf16[4,16,2176]{2,1,0:T(8,128)(2,1)S(1)}, bf16[4,16,2176]{2,1,0:T(8,128)(2,1)S(1)}, bf16[4,16,2...) fusion(bf16[32,16,2176]{2,1,0:T(8,128)(2,1)} %collective-permut, ...), kind=kLoop, calls=%fused_computation | loop fusion | flops 4456448 | bytes 6684672 | tf_op jit(solution)/shard_map/convert_element_type | solution.py:302
  45.2 2.5 %collective-permute-start.3 = (bf16[4,16,2176]{2,1,0:T(8,128)(2,1)S(1)}, bf16[4,16,2176]{2,1,0:T(8,128)(2,1)S(1)}, u32[]{:S(2)}, u32[]{:S(2)}) collective-permute-start(bf16[4,16,2176]{2,1,0:T(8,128)(2,1)S(1)} %get-tuple-element.56), channel_id=1, source_target_pairs={{0,96},{4,100},{8,104},{12,108},{16,112},{20,116},{24,120},{28,124... | collective-permute-start | bytes 835592 | tf_op jit(solution)/shard_map/ppermute | solution.py:36
  47.7 3.0 %collective-permute-done.6 = bf16[4,16,2176]{2,1,0:T(8,128)(2,1)S(1)} collective-permute-done((bf16[4,16,2176]{2,1,0:T(8,128)(2,1)S(1)}, bf16[4,16,2176]{2,1,0:T(8,128)(2,1)S(1)}, u32[]{:S(2)}, u32[]{:S(2)}) %collective-permute-start.6) | collective-permute-done | bytes 278560 | tf_op jit(solution)/shard_map/ppermute | solution.py:36
  50.7 7.4 %collective-permute-start.1 = (bf16[4,16,2176]{2,1,0:T(8,128)(2,1)S(1)}, bf16[4,16,2176]{2,1,0:T(8,128)(2,1)S(1)}, u32[]{:S(2)}, u32[]{:S(2)}) collective-permute-start(bf16[4,16,2176]{2,1,0:T(8,128)(2,1)S(1)} %get-tuple-element.58), channel_id=1, source_target_pairs={{0,64},{4,68},{8,72},{12,76},{16,80},{20,84},{24,88},{28,92},{32,9... | collective-permute-start | bytes 835592 | tf_op jit(solution)/shard_map/ppermute | solution.py:36
  58.6 5.4 %collective-permute-done.1 = bf16[4,16,2176]{2,1,0:T(8,128)(2,1)S(1)} collective-permute-done((bf16[4,16,2176]{2,1,0:T(8,128)(2,1)S(1)}, bf16[4,16,2176]{2,1,0:T(8,128)(2,1)S(1)}, u32[]{:S(2)}, u32[]{:S(2)}) %collective-permute-start.1) | collective-permute-done | bytes 278560 | tf_op jit(solution)/shard_map/ppermute | solution.py:36
  64.2 3.8 %collective-permute-start.9 = (bf16[16,2176]{1,0:T(8,128)(2,1)S(1)}, bf16[16,2176]{1,0:T(8,128)(2,1)S(1)}, u32[]{:S(2)}, u32[]{:S(2)}) collective-permute-start(bf16[16,2176]{1,0:T(8,128)(2,1)S(1)} %get-tuple-element.63), channel_id=1, source_target_pairs={{0,24},{4,28},{8,0},{12,4},{16,8},{20,12},{24,16},{28,20},{32,56},... | collective-permute-start | bytes 208904 | tf_op jit(solution)/shard_map/ppermute | solution.py:36
  68.0 1.3 collective-permute-start.7
  69.4 2.7 %collective-permute-start.12 = (bf16[16,2176]{1,0:T(8,128)(2,1)S(1)}, bf16[16,2176]{1,0:T(8,128)(2,1)S(1)}, u32[]{:S(2)}, u32[]{:S(2)}) collective-permute-start(bf16[16,2176]{1,0:T(8,128)(2,1)S(1)} %get-tuple-element.60), channel_id=1, source_target_pairs={{0,96},{4,100},{8,104},{12,108},{16,112},{20,116},{24,120},{28,124... | collective-permute-start | bytes 208904 | tf_op jit(solution)/shard_map/ppermute | solution.py:36
  72.1 1.7 collective-permute-start.10
  73.8 3.4 %collective-permute-done.11 = bf16[16,2176]{1,0:T(8,128)(2,1)S(1)} collective-permute-done((bf16[16,2176]{1,0:T(8,128)(2,1)S(1)}, bf16[16,2176]{1,0:T(8,128)(2,1)S(1)}, u32[]{:S(2)}, u32[]{:S(2)}) %collective-permute-start.11) | collective-permute-done | bytes 69664 | tf_op jit(solution)/shard_map/ppermute | solution.py:36
  77.3 7.0 %collective-permute-start.13 = (f32[16,2176]{1,0:T(8,128)S(1)}, f32[16,2176]{1,0:T(8,128)S(1)}, u32[]{:S(2)}, u32[]{:S(2)}) collective-permute-start(f32[16,2176]{1,0:T(8,128)S(1)} %fusion.1), channel_id=1, source_target_pairs={{0,128},{4,132},{8,136},{12,140},{16,144},{20,148},{24,152},{28,15... | collective-permute-start | bytes 417800 | tf_op jit(solution)/shard_map/ppermute | solution.py:36
  85.0 2.5 %collective-permute-start.36 = (s16[6,272,256]{2,1,0:T(8,128)(2,1)S(1)}, s16[6,272,256]{2,1,0:T(8,128)(2,1)S(1)}, u32[]{:S(2)}, u32[]{:S(2)}) collective-permute-start(s16[6,272,256]{2,1,0:T(8,128)(2,1)S(1)} %copy-done.7), channel_id=1, source_target_pairs={{0,3},{1,0},{2,1},{3,2},{4,7},{5,4},{6,5},{7,6},{8,11},{9,8},{10,9... | collective-permute-start | bytes 2506760 | tf_op jit(solution)/shard_map/ppermute | solution.py:292
  88.2 1.5 convert_bitcast_fusion
  89.7 5.5 %collective-permute-start.20 = (bf16[1,16,2048]{2,1,0:T(8,128)(2,1)S(1)}, bf16[1,16,2048]{2,1,0:T(8,128)(2,1)S(1)}, u32[]{:S(2)}, u32[]{:S(2)}) collective-permute-start(bf16[1,16,2048]{2,1,0:T(8,128)(2,1)S(1)} %get-tuple-element.49), channel_id=1, source_target_pairs={{0,128},{4,132},{8,136},{12,140},{16,144},{20,148},{24,152},{28,15... | collective-permute-start | bytes 196616 | tf_op jit(solution)/shard_map/ppermute | solution.py:36
  95.2 2.3 %collective-permute-start.16 = (bf16[1,16,2048]{2,1,0:T(8,128)(2,1)S(1)}, bf16[1,16,2048]{2,1,0:T(8,128)(2,1)S(1)}, u32[]{:S(2)}, u32[]{:S(2)}) collective-permute-start(bf16[1,16,2048]{2,1,0:T(8,128)(2,1)S(1)} %get-tuple-element.49), channel_id=1, source_target_pairs={{0,96},{4,100},{8,104},{12,108},{16,112},{20,116},{24,120},{28,124... | collective-permute-start | bytes 196616 | tf_op jit(solution)/shard_map/ppermute | solution.py:36
  97.5 28.4 %collective-permute-done.20 = bf16[1,16,2048]{2,1,0:T(8,128)(2,1)S(1)} collective-permute-done((bf16[1,16,2048]{2,1,0:T(8,128)(2,1)S(1)}, bf16[1,16,2048]{2,1,0:T(8,128)(2,1)S(1)}, u32[]{:S(2)}, u32[]{:S(2)}) %collective-permute-start.20) | collective-permute-done | bytes 65568 | tf_op jit(solution)/shard_map/ppermute | solution.py:36
  126.0 1.5 collective-permute-start.23
  127.5 2.7 %collective-permute-done.14 = bf16[1,16,2048]{2,1,0:T(8,128)(2,1)S(1)} collective-permute-done((bf16[1,16,2048]{2,1,0:T(8,128)(2,1)S(1)}, bf16[1,16,2048]{2,1,0:T(8,128)(2,1)S(1)}, u32[]{:S(2)}, u32[]{:S(2)}) %collective-permute-start.14) | collective-permute-done | bytes 65568 | tf_op jit(solution)/shard_map/ppermute | solution.py:36
  130.2 1.9 collective-permute-start.21
  132.1 2.4 %collective-permute-done.21 = bf16[1,16,2048]{2,1,0:T(8,128)(2,1)S(1)} collective-permute-done((bf16[1,16,2048]{2,1,0:T(8,128)(2,1)S(1)}, bf16[1,16,2048]{2,1,0:T(8,128)(2,1)S(1)}, u32[]{:S(2)}, u32[]{:S(2)}) %collective-permute-start.21) | collective-permute-done | bytes 65568 | tf_op jit(solution)/shard_map/ppermute | solution.py:36
  135.5 8.1 %collective-permute-start.27 = (bf16[4,16,2048]{2,1,0:T(8,128)(2,1)S(1)}, bf16[4,16,2048]{2,1,0:T(8,128)(2,1)S(1)}, u32[]{:S(2)}, u32[]{:S(2)}) collective-permute-start(bf16[4,16,2048]{2,1,0:T(8,128)(2,1)S(1)} %pad_maximum_fusion.refs_0_), channel_id=1, source_target_pairs={{0,4},{4,0},{8,12},{12,8},{16,20},{20,16},{24,28},{28,24},{32,36},... | collective-permute-start | bytes 786440 | tf_op jit(solution)/shard_map/ppermute | solution.py:36
  143.6 2.3 %collective-permute-start.19 = (bf16[4,16,2048]{2,1,0:T(8,128)(2,1)S(1)}, bf16[4,16,2048]{2,1,0:T(8,128)(2,1)S(1)}, u32[]{:S(2)}, u32[]{:S(2)}) collective-permute-start(bf16[4,16,2048]{2,1,0:T(8,128)(2,1)S(1)} %pad_maximum_fusion.refs_0_), channel_id=1, source_target_pairs={{0,24},{4,28},{8,0},{12,4},{16,8},{20,12},{24,16},{28,20},{32,56},... | collective-permute-start | bytes 786440 | tf_op jit(solution)/shard_map/ppermute | solution.py:36
  146.7 18.7 %collective-permute-done.37.refs_2_ = s16[6,272,256]{2,1,0:T(8,128)(2,1)S(1)} collective-permute-done((s16[6,272,256]{2,1,0:T(8,128)(2,1)S(1)}, s16[6,272,256]{2,1,0:T(8,128)(2,1)S(1)}, u32[]{:S(2)}, u32[]{:S(2)}) %collective-permute-start.37) | collective-permute-done | bytes 835616 | tf_op jit(solution)/shard_map/ppermute | solution.py:292
  165.4 1.4 collective-permute-start.31
  166.8 2.4 %collective-permute-start.26 = (bf16[4,16,2048]{2,1,0:T(8,128)(2,1)S(1)}, bf16[4,16,2048]{2,1,0:T(8,128)(2,1)S(1)}, u32[]{:S(2)}, u32[]{:S(2)}) collective-permute-start(bf16[4,16,2048]{2,1,0:T(8,128)(2,1)S(1)} %constant_dynamic-update-slice_fusion.refs_4_), channel_id=1, source_target_pairs={{0,96},{4,100},{8,104},{12,108},{16,112},{20,116},{24,120},{28,124... | collective-permute-start | bytes 786440 | tf_op jit(solution)/shard_map/ppermute | solution.py:36
  170.8 9.5 %collective-permute-done.26.refs_7_ = bf16[4,16,2048]{2,1,0:T(8,128)(2,1)S(1)} collective-permute-done((bf16[4,16,2048]{2,1,0:T(8,128)(2,1)S(1)}, bf16[4,16,2048]{2,1,0:T(8,128)(2,1)S(1)}, u32[]{:S(2)}, u32[]{:S(2)}) %collective-permute-start.26) | collective-permute-done | bytes 262176 | tf_op jit(solution)/shard_map/ppermute | solution.py:36
  181.3 2.8 %collective-permute-done.24.refs_5_ = bf16[4,16,2048]{2,1,0:T(8,128)(2,1)S(1)} collective-permute-done((bf16[4,16,2048]{2,1,0:T(8,128)(2,1)S(1)}, bf16[4,16,2048]{2,1,0:T(8,128)(2,1)S(1)}, u32[]{:S(2)}, u32[]{:S(2)}) %collective-permute-start.24) | collective-permute-done | bytes 262176 | tf_op jit(solution)/shard_map/ppermute | solution.py:36
  184.8 1.6 shard_map.122
  186.5 2.5 %shard_map.121 = bf16[64,16,2048]{2,1,0:T(8,128)(2,1)} custom-call(s32[64]{0:T(128)S(1)} %copy-done.1, s32[1]{0:T(128)} %bitcast.me_ref, bf16[4,16,2048]{2,1,0:T(8,128)(2,1)S(1)} %pad_maximum_fusion.refs_0_, bf16[4,16,2048]{2,1,0:T(8,128)(2,1)S(1)} %collective-permute-done.17.refs_1_, bf16[4,16,2048]{2,1,0:T(8,128)(2,1)S(1)} %collective-permute-done.18.refs_2_, ...), custom_call_target="tpu_custom_call" | custom-call | tf_op jit(solution)/shard_map/pallas_call | solution.py:268
  (78 shorter events, 10.3 us)
Async XLA Ops:
  13.6 26.6 %collective-permute-start = (bf16[32,16,2176]{2,1,0:T(8,128)(2,1)}, bf16[32,16,2176]{2,1,0:T(8,128)(2,1)}, u32[]{:S(2)}, u32[]{:S(2)}) collective-permute-start(bf16[32,16,2176]{2,1,0:T(8,128)(2,1)} %get-tuple-element.29), channel_id=1, source_target_pairs={{0,4},{4,0},{8,12},{12,8},{16,20},{20,16},{24,28},{28,24},{32,36},... | collective-permute-start | bytes 6684680 | tf_op jit(solution)/shard_map/ppermute | solution.py:36
  42.5 8.2 %collective-permute-start.6 = (bf16[4,16,2176]{2,1,0:T(8,128)(2,1)S(1)}, bf16[4,16,2176]{2,1,0:T(8,128)(2,1)S(1)}, u32[]{:S(2)}, u32[]{:S(2)}) collective-permute-start(bf16[4,16,2176]{2,1,0:T(8,128)(2,1)S(1)} %get-tuple-element.53), channel_id=1, source_target_pairs={{0,24},{4,28},{8,0},{12,4},{16,8},{20,12},{24,16},{28,20},{32,56},... | collective-permute-start | bytes 835592 | tf_op jit(solution)/shard_map/ppermute | solution.py:36
  43.6 15.1 %collective-permute-start.5 = (bf16[4,16,2176]{2,1,0:T(8,128)(2,1)S(1)}, bf16[4,16,2176]{2,1,0:T(8,128)(2,1)S(1)}, u32[]{:S(2)}, u32[]{:S(2)}) collective-permute-start(bf16[4,16,2176]{2,1,0:T(8,128)(2,1)S(1)} %get-tuple-element.54), channel_id=1, source_target_pairs={{0,8},{4,12},{8,16},{12,20},{16,24},{20,28},{24,0},{28,4},{32,40},... | collective-permute-start | bytes 835592 | tf_op jit(solution)/shard_map/ppermute | solution.py:36
  44.0 14.6 %collective-permute-start.4 = (bf16[4,16,2176]{2,1,0:T(8,128)(2,1)S(1)}, bf16[4,16,2176]{2,1,0:T(8,128)(2,1)S(1)}, u32[]{:S(2)}, u32[]{:S(2)}) collective-permute-start(bf16[4,16,2176]{2,1,0:T(8,128)(2,1)S(1)} %get-tuple-element.55), channel_id=1, source_target_pairs={{0,16},{4,20},{8,24},{12,28},{16,0},{20,4},{24,8},{28,12},{32,48},... | collective-permute-start | bytes 835592 | tf_op jit(solution)/shard_map/ppermute | solution.py:36
  45.2 13.4 %collective-permute-start.3 = (bf16[4,16,2176]{2,1,0:T(8,128)(2,1)S(1)}, bf16[4,16,2176]{2,1,0:T(8,128)(2,1)S(1)}, u32[]{:S(2)}, u32[]{:S(2)}) collective-permute-start(bf16[4,16,2176]{2,1,0:T(8,128)(2,1)S(1)} %get-tuple-element.56), channel_id=1, source_target_pairs={{0,96},{4,100},{8,104},{12,108},{16,112},{20,116},{24,120},{28,124... | collective-permute-start | bytes 835592 | tf_op jit(solution)/shard_map/ppermute | solution.py:36
  47.7 10.9 %collective-permute-start.2 = (bf16[4,16,2176]{2,1,0:T(8,128)(2,1)S(1)}, bf16[4,16,2176]{2,1,0:T(8,128)(2,1)S(1)}, u32[]{:S(2)}, u32[]{:S(2)}) collective-permute-start(bf16[4,16,2176]{2,1,0:T(8,128)(2,1)S(1)} %get-tuple-element.57), channel_id=1, source_target_pairs={{0,32},{4,36},{8,40},{12,44},{16,48},{20,52},{24,56},{28,60},{32,6... | collective-permute-start | bytes 835592 | tf_op jit(solution)/shard_map/ppermute | solution.py:36
  50.7 13.4 %collective-permute-start.1 = (bf16[4,16,2176]{2,1,0:T(8,128)(2,1)S(1)}, bf16[4,16,2176]{2,1,0:T(8,128)(2,1)S(1)}, u32[]{:S(2)}, u32[]{:S(2)}) collective-permute-start(bf16[4,16,2176]{2,1,0:T(8,128)(2,1)S(1)} %get-tuple-element.58), channel_id=1, source_target_pairs={{0,64},{4,68},{8,72},{12,76},{16,80},{20,84},{24,88},{28,92},{32,9... | collective-permute-start | bytes 835592 | tf_op jit(solution)/shard_map/ppermute | solution.py:36
  64.2 7.9 %collective-permute-start.9 = (bf16[16,2176]{1,0:T(8,128)(2,1)S(1)}, bf16[16,2176]{1,0:T(8,128)(2,1)S(1)}, u32[]{:S(2)}, u32[]{:S(2)}) collective-permute-start(bf16[16,2176]{1,0:T(8,128)(2,1)S(1)} %get-tuple-element.63), channel_id=1, source_target_pairs={{0,24},{4,28},{8,0},{12,4},{16,8},{20,12},{24,16},{28,20},{32,56},... | collective-permute-start | bytes 208904 | tf_op jit(solution)/shard_map/ppermute | solution.py:36
  68.0 5.8 %collective-permute-start.8 = (bf16[16,2176]{1,0:T(8,128)(2,1)S(1)}, bf16[16,2176]{1,0:T(8,128)(2,1)S(1)}, u32[]{:S(2)}, u32[]{:S(2)}) collective-permute-start(bf16[16,2176]{1,0:T(8,128)(2,1)S(1)} %get-tuple-element.64), channel_id=1, source_target_pairs={{0,8},{4,12},{8,16},{12,20},{16,24},{20,28},{24,0},{28,4},{32,40},... | collective-permute-start | bytes 208904 | tf_op jit(solution)/shard_map/ppermute | solution.py:36
  68.0 5.8 %collective-permute-start.7 = (bf16[16,2176]{1,0:T(8,128)(2,1)S(1)}, bf16[16,2176]{1,0:T(8,128)(2,1)S(1)}, u32[]{:S(2)}, u32[]{:S(2)}) collective-permute-start(bf16[16,2176]{1,0:T(8,128)(2,1)S(1)} %get-tuple-element.65), channel_id=1, source_target_pairs={{0,16},{4,20},{8,24},{12,28},{16,0},{20,4},{24,8},{28,12},{32,48},... | collective-permute-start | bytes 208904 | tf_op jit(solution)/shard_map/ppermute | solution.py:36
  72.1 5.1 %collective-permute-start.11 = (bf16[16,2176]{1,0:T(8,128)(2,1)S(1)}, bf16[16,2176]{1,0:T(8,128)(2,1)S(1)}, u32[]{:S(2)}, u32[]{:S(2)}) collective-permute-start(bf16[16,2176]{1,0:T(8,128)(2,1)S(1)} %get-tuple-element.61), channel_id=1, source_target_pairs={{0,32},{4,36},{8,40},{12,44},{16,48},{20,52},{24,56},{28,60},{32,6... | collective-permute-start | bytes 208904 | tf_op jit(solution)/shard_map/ppermute | solution.py:36
  72.1 5.1 %collective-permute-start.10 = (bf16[16,2176]{1,0:T(8,128)(2,1)S(1)}, bf16[16,2176]{1,0:T(8,128)(2,1)S(1)}, u32[]{:S(2)}, u32[]{:S(2)}) collective-permute-start(bf16[16,2176]{1,0:T(8,128)(2,1)S(1)} %get-tuple-element.62), channel_id=1, source_target_pairs={{0,64},{4,68},{8,72},{12,76},{16,80},{20,84},{24,88},{28,92},{32,9... | collective-permute-start | bytes 208904 | tf_op jit(solution)/shard_map/ppermute | solution.py:36
  77.3 10.3 %collective-permute-start.13 = (f32[16,2176]{1,0:T(8,128)S(1)}, f32[16,2176]{1,0:T(8,128)S(1)}, u32[]{:S(2)}, u32[]{:S(2)}) collective-permute-start(f32[16,2176]{1,0:T(8,128)S(1)} %fusion.1), channel_id=1, source_target_pairs={{0,128},{4,132},{8,136},{12,140},{16,144},{20,148},{24,152},{28,15... | collective-permute-start | bytes 417800 | tf_op jit(solution)/shard_map/ppermute | solution.py:36
  84.2 51.3 %collective-permute-start.35 = (s16[6,272,256]{2,1,0:T(8,128)(2,1)S(1)}, s16[6,272,256]{2,1,0:T(8,128)(2,1)S(1)}, u32[]{:S(2)}, u32[]{:S(2)}) collective-permute-start(s16[6,272,256]{2,1,0:T(8,128)(2,1)S(1)} %copy-done.8), channel_id=1, source_target_pairs={{0,1},{1,2},{2,3},{3,0},{4,5},{5,6},{6,7},{7,4},{8,9},{9,10},{10,1... | collective-permute-start | bytes 2506760 | tf_op jit(solution)/shard_map/ppermute | solution.py:292
  85.0 58.6 %collective-permute-start.36 = (s16[6,272,256]{2,1,0:T(8,128)(2,1)S(1)}, s16[6,272,256]{2,1,0:T(8,128)(2,1)S(1)}, u32[]{:S(2)}, u32[]{:S(2)}) collective-permute-start(s16[6,272,256]{2,1,0:T(8,128)(2,1)S(1)} %copy-done.7), channel_id=1, source_target_pairs={{0,3},{1,0},{2,1},{3,2},{4,7},{5,4},{6,5},{7,6},{8,11},{9,8},{10,9... | collective-permute-start | bytes 2506760 | tf_op jit(solution)/shard_map/ppermute | solution.py:292
  89.7 36.2 %collective-permute-start.20 = (bf16[1,16,2048]{2,1,0:T(8,128)(2,1)S(1)}, bf16[1,16,2048]{2,1,0:T(8,128)(2,1)S(1)}, u32[]{:S(2)}, u32[]{:S(2)}) collective-permute-start(bf16[1,16,2048]{2,1,0:T(8,128)(2,1)S(1)} %get-tuple-element.49), channel_id=1, source_target_pairs={{0,128},{4,132},{8,136},{12,140},{16,144},{20,148},{24,152},{28,15... | collective-permute-start | bytes 196616 | tf_op jit(solution)/shard_map/ppermute | solution.py:36
  95.2 30.7 %collective-permute-start.16 = (bf16[1,16,2048]{2,1,0:T(8,128)(2,1)S(1)}, bf16[1,16,2048]{2,1,0:T(8,128)(2,1)S(1)}, u32[]{:S(2)}, u32[]{:S(2)}) collective-permute-start(bf16[1,16,2048]{2,1,0:T(8,128)(2,1)S(1)} %get-tuple-element.49), channel_id=1, source_target_pairs={{0,96},{4,100},{8,104},{12,108},{16,112},{20,116},{24,120},{28,124... | collective-permute-start | bytes 196616 | tf_op jit(solution)/shard_map/ppermute | solution.py:36
  97.5 28.5 %collective-permute-start.15 = (bf16[1,16,2048]{2,1,0:T(8,128)(2,1)S(1)}, bf16[1,16,2048]{2,1,0:T(8,128)(2,1)S(1)}, u32[]{:S(2)}, u32[]{:S(2)}) collective-permute-start(bf16[1,16,2048]{2,1,0:T(8,128)(2,1)S(1)} %get-tuple-element.49), channel_id=1, source_target_pairs={{0,64},{4,68},{8,72},{12,76},{16,80},{20,84},{24,88},{28,92},{32,9... | collective-permute-start | bytes 196616 | tf_op jit(solution)/shard_map/ppermute | solution.py:36
  125.9 39.5 %collective-permute-start.37 = (s16[6,272,256]{2,1,0:T(8,128)(2,1)S(1)}, s16[6,272,256]{2,1,0:T(8,128)(2,1)S(1)}, u32[]{:S(2)}, u32[]{:S(2)}) collective-permute-start(s16[6,272,256]{2,1,0:T(8,128)(2,1)S(1)} %copy-done.6), channel_id=1, source_target_pairs={{0,2},{1,3},{2,0},{3,1},{4,6},{5,7},{6,4},{7,5},{8,10},{9,11},{10,... | collective-permute-start | bytes 2506760 | tf_op jit(solution)/shard_map/ppermute | solution.py:292
  126.0 20.0 %collective-permute-start.23 = (bf16[1,16,2048]{2,1,0:T(8,128)(2,1)S(1)}, bf16[1,16,2048]{2,1,0:T(8,128)(2,1)S(1)}, u32[]{:S(2)}, u32[]{:S(2)}) collective-permute-start(bf16[1,16,2048]{2,1,0:T(8,128)(2,1)S(1)} %collective-permute-done.20), channel_id=1, source_target_pairs={{0,24},{4,28},{8,0},{12,4},{16,8},{20,12},{24,16},{28,20},{32,56},... | collective-permute-start | bytes 196616 | tf_op jit(solution)/shard_map/ppermute | solution.py:36
  134.5 11.5 %collective-permute-start.22 = (bf16[1,16,2048]{2,1,0:T(8,128)(2,1)S(1)}, bf16[1,16,2048]{2,1,0:T(8,128)(2,1)S(1)}, u32[]{:S(2)}, u32[]{:S(2)}) collective-permute-start(bf16[1,16,2048]{2,1,0:T(8,128)(2,1)S(1)} %collective-permute-done.20), channel_id=1, source_target_pairs={{0,16},{4,20},{8,24},{12,28},{16,0},{20,4},{24,8},{28,12},{32,48},... | collective-permute-start | bytes 196616 | tf_op jit(solution)/shard_map/ppermute | solution.py:36
  135.5 31.3 %collective-permute-start.27 = (bf16[4,16,2048]{2,1,0:T(8,128)(2,1)S(1)}, bf16[4,16,2048]{2,1,0:T(8,128)(2,1)S(1)}, u32[]{:S(2)}, u32[]{:S(2)}) collective-permute-start(bf16[4,16,2048]{2,1,0:T(8,128)(2,1)S(1)} %pad_maximum_fusion.refs_0_), channel_id=1, source_target_pairs={{0,4},{4,0},{8,12},{12,8},{16,20},{20,16},{24,28},{28,24},{32,36},... | collective-permute-start | bytes 786440 | tf_op jit(solution)/shard_map/ppermute | solution.py:36
  143.6 25.5 %collective-permute-start.19 = (bf16[4,16,2048]{2,1,0:T(8,128)(2,1)S(1)}, bf16[4,16,2048]{2,1,0:T(8,128)(2,1)S(1)}, u32[]{:S(2)}, u32[]{:S(2)}) collective-permute-start(bf16[4,16,2048]{2,1,0:T(8,128)(2,1)S(1)} %pad_maximum_fusion.refs_0_), channel_id=1, source_target_pairs={{0,24},{4,28},{8,0},{12,4},{16,8},{20,12},{24,16},{28,20},{32,56},... | collective-permute-start | bytes 786440 | tf_op jit(solution)/shard_map/ppermute | solution.py:36
  146.0 23.2 %collective-permute-start.18 = (bf16[4,16,2048]{2,1,0:T(8,128)(2,1)S(1)}, bf16[4,16,2048]{2,1,0:T(8,128)(2,1)S(1)}, u32[]{:S(2)}, u32[]{:S(2)}) collective-permute-start(bf16[4,16,2048]{2,1,0:T(8,128)(2,1)S(1)} %pad_maximum_fusion.refs_0_), channel_id=1, source_target_pairs={{0,16},{4,20},{8,24},{12,28},{16,0},{20,4},{24,8},{28,12},{32,48},... | collective-permute-start | bytes 786440 | tf_op jit(solution)/shard_map/ppermute | solution.py:36
  146.0 23.9 %collective-permute-start.17 = (bf16[4,16,2048]{2,1,0:T(8,128)(2,1)S(1)}, bf16[4,16,2048]{2,1,0:T(8,128)(2,1)S(1)}, u32[]{:S(2)}, u32[]{:S(2)}) collective-permute-start(bf16[4,16,2048]{2,1,0:T(8,128)(2,1)S(1)} %pad_maximum_fusion.refs_0_), channel_id=1, source_target_pairs={{0,8},{4,12},{8,16},{12,20},{16,24},{20,28},{24,0},{28,4},{32,40},... | collective-permute-start | bytes 786440 | tf_op jit(solution)/shard_map/ppermute | solution.py:36
  165.4 5.3 %collective-permute-start.31 = (bf16[4,16,2048]{2,1,0:T(8,128)(2,1)S(1)}, bf16[4,16,2048]{2,1,0:T(8,128)(2,1)S(1)}, u32[]{:S(2)}, u32[]{:S(2)}) collective-permute-start(bf16[4,16,2048]{2,1,0:T(8,128)(2,1)S(1)} %constant_dynamic-update-slice_fusion.refs_4_), channel_id=1, source_target_pairs={{0,4},{4,0},{8,12},{12,8},{16,20},{20,16},{24,28},{28,24},{32,36},... | collective-permute-start | bytes 786440 | tf_op jit(solution)/shard_map/ppermute | solution.py:36
  166.8 13.5 %collective-permute-start.26 = (bf16[4,16,2048]{2,1,0:T(8,128)(2,1)S(1)}, bf16[4,16,2048]{2,1,0:T(8,128)(2,1)S(1)}, u32[]{:S(2)}, u32[]{:S(2)}) collective-permute-start(bf16[4,16,2048]{2,1,0:T(8,128)(2,1)S(1)} %constant_dynamic-update-slice_fusion.refs_4_), channel_id=1, source_target_pairs={{0,96},{4,100},{8,104},{12,108},{16,112},{20,116},{24,120},{28,124... | collective-permute-start | bytes 786440 | tf_op jit(solution)/shard_map/ppermute | solution.py:36
  169.2 12.2 %collective-permute-start.25 = (bf16[4,16,2048]{2,1,0:T(8,128)(2,1)S(1)}, bf16[4,16,2048]{2,1,0:T(8,128)(2,1)S(1)}, u32[]{:S(2)}, u32[]{:S(2)}) collective-permute-start(bf16[4,16,2048]{2,1,0:T(8,128)(2,1)S(1)} %constant_dynamic-update-slice_fusion.refs_4_), channel_id=1, source_target_pairs={{0,64},{4,68},{8,72},{12,76},{16,80},{20,84},{24,88},{28,92},{32,9... | collective-permute-start | bytes 786440 | tf_op jit(solution)/shard_map/ppermute | solution.py:36
  169.2 14.9 %collective-permute-start.24 = (bf16[4,16,2048]{2,1,0:T(8,128)(2,1)S(1)}, bf16[4,16,2048]{2,1,0:T(8,128)(2,1)S(1)}, u32[]{:S(2)}, u32[]{:S(2)}) collective-permute-start(bf16[4,16,2048]{2,1,0:T(8,128)(2,1)S(1)} %constant_dynamic-update-slice_fusion.refs_4_), channel_id=1, source_target_pairs={{0,32},{4,36},{8,40},{12,44},{16,48},{20,52},{24,56},{28,60},{32,6... | collective-permute-start | bytes 786440 | tf_op jit(solution)/shard_map/ppermute | solution.py:36
  169.9 14.9 %collective-permute-start.30 = (bf16[4,16,2048]{2,1,0:T(8,128)(2,1)S(1)}, bf16[4,16,2048]{2,1,0:T(8,128)(2,1)S(1)}, u32[]{:S(2)}, u32[]{:S(2)}) collective-permute-start(bf16[4,16,2048]{2,1,0:T(8,128)(2,1)S(1)} %collective-permute-done.19.refs_3_), channel_id=1, source_target_pairs={{0,4},{4,0},{8,12},{12,8},{16,20},{20,16},{24,28},{28,24},{32,36},... | collective-permute-start | bytes 786440 | tf_op jit(solution)/shard_map/ppermute | solution.py:36
  170.7 15.7 %collective-permute-start.29 = (bf16[4,16,2048]{2,1,0:T(8,128)(2,1)S(1)}, bf16[4,16,2048]{2,1,0:T(8,128)(2,1)S(1)}, u32[]{:S(2)}, u32[]{:S(2)}) collective-permute-start(bf16[4,16,2048]{2,1,0:T(8,128)(2,1)S(1)} %collective-permute-done.18.refs_2_), channel_id=1, source_target_pairs={{0,4},{4,0},{8,12},{12,8},{16,20},{20,16},{24,28},{28,24},{32,36},... | collective-permute-start | bytes 786440 | tf_op jit(solution)/shard_map/ppermute | solution.py:36
  180.3 6.1 %collective-permute-start.28 = (bf16[4,16,2048]{2,1,0:T(8,128)(2,1)S(1)}, bf16[4,16,2048]{2,1,0:T(8,128)(2,1)S(1)}, u32[]{:S(2)}, u32[]{:S(2)}) collective-permute-start(bf16[4,16,2048]{2,1,0:T(8,128)(2,1)S(1)} %collective-permute-done.17.refs_1_), channel_id=1, source_target_pairs={{0,4},{4,0},{8,12},{12,8},{16,20},{20,16},{24,28},{28,24},{32,36},... | collective-permute-start | bytes 786440 | tf_op jit(solution)/shard_map/ppermute | solution.py:36
  (15 other events, 513.3 us)
where the time goes:
time: 189 us
  waiting for transfers between devices  76.8 us (41%)
  starting transfers between devices  66.2 us (35%)
  Pallas kernels  39.8 us (21%)
  other arithmetic  4.61 us (2%)
    ppermute x35, starting transfers between devices, move(): return lax.ppermute(value, 'dp', pairs)  62.8 us
    ppermute x35, waiting for transfers between devices, move(): return lax.ppermute(value, 'dp', pairs)  58.1 us
    pallas_call x1, Pallas kernels, input_shares(): pl.pallas_call(kernel, grid=(tokens // tall,), out_shape=(jax.ShapeDtypeS...  23.3 us
    ppermute x3, waiting for transfers between devices, pass_share(): return lax.ppermute(coded[offset - 1], 'mp', ring)  18.7 us
    pallas_call x1, Pallas kernels, weight_partials(): pl.pallas_call(kernel, grid=(steps + 1,), out_shape=(out, out), in_specs=...  12.3 us
  transfers between devices with their start and end apart: 38, of which 10 were waited for; matrix products, arithmetic and copies ran while one was open for 1% of the time, Pallas kernels for 13%

commit v1 on v0

--- a/solution.py
+++ b/solution.py
@@ -138,45 +138,25 @@
     )(count, owner_map, me, acts, grads)
 
 
-def input_shares(grads, weight, count, mine, ways, interpret=False):
+def input_shares(grads, weight, count, mine, ways, offsets, interpret=False):
     tokens, columns = grads.shape
     hidden = weight.shape[0]
     width = hidden // ways
-    tall = 256
+    tall = 512
     groups = tall // GROUP
     extra = 16
 
-    def kernel(count_ref, mine_ref, grads_ref, weight_ref, own_ref, *refs):
-        coded, held, sems = refs[:-2], refs[-2], refs[-1]
+    def kernel(count_ref, mine_ref, grads_ref, *refs):
         step = pl.program_id(0)
         live = lax.broadcasted_iota(jnp.int32, (tall, width), 0) + step * tall < count_ref[0]
-        order = (*range(1, ways), 0)
-
-        def load(offset):
-            at = lax.rem(mine_ref[0] + offset, ways) * width
-            return pltpu.make_async_copy(
-                weight_ref.at[pl.ds(pl.multiple_of(at, width), width)], held.at[offset], sems.at[offset]
-            )
-
-        @pl.when(step == 0)
-        def _():
-            for offset in order:
-                load(offset).start()
-
-        for offset in order:
-
-            @pl.when(step == 0)
-            def _(offset=offset):
-                load(offset).wait()
-
+        for offset, part, out in zip(offsets, refs[: len(offsets)], refs[len(offsets) :]):
             share = lax.dot_general(
-                grads_ref[...], held[offset], (((1,), (1,)), ((), ())), preferred_element_type=f32
+                grads_ref[...], part[...], (((1,), (1,)), ((), ())), preferred_element_type=f32
             )
             share = jnp.where(live, share, 0.0)
             if offset == 0:
-                own_ref[...] = share
+                out[...] = share
                 continue
-            out = coded[offset - 1]
             largest = jnp.max(jnp.abs(share).reshape(groups, GROUP, width), axis=1)
             largest = jnp.max(largest, axis=1, keepdims=True)
             power = jnp.floor(jnp.log2(32000.0 / jnp.maximum(largest, 1e-25)))
@@ -185,25 +165,30 @@
             for g in range(groups):
                 code = jnp.round(share[g * GROUP : (g + 1) * GROUP] * factor[g : g + 1])
                 out[0, g * GROUP : (g + 1) * GROUP, :] = code.astype(jnp.int32).astype(i16)
-            power = jnp.concatenate([power] * (extra // groups), axis=0)
             out[0, tall : tall + extra, :] = power.astype(jnp.int32).astype(i16)
 
+    def part_of(offset):
+        return pl.BlockSpec(
+            (width, columns), lambda n, count, mine: (lax.rem(mine[0] + offset, ways), 0)
+        )
+
+    own = jax.ShapeDtypeStruct((tokens, width), f32)
     code = jax.ShapeDtypeStruct((tokens // tall, tall + extra, width), i16)
+    own_spec = pl.BlockSpec((tall, width), lambda n, *_: (n, 0))
+    code_spec = pl.BlockSpec((1, tall + extra, width), lambda n, *_: (n, 0, 0))
     return pl.pallas_call(
         kernel,
-        grid=(tokens // tall,),
-        out_shape=(jax.ShapeDtypeStruct((tokens, width), f32),) + (code,) * (ways - 1),
-        in_specs=[pl.BlockSpec(memory_space=pltpu.SMEM)] * 2
-        + [
-            pl.BlockSpec((tall, columns), lambda n: (n, 0)),
-            pl.BlockSpec(memory_space=pl.ANY),
-        ],
-        out_specs=(pl.BlockSpec((tall, width), lambda n: (n, 0)),)
-        + (pl.BlockSpec((1, tall + extra, width), lambda n: (n, 0, 0)),) * (ways - 1),
-        scratch_shapes=[pltpu.VMEM((ways, width, columns), bf16), pltpu.SemaphoreType.DMA((ways,))],
+        grid_spec=pltpu.PrefetchScalarGridSpec(
+            num_scalar_prefetch=2,
+            grid=(tokens // tall,),
+            in_specs=[pl.BlockSpec((tall, columns), lambda n, *_: (n, 0))]
+            + [part_of(offset) for offset in offsets],
+            out_specs=[own_spec if offset == 0 else code_spec for offset in offsets],
+        ),
+        out_shape=[own if offset == 0 else code for offset in offsets],
         compiler_params=pltpu.CompilerParams(vmem_limit_bytes=60 * 2**20),
         interpret=interpret,
-    )(count, mine, grads, weight)
+    )(count, mine, grads, *[weight] * len(offsets))
 
 
 def add_shares(own, coded, interpret=False):
@@ -289,14 +274,15 @@
 
     def pass_share(coded, offset):
         ring = [(source, (source + offset) % ways) for source in range(ways)]
-        return lax.ppermute(coded[offset - 1], "mp", ring)
-
-    keep, send = weight_partials(hidden_acts, out_grads, token_counts, owner_map, me)
+        return lax.ppermute(coded, "mp", ring)
+
+    (up,) = input_shares(out_grads, down_weight, token_counts, my_mp, ways, (1,))
+    shares = [pass_share(up, 1)]
+    acts, _ = lax.optimization_barrier((hidden_acts, up))
+    keep, send = weight_partials(acts, out_grads, token_counts, owner_map, me)
     arrived = to_core(send)
-    out_grads, keep = lax.optimization_barrier((out_grads, keep))
-    own, *coded = input_shares(out_grads, down_weight, token_counts, my_mp, ways)
-    arrived, own = lax.optimization_barrier((arrived, own))
-    shares = [pass_share(coded, 1), pass_share(coded, 3)]
+    states = jnp.stack([master, moment1, moment2.astype(f32)])
+    other_states = to_zh(states)
 
     pair = [
         (keep[4 * i : 4 * i + 4].astype(f32) + arrived[4 * i : 4 * i + 4].astype(f32)).astype(bf16)
@@ -307,6 +293,10 @@
         for colour, (first, _) in enumerate(rings)
     ]
     got = lax.optimization_barrier(got)
+    down, across, own = input_shares(
+        out_grads, down_weight, token_counts, my_mp, ways, (3, 2, 0)
+    )
+    shares.append(pass_share(down, 3))
     lines = [
         [
             sum((g[e].astype(f32) for g in got[colour]), pair[4 * colour][e].astype(f32)).astype(bf16)
@@ -315,31 +305,41 @@
         for colour in range(2)
     ]
     got = [
-        [shift(line[d], second, d) for d in (2, 1, 3)] for line, (_, second) in zip(lines, rings)
+        [shift(line[d], second, d) for d in (2, 1, 3)]
+        for line, (_, second) in zip(lines, rings)
     ]
     got = lax.optimization_barrier(got)
     sums = [
         sum((g.astype(f32) for g in group), line[0].astype(f32)) for group, line in zip(got, lines)
     ]
-    summed = sums[0] + to_zh(sums[1])
-
-    digits = summed[0, columns : columns + DIGITS]
-    total = jnp.sum(digits * (4.0 ** jnp.arange(DIGITS, dtype=f32)))
-    grad = summed[:, :columns] / total
-    moment1_new = beta_one * moment1 + (1.0 - beta_one) * grad
-    second = beta_two * moment2.astype(f32) + (1.0 - beta_two) * grad * grad
-    moment2_new = second.astype(bf16)
-    master_new = master - learn_rate * (moment1_new / correct_one) / (
+    sums = lax.optimization_barrier(jnp.stack(sums))
+    theirs = to_zh(sums)
+    shares.append(pass_share(across, 2))
+
+    summed = sums + theirs[::-1]
+    digits = summed[:, :1, columns : columns + DIGITS]
+    total = jnp.sum(digits * (4.0 ** jnp.arange(DIGITS, dtype=f32)), axis=(1, 2), keepdims=True)
+    grad = summed[:, :, :columns] / total
+    old_master, old_first, old_second = jnp.stack([states, other_states], axis=1)
+    moment1_new = beta_one * old_first + (1.0 - beta_one) * grad
+    second = beta_two * old_second + (1.0 - beta_two) * grad * grad
+    master_new = old_master - learn_rate * (moment1_new / correct_one) / (
         jnp.sqrt(second / correct_two) + epsilon
     )
-
-    weights = master_new.astype(bf16)[None]
-    other = to_zh(weights)
-    shares.append(pass_share(coded, 2))
+    weights = master_new.astype(bf16)
+    master_new, moment1_new, moment2_new = master_new[0], moment1_new[0], second[0].astype(bf16)
+
+    got = [
+        [shift(weights[colour : colour + 1], first, d) for d in (2, 1, 3)]
+        for colour, (first, _) in enumerate(rings)
+    ]
+    got = lax.optimization_barrier(got)
     pieces = []
-    for part, (first, second) in zip((weights, other), rings):
-        line = jnp.concatenate([part] + [shift(part, first, d) for d in (1, 2, 3)])
-        pieces += [line] + [shift(line, second, d) for d in (1, 2, 3)]
+    for colour, (_, second) in enumerate(rings):
+        two, one, three = got[colour]
+        line = jnp.concatenate([weights[colour : colour + 1], one, two, three])
+        two, one, three = [shift(line, second, d) for d in (2, 1, 3)]
+        pieces += [line, one, two, three]
     pieces += [to_core(piece) for piece in pieces]
     input_grads = add_shares(own, shares)
     weights_new = place_blocks(pieces, owner_map, me).reshape(hidden, columns)

time: 189 us -> 200 us (1.058)
  waiting for transfers between devices: 76.8 us -> 102 us
  Pallas kernels: 39.8 us -> 31.8 us
  starting transfers between devices: 66.2 us -> 58.9 us
    ppermute x3, waiting for transfers between devices: 18.7 us -> 58.3 us  [pass_share(): return lax.ppermute(coded, 'mp', ring)]
    ppermute x35, waiting for transfers between devices: 58.1 us -> 44.1 us  [move(): return lax.ppermute(value, 'dp', pairs)]
    ppermute x35, starting transfers between devices: 62.8 us -> 54.4 us  [move(): return lax.ppermute(value, 'dp', pairs)]
    pallas_call x1 -> x2, Pallas kernels: 23.3 us -> 15.4 us  [input_shares(): pl.pallas_call(kernel, grid_spec=pltpu.PrefetchScalarGridSpec(num_scalar_...]
  transfers between devices with their start and end apart: 38 -> 38, of which waited for: 10 -> 15; matrix products, arithmetic and copies ran while one was open for 1% -> 1% of each run, Pallas kernels for 13% -> 5%
where the time goes in v1:
time: 200 us
  waiting for transfers between devices  102 us (51%)
  starting transfers between devices  58.9 us (29%)
  Pallas kernels  31.8 us (16%)
  other arithmetic  3.07 us (2%)
  local copies, waits for them, and re-layouts  2.01 us (1%)
    ppermute x3, waiting for transfers between devices, pass_share(): return lax.ppermute(coded, 'mp', ring)  58.3 us
    ppermute x35, starting transfers between devices, move(): return lax.ppermute(value, 'dp', pairs)  54.4 us
    ppermute x35, waiting for transfers between devices, move(): return lax.ppermute(value, 'dp', pairs)  44.1 us
    pallas_call x2, Pallas kernels, input_shares(): pl.pallas_call(kernel, grid_spec=pltpu.PrefetchScalarGridSpec(num_scalar_...  15.4 us
    pallas_call x1, Pallas kernels, weight_partials(): pl.pallas_call(kernel, grid=(steps + 1,), out_shape=(out, out), in_specs=...  12.3 us
    ppermute x3, starting transfers between devices, pass_share(): return lax.ppermute(coded, 'mp', ring)  4.5 us
  transfers between devices with their start and end apart: 38, of which 15 were waited for; matrix products, arithmetic and copies ran while one was open for 1% of the time, Pallas kernels for 5%

profile of v1, /device:TPU:1, one launch (start us, length us, event | category | flops | bytes accessed | tf_op | source)
XLA Modules:
  0.0 199.8 jit_solution(3129974816627557641)
XLA Ops:
  1.3 6.0 %shard_map.119 = s16[3,528,256]{2,1,0:T(8,128)(2,1)} custom-call(s32[1]{0:T(128)S(6)} %copy.14.count_ref, s32[1]{0:T(128)} %bitcast.9.mine_ref, bf16[1536,2048]{1,0:T(8,128)(2,1)} %grads_ref.5, bf16[1024,2048]{1,0:T(8,128)(2,1)} %refs_2_.1), custom_call_target="tpu_custom_call" | custom-call | tf_op jit(solution)/shard_map/pallas_call | solution.py:179
  7.3 12.3 %shard_map.120 = (bf16[32,16,2176]{2,1,0:T(8,128)(2,1)}, bf16[32,16,2176]{2,1,0:T(8,128)(2,1)}) custom-call(s32[1]{0:T(128)S(6)} %copy.14.count_ref, s32[64]{0:T(128)} %map_ref.3, s32[1]{0:T(128)} %bitcast.8.me_ref, bf16[1536,1024]{1,0:T(8,128)(2,1)} %acts_ref, bf16[1536,2048]{1,0:T(8,128)(2,1)} %grads_ref.5), custom_call_target="tpu_custom_call" | custom-call | tf_op jit(solution)/shard_map/pallas_call | solution.py:120
  19.6 3.3 %collective-permute-start.1 = (bf16[32,16,2176]{2,1,0:T(8,128)(2,1)}, bf16[32,16,2176]{2,1,0:T(8,128)(2,1)S(1)}, u32[]{:S(2)}, u32[]{:S(2)}) collective-permute-start(bf16[32,16,2176]{2,1,0:T(8,128)(2,1)} %get-tuple-element.31), channel_id=1, source_target_pairs={{0,4},{4,0},{8,12},{12,8},{16,20},{20,16},{24,28},{28,24},{32,36},... | collective-permute-start | bytes 6684680 | tf_op jit(solution)/shard_map/ppermute | solution.py:36
  22.9 4.2 %collective-permute-done.1 = bf16[32,16,2176]{2,1,0:T(8,128)(2,1)S(1)} collective-permute-done((bf16[32,16,2176]{2,1,0:T(8,128)(2,1)}, bf16[32,16,2176]{2,1,0:T(8,128)(2,1)S(1)}, u32[]{:S(2)}, u32[]{:S(2)}) %collective-permute-start.1) | collective-permute-done | bytes 2228256 | tf_op jit(solution)/shard_map/ppermute | solution.py:36
  27.1 2.2 %add_convert_fusion = (bf16[4,16,2176]{2,1,0:T(8,128)(2,1)S(1)}, bf16[4,16,2176]{2,1,0:T(8,128)(2,1)S(1)}, bf16[4,16,2176]{2,1,0:T(8,128)(2,1)S(1)}, bf16[4,16,2...) fusion(bf16[32,16,2176]{2,1,0:T(8,128)(2,1)S(1)} %collective-pe, ...), kind=kLoop, calls=%fused_computation.4 | loop fusion | flops 4456448 | bytes 6684672 | tf_op jit(solution)/shard_map/convert_element_type | solution.py:288
  32.1 2.5 %collective-permute-start.4 = (bf16[4,16,2176]{2,1,0:T(8,128)(2,1)S(1)}, bf16[4,16,2176]{2,1,0:T(8,128)(2,1)S(1)}, u32[]{:S(2)}, u32[]{:S(2)}) collective-permute-start(bf16[4,16,2176]{2,1,0:T(8,128)(2,1)S(1)} %get-tuple-element.61), channel_id=1, source_target_pairs={{0,96},{4,100},{8,104},{12,108},{16,112},{20,116},{24,120},{28,124... | collective-permute-start | bytes 835592 | tf_op jit(solution)/shard_map/ppermute | solution.py:36
  34.6 2.7 %collective-permute-done.7 = bf16[4,16,2176]{2,1,0:T(8,128)(2,1)S(1)} collective-permute-done((bf16[4,16,2176]{2,1,0:T(8,128)(2,1)S(1)}, bf16[4,16,2176]{2,1,0:T(8,128)(2,1)S(1)}, u32[]{:S(2)}, u32[]{:S(2)}) %collective-permute-start.7) | collective-permute-done | bytes 278560 | tf_op jit(solution)/shard_map/ppermute | solution.py:36
  37.2 7.4 %collective-permute-start.2 = (bf16[4,16,2176]{2,1,0:T(8,128)(2,1)S(1)}, bf16[4,16,2176]{2,1,0:T(8,128)(2,1)S(1)}, u32[]{:S(2)}, u32[]{:S(2)}) collective-permute-start(bf16[4,16,2176]{2,1,0:T(8,128)(2,1)S(1)} %get-tuple-element.63), channel_id=1, source_target_pairs={{0,64},{4,68},{8,72},{12,76},{16,80},{20,84},{24,88},{28,92},{32,9... | collective-permute-start | bytes 835592 | tf_op jit(solution)/shard_map/ppermute | solution.py:36
  44.7 5.6 %collective-permute-done.2 = bf16[4,16,2176]{2,1,0:T(8,128)(2,1)S(1)} collective-permute-done((bf16[4,16,2176]{2,1,0:T(8,128)(2,1)S(1)}, bf16[4,16,2176]{2,1,0:T(8,128)(2,1)S(1)}, u32[]{:S(2)}, u32[]{:S(2)}) %collective-permute-start.2) | collective-permute-done | bytes 278560 | tf_op jit(solution)/shard_map/ppermute | solution.py:36
  50.4 3.8 %collective-permute-start.10 = (bf16[16,2176]{1,0:T(8,128)(2,1)S(1)}, bf16[16,2176]{1,0:T(8,128)(2,1)S(1)}, u32[]{:S(2)}, u32[]{:S(2)}) collective-permute-start(bf16[16,2176]{1,0:T(8,128)(2,1)S(1)} %get-tuple-element.68), channel_id=1, source_target_pairs={{0,24},{4,28},{8,0},{12,4},{16,8},{20,12},{24,16},{28,20},{32,56},... | collective-permute-start | bytes 208904 | tf_op jit(solution)/shard_map/ppermute | solution.py:36
  55.6 2.5 %collective-permute-start.13 = (bf16[16,2176]{1,0:T(8,128)(2,1)S(1)}, bf16[16,2176]{1,0:T(8,128)(2,1)S(1)}, u32[]{:S(2)}, u32[]{:S(2)}) collective-permute-start(bf16[16,2176]{1,0:T(8,128)(2,1)S(1)} %get-tuple-element.65), channel_id=1, source_target_pairs={{0,96},{4,100},{8,104},{12,108},{16,112},{20,116},{24,120},{28,124... | collective-permute-start | bytes 208904 | tf_op jit(solution)/shard_map/ppermute | solution.py:36
  58.1 1.7 collective-permute-start.11
  59.8 1.7 collective-permute-start.35
  61.6 1.6 collective-permute-done.12
  63.3 7.0 %collective-permute-start.14 = (f32[2,16,2176]{2,1,0:T(8,128)S(1)}, f32[2,16,2176]{2,1,0:T(8,128)S(1)}, u32[]{:S(2)}, u32[]{:S(2)}) collective-permute-start(f32[2,16,2176]{2,1,0:T(8,128)S(1)} %pad_maximum_fusion.1), channel_id=1, source_target_pairs={{0,128},{4,132},{8,136},{12,140},{16,144},{20,148},{24,152},{28,15... | collective-permute-start | bytes 835592 | tf_op jit(solution)/shard_map/ppermute | solution.py:36
  70.5 9.3 %shard_map.122 = (s16[3,528,256]{2,1,0:T(8,128)(2,1)}, s16[3,528,256]{2,1,0:T(8,128)(2,1)}, f32[1536,256]{1,0:T(8,128)}) custom-call(s32[1]{0:T(128)S(6)} %copy.14.count_ref, s32[1]{0:T(128)} %bitcast.9.mine_ref, bf16[1536,2048]{1,0:T(8,128)(2,1)} %grads_ref.5, bf16[1024,2048]{1,0:T(8,128)(2,1)} %refs_2_.1, bf16[1024,2048]{1,0:T(8,128)(2,1)} %refs_2_.1, ...), custom_call_target="tpu_custom_call" | custom-call | tf_op jit(solution)/shard_map/pallas_call | solution.py:179
  79.9 2.8 %collective-permute-start.36 = (s16[3,528,256]{2,1,0:T(8,128)(2,1)}, s16[3,528,256]{2,1,0:T(8,128)(2,1)S(1)}, u32[]{:S(2)}, u32[]{:S(2)}) collective-permute-start(s16[3,528,256]{2,1,0:T(8,128)(2,1)} %get-tuple-element.51), channel_id=1, source_target_pairs={{0,3},{1,0},{2,1},{3,2},{4,7},{5,4},{6,5},{7,6},{8,11},{9,8},{10,9... | collective-permute-start | bytes 2433032 | tf_op jit(solution)/shard_map/ppermute | solution.py:277
  82.7 7.2 %collective-permute-done.14 = f32[2,16,2176]{2,1,0:T(8,128)S(1)} collective-permute-done((f32[2,16,2176]{2,1,0:T(8,128)S(1)}, f32[2,16,2176]{2,1,0:T(8,128)S(1)}, u32[]{:S(2)}, u32[]{:S(2)}) %collective-permute-start.14) | collective-permute-done | bytes 278560 | tf_op jit(solution)/shard_map/ppermute | solution.py:36
  90.0 9.6 %collective-permute-done = f32[3,16,2048]{2,1,0:T(8,128)S(1)} collective-permute-done((f32[3,16,2048]{2,1,0:T(8,128)S(1)}, f32[3,16,2048]{2,1,0:T(8,128)S(1)}, u32[]{:S(2)}, u32[]{:S(2)}) %collective-permute-start) | collective-permute-done | bytes 393248 | tf_op jit(solution)/shard_map/ppermute | solution.py:36
  101.9 1.7 collective-permute-start.18
  103.6 25.4 %collective-permute-done.36.refs_1_ = s16[3,528,256]{2,1,0:T(8,128)(2,1)S(1)} collective-permute-done((s16[3,528,256]{2,1,0:T(8,128)(2,1)}, s16[3,528,256]{2,1,0:T(8,128)(2,1)S(1)}, u32[]{:S(2)}, u32[]{:S(2)}) %collective-permute-start.36) | collective-permute-done | bytes 811040 | tf_op jit(solution)/shard_map/ppermute | solution.py:277
  129.0 1.8 collective-permute-start.17
  130.8 32.9 %collective-permute-done.37.refs_2_ = s16[3,528,256]{2,1,0:T(8,128)(2,1)S(1)} collective-permute-done((s16[3,528,256]{2,1,0:T(8,128)(2,1)}, s16[3,528,256]{2,1,0:T(8,128)(2,1)S(1)}, u32[]{:S(2)}, u32[]{:S(2)}) %collective-permute-start.37) | collective-permute-done | bytes 811040 | tf_op jit(solution)/shard_map/ppermute | solution.py:277
  168.4 1.7 collective-permute-done.15
  170.1 1.9 collective-permute-start.31
  176.9 2.9 %collective-permute-done.26.refs_7_ = bf16[4,16,2048]{2,1,0:T(8,128)(2,1)S(1)} collective-permute-done((bf16[4,16,2048]{2,1,0:T(8,128)(2,1)S(1)}, bf16[4,16,2048]{2,1,0:T(8,128)(2,1)S(1)}, u32[]{:S(2)}, u32[]{:S(2)}) %collective-permute-start.26) | collective-permute-done | bytes 262176 | tf_op jit(solution)/shard_map/ppermute | solution.py:36
  179.8 1.7 collective-permute-start.22
  182.1 2.0 collective-permute-start.21
  184.1 4.3 %collective-permute-done.24.refs_5_ = bf16[4,16,2048]{2,1,0:T(8,128)(2,1)S(1)} collective-permute-done((bf16[4,16,2048]{2,1,0:T(8,128)(2,1)S(1)}, bf16[4,16,2048]{2,1,0:T(8,128)(2,1)S(1)}, u32[]{:S(2)}, u32[]{:S(2)}) %collective-permute-start.24) | collective-permute-done | bytes 262176 | tf_op jit(solution)/shard_map/ppermute | solution.py:36
  190.1 1.8 collective-permute-start.30
  191.9 2.8 %collective-permute-done.21.refs_1_ = bf16[4,16,2048]{2,1,0:T(8,128)(2,1)S(1)} collective-permute-done((bf16[4,16,2048]{2,1,0:T(8,128)(2,1)S(1)}, bf16[4,16,2048]{2,1,0:T(8,128)(2,1)S(1)}, u32[]{:S(2)}, u32[]{:S(2)}) %collective-permute-start.21) | collective-permute-done | bytes 262176 | tf_op jit(solution)/shard_map/ppermute | solution.py:36
  197.1 2.5 %shard_map.121 = bf16[64,16,2048]{2,1,0:T(8,128)(2,1)} custom-call(s32[64]{0:T(128)S(1)} %copy-done.1, s32[1]{0:T(128)} %bitcast.8.me_ref, bf16[4,16,2048]{2,1,0:T(8,128)(2,1)S(1)} %pad_maximum_fusion.3.refs_0_, bf16[4,16,2048]{2,1,0:T(8,128)(2,1)S(1)} %collective-permute-done.21.refs_1_, bf16[4,16,2048]{2,1,0:T(8,128)(2,1)S(1)} %collective-permute-done.22.refs_2_, ...), custom_call_target="tpu_custom_call" | custom-call | tf_op jit(solution)/shard_map/pallas_call | solution.py:253
  (78 shorter events, 21.4 us)
Async XLA Ops:
  19.6 7.5 %collective-permute-start.1 = (bf16[32,16,2176]{2,1,0:T(8,128)(2,1)}, bf16[32,16,2176]{2,1,0:T(8,128)(2,1)S(1)}, u32[]{:S(2)}, u32[]{:S(2)}) collective-permute-start(bf16[32,16,2176]{2,1,0:T(8,128)(2,1)} %get-tuple-element.31), channel_id=1, source_target_pairs={{0,4},{4,0},{8,12},{12,8},{16,20},{20,16},{24,28},{28,24},{32,36},... | collective-permute-start | bytes 6684680 | tf_op jit(solution)/shard_map/ppermute | solution.py:36
  29.3 7.9 %collective-permute-start.7 = (bf16[4,16,2176]{2,1,0:T(8,128)(2,1)S(1)}, bf16[4,16,2176]{2,1,0:T(8,128)(2,1)S(1)}, u32[]{:S(2)}, u32[]{:S(2)}) collective-permute-start(bf16[4,16,2176]{2,1,0:T(8,128)(2,1)S(1)} %get-tuple-element.58), channel_id=1, source_target_pairs={{0,24},{4,28},{8,0},{12,4},{16,8},{20,12},{24,16},{28,20},{32,56},... | collective-permute-start | bytes 835592 | tf_op jit(solution)/shard_map/ppermute | solution.py:36
  30.4 14.2 %collective-permute-start.6 = (bf16[4,16,2176]{2,1,0:T(8,128)(2,1)S(1)}, bf16[4,16,2176]{2,1,0:T(8,128)(2,1)S(1)}, u32[]{:S(2)}, u32[]{:S(2)}) collective-permute-start(bf16[4,16,2176]{2,1,0:T(8,128)(2,1)S(1)} %get-tuple-element.59), channel_id=1, source_target_pairs={{0,8},{4,12},{8,16},{12,20},{16,24},{20,28},{24,0},{28,4},{32,40},... | collective-permute-start | bytes 835592 | tf_op jit(solution)/shard_map/ppermute | solution.py:36
  30.9 13.8 %collective-permute-start.5 = (bf16[4,16,2176]{2,1,0:T(8,128)(2,1)S(1)}, bf16[4,16,2176]{2,1,0:T(8,128)(2,1)S(1)}, u32[]{:S(2)}, u32[]{:S(2)}) collective-permute-start(bf16[4,16,2176]{2,1,0:T(8,128)(2,1)S(1)} %get-tuple-element.60), channel_id=1, source_target_pairs={{0,16},{4,20},{8,24},{12,28},{16,0},{20,4},{24,8},{28,12},{32,48},... | collective-permute-start | bytes 835592 | tf_op jit(solution)/shard_map/ppermute | solution.py:36
  32.1 12.6 %collective-permute-start.4 = (bf16[4,16,2176]{2,1,0:T(8,128)(2,1)S(1)}, bf16[4,16,2176]{2,1,0:T(8,128)(2,1)S(1)}, u32[]{:S(2)}, u32[]{:S(2)}) collective-permute-start(bf16[4,16,2176]{2,1,0:T(8,128)(2,1)S(1)} %get-tuple-element.61), channel_id=1, source_target_pairs={{0,96},{4,100},{8,104},{12,108},{16,112},{20,116},{24,120},{28,124... | collective-permute-start | bytes 835592 | tf_op jit(solution)/shard_map/ppermute | solution.py:36
  34.5 10.1 %collective-permute-start.3 = (bf16[4,16,2176]{2,1,0:T(8,128)(2,1)S(1)}, bf16[4,16,2176]{2,1,0:T(8,128)(2,1)S(1)}, u32[]{:S(2)}, u32[]{:S(2)}) collective-permute-start(bf16[4,16,2176]{2,1,0:T(8,128)(2,1)S(1)} %get-tuple-element.62), channel_id=1, source_target_pairs={{0,32},{4,36},{8,40},{12,44},{16,48},{20,52},{24,56},{28,60},{32,6... | collective-permute-start | bytes 835592 | tf_op jit(solution)/shard_map/ppermute | solution.py:36
  37.2 13.1 %collective-permute-start.2 = (bf16[4,16,2176]{2,1,0:T(8,128)(2,1)S(1)}, bf16[4,16,2176]{2,1,0:T(8,128)(2,1)S(1)}, u32[]{:S(2)}, u32[]{:S(2)}) collective-permute-start(bf16[4,16,2176]{2,1,0:T(8,128)(2,1)S(1)} %get-tuple-element.63), channel_id=1, source_target_pairs={{0,64},{4,68},{8,72},{12,76},{16,80},{20,84},{24,88},{28,92},{32,9... | collective-permute-start | bytes 835592 | tf_op jit(solution)/shard_map/ppermute | solution.py:36
  50.4 7.7 %collective-permute-start.10 = (bf16[16,2176]{1,0:T(8,128)(2,1)S(1)}, bf16[16,2176]{1,0:T(8,128)(2,1)S(1)}, u32[]{:S(2)}, u32[]{:S(2)}) collective-permute-start(bf16[16,2176]{1,0:T(8,128)(2,1)S(1)} %get-tuple-element.68), channel_id=1, source_target_pairs={{0,24},{4,28},{8,0},{12,4},{16,8},{20,12},{24,16},{28,20},{32,56},... | collective-permute-start | bytes 208904 | tf_op jit(solution)/shard_map/ppermute | solution.py:36
  54.2 5.6 %collective-permute-start.9 = (bf16[16,2176]{1,0:T(8,128)(2,1)S(1)}, bf16[16,2176]{1,0:T(8,128)(2,1)S(1)}, u32[]{:S(2)}, u32[]{:S(2)}) collective-permute-start(bf16[16,2176]{1,0:T(8,128)(2,1)S(1)} %get-tuple-element.69), channel_id=1, source_target_pairs={{0,8},{4,12},{8,16},{12,20},{16,24},{20,28},{24,0},{28,4},{32,40},... | collective-permute-start | bytes 208904 | tf_op jit(solution)/shard_map/ppermute | solution.py:36
  54.2 7.4 %collective-permute-start.8 = (bf16[16,2176]{1,0:T(8,128)(2,1)S(1)}, bf16[16,2176]{1,0:T(8,128)(2,1)S(1)}, u32[]{:S(2)}, u32[]{:S(2)}) collective-permute-start(bf16[16,2176]{1,0:T(8,128)(2,1)S(1)} %get-tuple-element.70), channel_id=1, source_target_pairs={{0,16},{4,20},{8,24},{12,28},{16,0},{20,4},{24,8},{28,12},{32,48},... | collective-permute-start | bytes 208904 | tf_op jit(solution)/shard_map/ppermute | solution.py:36
  55.6 6.0 %collective-permute-start.13 = (bf16[16,2176]{1,0:T(8,128)(2,1)S(1)}, bf16[16,2176]{1,0:T(8,128)(2,1)S(1)}, u32[]{:S(2)}, u32[]{:S(2)}) collective-permute-start(bf16[16,2176]{1,0:T(8,128)(2,1)S(1)} %get-tuple-element.65), channel_id=1, source_target_pairs={{0,96},{4,100},{8,104},{12,108},{16,112},{20,116},{24,120},{28,124... | collective-permute-start | bytes 208904 | tf_op jit(solution)/shard_map/ppermute | solution.py:36
  59.8 42.1 %collective-permute-start.35 = (s16[3,528,256]{2,1,0:T(8,128)(2,1)S(1)}, s16[3,528,256]{2,1,0:T(8,128)(2,1)S(1)}, u32[]{:S(2)}, u32[]{:S(2)}) collective-permute-start(s16[3,528,256]{2,1,0:T(8,128)(2,1)S(1)} %copy-done.2), channel_id=1, source_target_pairs={{0,1},{1,2},{2,3},{3,0},{4,5},{5,6},{6,7},{7,4},{8,9},{9,10},{10,1... | collective-permute-start | bytes 2433032 | tf_op jit(solution)/shard_map/ppermute | solution.py:277
  63.3 26.5 %collective-permute-start.14 = (f32[2,16,2176]{2,1,0:T(8,128)S(1)}, f32[2,16,2176]{2,1,0:T(8,128)S(1)}, u32[]{:S(2)}, u32[]{:S(2)}) collective-permute-start(f32[2,16,2176]{2,1,0:T(8,128)S(1)} %pad_maximum_fusion.1), channel_id=1, source_target_pairs={{0,128},{4,132},{8,136},{12,140},{16,144},{20,148},{24,152},{28,15... | collective-permute-start | bytes 835592 | tf_op jit(solution)/shard_map/ppermute | solution.py:36
  70.4 29.2 %collective-permute-start = (f32[3,16,2048]{2,1,0:T(8,128)S(1)}, f32[3,16,2048]{2,1,0:T(8,128)S(1)}, u32[]{:S(2)}, u32[]{:S(2)}) collective-permute-start(f32[3,16,2048]{2,1,0:T(8,128)S(1)} %get-tuple-element.72), channel_id=1, source_target_pairs={{0,128},{4,132},{8,136},{12,140},{16,144},{20,148},{24,152},{28,15... | collective-permute-start | bytes 1179656 | tf_op jit(solution)/shard_map/ppermute | solution.py:36
  79.9 49.1 %collective-permute-start.36 = (s16[3,528,256]{2,1,0:T(8,128)(2,1)}, s16[3,528,256]{2,1,0:T(8,128)(2,1)S(1)}, u32[]{:S(2)}, u32[]{:S(2)}) collective-permute-start(s16[3,528,256]{2,1,0:T(8,128)(2,1)} %get-tuple-element.51), channel_id=1, source_target_pairs={{0,3},{1,0},{2,1},{3,2},{4,7},{5,4},{6,5},{7,6},{8,11},{9,8},{10,9... | collective-permute-start | bytes 2433032 | tf_op jit(solution)/shard_map/ppermute | solution.py:277
  82.7 81.1 %collective-permute-start.37 = (s16[3,528,256]{2,1,0:T(8,128)(2,1)}, s16[3,528,256]{2,1,0:T(8,128)(2,1)S(1)}, u32[]{:S(2)}, u32[]{:S(2)}) collective-permute-start(s16[3,528,256]{2,1,0:T(8,128)(2,1)} %get-tuple-element.52), channel_id=1, source_target_pairs={{0,2},{1,3},{2,0},{3,1},{4,6},{5,7},{6,4},{7,5},{8,10},{9,11},{10,... | collective-permute-start | bytes 2433032 | tf_op jit(solution)/shard_map/ppermute | solution.py:277
  99.9 65.4 %collective-permute-start.20 = (bf16[1,16,2048]{2,1,0:T(8,128)(2,1)S(1)}, bf16[1,16,2048]{2,1,0:T(8,128)(2,1)S(1)}, u32[]{:S(2)}, u32[]{:S(2)}) collective-permute-start(bf16[1,16,2048]{2,1,0:T(8,128)(2,1)S(1)} %get-tuple-element.73), channel_id=1, source_target_pairs={{0,24},{4,28},{8,0},{12,4},{16,8},{20,12},{24,16},{28,20},{32,56},... | collective-permute-start | bytes 196616 | tf_op jit(solution)/shard_map/ppermute | solution.py:36
  101.1 67.2 %collective-permute-start.19 = (bf16[1,16,2048]{2,1,0:T(8,128)(2,1)S(1)}, bf16[1,16,2048]{2,1,0:T(8,128)(2,1)S(1)}, u32[]{:S(2)}, u32[]{:S(2)}) collective-permute-start(bf16[1,16,2048]{2,1,0:T(8,128)(2,1)S(1)} %get-tuple-element.73), channel_id=1, source_target_pairs={{0,8},{4,12},{8,16},{12,20},{16,24},{20,28},{24,0},{28,4},{32,40},... | collective-permute-start | bytes 196616 | tf_op jit(solution)/shard_map/ppermute | solution.py:36
  101.9 66.4 %collective-permute-start.18 = (bf16[1,16,2048]{2,1,0:T(8,128)(2,1)S(1)}, bf16[1,16,2048]{2,1,0:T(8,128)(2,1)S(1)}, u32[]{:S(2)}, u32[]{:S(2)}) collective-permute-start(bf16[1,16,2048]{2,1,0:T(8,128)(2,1)S(1)} %get-tuple-element.73), channel_id=1, source_target_pairs={{0,16},{4,20},{8,24},{12,28},{16,0},{20,4},{24,8},{28,12},{32,48},... | collective-permute-start | bytes 196616 | tf_op jit(solution)/shard_map/ppermute | solution.py:36
  129.0 39.4 %collective-permute-start.17 = (bf16[1,16,2048]{2,1,0:T(8,128)(2,1)S(1)}, bf16[1,16,2048]{2,1,0:T(8,128)(2,1)S(1)}, u32[]{:S(2)}, u32[]{:S(2)}) collective-permute-start(bf16[1,16,2048]{2,1,0:T(8,128)(2,1)S(1)} %get-tuple-element.74), channel_id=1, source_target_pairs={{0,96},{4,100},{8,104},{12,108},{16,112},{20,116},{24,120},{28,124... | collective-permute-start | bytes 196616 | tf_op jit(solution)/shard_map/ppermute | solution.py:36
  170.1 5.9 %collective-permute-start.31 = (bf16[4,16,2048]{2,1,0:T(8,128)(2,1)S(1)}, bf16[4,16,2048]{2,1,0:T(8,128)(2,1)S(1)}, u32[]{:S(2)}, u32[]{:S(2)}) collective-permute-start(bf16[4,16,2048]{2,1,0:T(8,128)(2,1)S(1)} %pad_maximum_fusion.4.refs_4_), channel_id=1, source_target_pairs={{0,4},{4,0},{8,12},{12,8},{16,20},{20,16},{24,28},{28,24},{32,36},... | collective-permute-start | bytes 786440 | tf_op jit(solution)/shard_map/ppermute | solution.py:36
  172.0 7.8 %collective-permute-start.26 = (bf16[4,16,2048]{2,1,0:T(8,128)(2,1)S(1)}, bf16[4,16,2048]{2,1,0:T(8,128)(2,1)S(1)}, u32[]{:S(2)}, u32[]{:S(2)}) collective-permute-start(bf16[4,16,2048]{2,1,0:T(8,128)(2,1)S(1)} %pad_maximum_fusion.4.refs_4_), channel_id=1, source_target_pairs={{0,96},{4,100},{8,104},{12,108},{16,112},{20,116},{24,120},{28,124... | collective-permute-start | bytes 786440 | tf_op jit(solution)/shard_map/ppermute | solution.py:36
  173.1 9.0 %collective-permute-start.25 = (bf16[4,16,2048]{2,1,0:T(8,128)(2,1)S(1)}, bf16[4,16,2048]{2,1,0:T(8,128)(2,1)S(1)}, u32[]{:S(2)}, u32[]{:S(2)}) collective-permute-start(bf16[4,16,2048]{2,1,0:T(8,128)(2,1)S(1)} %pad_maximum_fusion.4.refs_4_), channel_id=1, source_target_pairs={{0,64},{4,68},{8,72},{12,76},{16,80},{20,84},{24,88},{28,92},{32,9... | collective-permute-start | bytes 786440 | tf_op jit(solution)/shard_map/ppermute | solution.py:36
  174.0 14.5 %collective-permute-start.24 = (bf16[4,16,2048]{2,1,0:T(8,128)(2,1)S(1)}, bf16[4,16,2048]{2,1,0:T(8,128)(2,1)S(1)}, u32[]{:S(2)}, u32[]{:S(2)}) collective-permute-start(bf16[4,16,2048]{2,1,0:T(8,128)(2,1)S(1)} %pad_maximum_fusion.4.refs_4_), channel_id=1, source_target_pairs={{0,32},{4,36},{8,40},{12,44},{16,48},{20,52},{24,56},{28,60},{32,6... | collective-permute-start | bytes 786440 | tf_op jit(solution)/shard_map/ppermute | solution.py:36
  175.0 14.6 %collective-permute-start.27 = (bf16[4,16,2048]{2,1,0:T(8,128)(2,1)S(1)}, bf16[4,16,2048]{2,1,0:T(8,128)(2,1)S(1)}, u32[]{:S(2)}, u32[]{:S(2)}) collective-permute-start(bf16[4,16,2048]{2,1,0:T(8,128)(2,1)S(1)} %pad_maximum_fusion.3.refs_0_), channel_id=1, source_target_pairs={{0,4},{4,0},{8,12},{12,8},{16,20},{20,16},{24,28},{28,24},{32,36},... | collective-permute-start | bytes 786440 | tf_op jit(solution)/shard_map/ppermute | solution.py:36
  176.0 13.6 %collective-permute-start.23 = (bf16[4,16,2048]{2,1,0:T(8,128)(2,1)S(1)}, bf16[4,16,2048]{2,1,0:T(8,128)(2,1)S(1)}, u32[]{:S(2)}, u32[]{:S(2)}) collective-permute-start(bf16[4,16,2048]{2,1,0:T(8,128)(2,1)S(1)} %pad_maximum_fusion.3.refs_0_), channel_id=1, source_target_pairs={{0,24},{4,28},{8,0},{12,4},{16,8},{20,12},{24,16},{28,20},{32,56},... | collective-permute-start | bytes 786440 | tf_op jit(solution)/shard_map/ppermute | solution.py:36
  179.8 10.4 %collective-permute-start.22 = (bf16[4,16,2048]{2,1,0:T(8,128)(2,1)S(1)}, bf16[4,16,2048]{2,1,0:T(8,128)(2,1)S(1)}, u32[]{:S(2)}, u32[]{:S(2)}) collective-permute-start(bf16[4,16,2048]{2,1,0:T(8,128)(2,1)S(1)} %pad_maximum_fusion.3.refs_0_), channel_id=1, source_target_pairs={{0,16},{4,20},{8,24},{12,28},{16,0},{20,4},{24,8},{28,12},{32,48},... | collective-permute-start | bytes 786440 | tf_op jit(solution)/shard_map/ppermute | solution.py:36
  182.1 12.6 %collective-permute-start.21 = (bf16[4,16,2048]{2,1,0:T(8,128)(2,1)S(1)}, bf16[4,16,2048]{2,1,0:T(8,128)(2,1)S(1)}, u32[]{:S(2)}, u32[]{:S(2)}) collective-permute-start(bf16[4,16,2048]{2,1,0:T(8,128)(2,1)S(1)} %pad_maximum_fusion.3.refs_0_), channel_id=1, source_target_pairs={{0,8},{4,12},{8,16},{12,20},{16,24},{20,28},{24,0},{28,4},{32,40},... | collective-permute-start | bytes 786440 | tf_op jit(solution)/shard_map/ppermute | solution.py:36
  188.4 7.2 %collective-permute-start.34 = (bf16[4,16,2048]{2,1,0:T(8,128)(2,1)S(1)}, bf16[4,16,2048]{2,1,0:T(8,128)(2,1)S(1)}, u32[]{:S(2)}, u32[]{:S(2)}) collective-permute-start(bf16[4,16,2048]{2,1,0:T(8,128)(2,1)S(1)} %collective-permute-done.26.refs_7_), channel_id=1, source_target_pairs={{0,4},{4,0},{8,12},{12,8},{16,20},{20,16},{24,28},{28,24},{32,36},... | collective-permute-start | bytes 786440 | tf_op jit(solution)/shard_map/ppermute | solution.py:36
  189.6 6.6 %collective-permute-start.33 = (bf16[4,16,2048]{2,1,0:T(8,128)(2,1)S(1)}, bf16[4,16,2048]{2,1,0:T(8,128)(2,1)S(1)}, u32[]{:S(2)}, u32[]{:S(2)}) collective-permute-start(bf16[4,16,2048]{2,1,0:T(8,128)(2,1)S(1)} %collective-permute-done.25.refs_6_), channel_id=1, source_target_pairs={{0,4},{4,0},{8,12},{12,8},{16,20},{20,16},{24,28},{28,24},{32,36},... | collective-permute-start | bytes 786440 | tf_op jit(solution)/shard_map/ppermute | solution.py:36
  189.6 6.6 %collective-permute-start.32 = (bf16[4,16,2048]{2,1,0:T(8,128)(2,1)S(1)}, bf16[4,16,2048]{2,1,0:T(8,128)(2,1)S(1)}, u32[]{:S(2)}, u32[]{:S(2)}) collective-permute-start(bf16[4,16,2048]{2,1,0:T(8,128)(2,1)S(1)} %collective-permute-done.24.refs_5_), channel_id=1, source_target_pairs={{0,4},{4,0},{8,12},{12,8},{16,20},{20,16},{24,28},{28,24},{32,36},... | collective-permute-start | bytes 786440 | tf_op jit(solution)/shard_map/ppermute | solution.py:36
  190.1 6.1 %collective-permute-start.30 = (bf16[4,16,2048]{2,1,0:T(8,128)(2,1)S(1)}, bf16[4,16,2048]{2,1,0:T(8,128)(2,1)S(1)}, u32[]{:S(2)}, u32[]{:S(2)}) collective-permute-start(bf16[4,16,2048]{2,1,0:T(8,128)(2,1)S(1)} %collective-permute-done.23.refs_3_), channel_id=1, source_target_pairs={{0,4},{4,0},{8,12},{12,8},{16,20},{20,16},{24,28},{28,24},{32,36},... | collective-permute-start | bytes 786440 | tf_op jit(solution)/shard_map/ppermute | solution.py:36
  (12 other events, 285.7 us)

commit v2 on v1

--- a/solution.py
+++ b/solution.py
@@ -59,7 +59,24 @@
     return index_of(1 - my_zh if zh else my_zh, x, y, 1 - my_core if core else my_core)
 
 
-def weight_partials(acts, grads, count, owner_map, me, interpret=False):
+def encode(share, out, at):
+    tall, width = share.shape
+    groups = tall // GROUP
+    largest = jnp.max(jnp.abs(share).reshape(groups, GROUP, width), axis=1)
+    largest = jnp.max(largest, axis=1, keepdims=True)
+    power = jnp.floor(jnp.log2(32000.0 / jnp.maximum(largest, 1e-25)))
+    power = jnp.broadcast_to(jnp.minimum(power, 90.0), (groups, width))
+    factor = jnp.exp2(power)
+    for g in range(groups):
+        code = jnp.round(share[g * GROUP : (g + 1) * GROUP] * factor[g : g + 1])
+        out[at, g * GROUP : (g + 1) * GROUP, :] = code.astype(jnp.int32).astype(i16)
+    out[at, tall : tall + groups, :] = power.astype(jnp.int32).astype(i16)
+
+
+TALL = 512
+
+
+def weight_partials(acts, grads, weight, count, owner_map, me, mine, ways, interpret=False):
     tokens, hidden = acts.shape
     columns = grads.shape[1]
     blocks = owner_map.shape[0]
@@ -70,8 +87,27 @@
     chunk = 512
     parts = tokens // chunk
 
-    def kernel(count_ref, map_ref, me_ref, acts_ref, grads_ref, keep_ref, send_ref, raw, turned, part, sems):
+    width = hidden // ways
+    extra = TALL // GROUP
+
+    def kernel(
+        count_ref, map_ref, me_ref, mine_ref, acts_ref, grads_ref, weight_ref,
+        keep_ref, send_ref, up_ref, raw, turned, part, total, sems,
+    ):
         step = pl.program_id(0)
+
+        def add_up():
+            value = lax.dot_general(
+                grads_ref[...], weight_ref[...], (((1,), (1,)), ((), ())), preferred_element_type=f32
+            )
+
+            @pl.when(step == 0)
+            def _():
+                total[...] = value
+
+            @pl.when(step > 0)
+            def _():
+                total[...] += value
 
         def put():
             for p in range(blocks):
@@ -101,11 +137,13 @@
                 else:
                     part[...] += value
             put()
+            add_up()
 
         @pl.when((step > 0) & (step < steps))
         def _():
             part[...] = jnp.dot(turned[...], grads_ref[...], preferred_element_type=f32)
             put()
+            add_up()
 
         @pl.when(step == steps)
         def _():
@@ -114,37 +152,50 @@
             value = digit.astype(f32).astype(bf16)
             keep_ref[:, :, :EXTRA] = value
             send_ref[:, :, :EXTRA] = value
+            for i in range(tokens // TALL):
+                live = lax.broadcasted_iota(jnp.int32, (TALL, width), 0) + i * TALL < count_ref[0]
+                encode(jnp.where(live, total[i * TALL : (i + 1) * TALL], 0.0), up_ref, i)
 
     out = jax.ShapeDtypeStruct((near, height, columns + EXTRA), bf16)
-    spec = pl.BlockSpec((near, height, wide), lambda n: (0, 0, n))
+    spec = pl.BlockSpec((near, height, wide), lambda n, *_: (0, 0, n))
+    code = (tokens // TALL, TALL + extra, width)
     return pl.pallas_call(
         kernel,
-        grid=(steps + 1,),
-        out_shape=(out, out),
-        in_specs=[pl.BlockSpec(memory_space=pltpu.SMEM)] * 3
-        + [
-            pl.BlockSpec(memory_space=pl.ANY),
-            pl.BlockSpec((tokens, wide), lambda n: (0, jnp.minimum(n, steps - 1))),
-        ],
-        out_specs=(spec, spec),
-        scratch_shapes=[
-            pltpu.VMEM((tokens, hidden), bf16),
-            pltpu.VMEM((hidden, tokens), bf16),
-            pltpu.VMEM((hidden, wide), f32),
-            pltpu.SemaphoreType.DMA((parts,)),
-        ],
+        grid_spec=pltpu.PrefetchScalarGridSpec(
+            num_scalar_prefetch=4,
+            grid=(steps + 1,),
+            in_specs=[
+                pl.BlockSpec(memory_space=pl.ANY),
+                pl.BlockSpec((tokens, wide), lambda n, *_: (0, jnp.minimum(n, steps - 1))),
+                pl.BlockSpec(
+                    (width, wide),
+                    lambda n, count, map, me, mine: (
+                        lax.rem(mine[0] + 1, ways),
+                        jnp.minimum(n, steps - 1),
+                    ),
+                ),
+            ],
+            out_specs=[spec, spec, pl.BlockSpec(code, lambda n, *_: (0, 0, 0))],
+            scratch_shapes=[
+                pltpu.VMEM((tokens, hidden), bf16),
+                pltpu.VMEM((hidden, tokens), bf16),
+                pltpu.VMEM((hidden, wide), f32),
+                pltpu.VMEM((tokens, width), f32),
+                pltpu.SemaphoreType.DMA((parts,)),
+            ],
+        ),
+        out_shape=[out, out, jax.ShapeDtypeStruct(code, i16)],
         compiler_params=pltpu.CompilerParams(vmem_limit_bytes=60 * 2**20),
         interpret=interpret,
-    )(count, owner_map, me, acts, grads)
+    )(count, owner_map, me, mine, acts, grads, weight)
 
 
 def input_shares(grads, weight, count, mine, ways, offsets, interpret=False):
     tokens, columns = grads.shape
     hidden = weight.shape[0]
     width = hidden // ways
-    tall = 512
-    groups = tall // GROUP
-    extra = 16
+    tall = TALL
+    extra = tall // GROUP
 
     def kernel(count_ref, mine_ref, grads_ref, *refs):
         step = pl.program_id(0)
@@ -157,15 +208,7 @@
             if offset == 0:
                 out[...] = share
                 continue
-            largest = jnp.max(jnp.abs(share).reshape(groups, GROUP, width), axis=1)
-            largest = jnp.max(largest, axis=1, keepdims=True)
-            power = jnp.floor(jnp.log2(32000.0 / jnp.maximum(largest, 1e-25)))
-            power = jnp.broadcast_to(jnp.minimum(power, 90.0), (groups, width))
-            factor = jnp.exp2(power)
-            for g in range(groups):
-                code = jnp.round(share[g * GROUP : (g + 1) * GROUP] * factor[g : g + 1])
-                out[0, g * GROUP : (g + 1) * GROUP, :] = code.astype(jnp.int32).astype(i16)
-            out[0, tall : tall + extra, :] = power.astype(jnp.int32).astype(i16)
+            encode(share, out, 0)
 
     def part_of(offset):
         return pl.BlockSpec(
@@ -276,11 +319,11 @@
         ring = [(source, (source + offset) % ways) for source in range(ways)]
         return lax.ppermute(coded, "mp", ring)
 
-    (up,) = input_shares(out_grads, down_weight, token_counts, my_mp, ways, (1,))
+    keep, send, up = weight_partials(
+        hidden_acts, out_grads, down_weight, token_counts, owner_map, me, my_mp, ways
+    )
+    arrived = to_core(send)
     shares = [pass_share(up, 1)]
-    acts, _ = lax.optimization_barrier((hidden_acts, up))
-    keep, send = weight_partials(acts, out_grads, token_counts, owner_map, me)
-    arrived = to_core(send)
     states = jnp.stack([master, moment1, moment2.astype(f32)])
     other_states = to_zh(states)
 
@@ -293,9 +336,7 @@
         for colour, (first, _) in enumerate(rings)
     ]
     got = lax.optimization_barrier(got)
-    down, across, own = input_shares(
-        out_grads, down_weight, token_counts, my_mp, ways, (3, 2, 0)
-    )
+    (down,) = input_shares(out_grads, down_weight, token_counts, my_mp, ways, (3,))
     shares.append(pass_share(down, 3))
     lines = [
         [
@@ -314,6 +355,7 @@
     ]
     sums = lax.optimization_barrier(jnp.stack(sums))
     theirs = to_zh(sums)
+    across, own = input_shares(out_grads, down_weight, token_counts, my_mp, ways, (2, 0))
     shares.append(pass_share(across, 2))
 
     summed = sums + theirs[::-1]

time: 200 us -> 194 us (0.970)
  starting transfers between devices: 58.9 us -> 54.4 us
  waiting for transfers between devices: 102 us -> 99.5 us
    ppermute x35, waiting for transfers between devices: 44.1 us -> 24.3 us  [move(): return lax.ppermute(value, 'dp', pairs)]
    ppermute x3, waiting for transfers between devices: 58.3 us -> 75.2 us  [pass_share(): return lax.ppermute(coded, 'mp', ring)]
    ppermute x35, starting transfers between devices: 54.4 us -> 51.1 us  [move(): return lax.ppermute(value, 'dp', pairs)]
    pallas_call x1, Pallas kernels: 12.3 us -> 15.4 us  [weight_partials(): pl.pallas_call(kernel, grid_spec=pltpu.PrefetchScalarGridSpec(num_scalar_...]
  transfers between devices with their start and end apart: 38 -> 38, of which waited for: 15 -> 14; matrix products, arithmetic and copies ran while one was open for 1% -> 1% of each run, Pallas kernels for 5% -> 8%
where the time goes in v2:
time: 194 us
  waiting for transfers between devices  99.5 us (51%)
  starting transfers between devices  54.4 us (28%)
  Pallas kernels  33.1 us (17%)
  other arithmetic  3.08 us (2%)
  local copies, waits for them, and re-layouts  2.01 us (1%)
    ppermute x3, waiting for transfers between devices, pass_share(): return lax.ppermute(coded, 'mp', ring)  75.2 us
    ppermute x35, starting transfers between devices, move(): return lax.ppermute(value, 'dp', pairs)  51.1 us
    ppermute x35, waiting for transfers between devices, move(): return lax.ppermute(value, 'dp', pairs)  24.3 us
    pallas_call x1, Pallas kernels, weight_partials(): pl.pallas_call(kernel, grid_spec=pltpu.PrefetchScalarGridSpec(num_scalar_...  15.4 us
    pallas_call x2, Pallas kernels, input_shares(): pl.pallas_call(kernel, grid_spec=pltpu.PrefetchScalarGridSpec(num_scalar_...  13.5 us
  transfers between devices with their start and end apart: 38, of which 14 were waited for; matrix products, arithmetic and copies ran while one was open for 1% of the time, Pallas kernels for 8%

profile of v2, /device:TPU:1, one launch (start us, length us, event | category | flops | bytes accessed | tf_op | source)
XLA Modules:
  0.0 193.7 jit_solution(443707479954487194)
XLA Ops:
  1.3 15.4 %shard_map.119 = (bf16[32,16,2176]{2,1,0:T(8,128)(2,1)}, bf16[32,16,2176]{2,1,0:T(8,128)(2,1)}, s16[3,528,256]{2,1,0:T(8,128)(2,1)}) custom-call(s32[1]{0:T(128)S(6)} %copy.14.count_ref, s32[64]{0:T(128)} %map_ref.3, s32[1]{0:T(128)} %bitcast.8.me_ref, s32[1]{0:T(128)} %bitcast.9.mine_ref, bf16[1536,1024]{1,0:T(8,128)(2,1)} %acts_ref.1, ...), custom_call_target="tpu_custom_call" | custom-call | tf_op jit(solution)/shard_map/pallas_call | solution.py:162
  16.7 3.3 %collective-permute-start.1 = (bf16[32,16,2176]{2,1,0:T(8,128)(2,1)}, bf16[32,16,2176]{2,1,0:T(8,128)(2,1)S(1)}, u32[]{:S(2)}, u32[]{:S(2)}) collective-permute-start(bf16[32,16,2176]{2,1,0:T(8,128)(2,1)} %get-tuple-element.29), channel_id=1, source_target_pairs={{0,4},{4,0},{8,12},{12,8},{16,20},{20,16},{24,28},{28,24},{32,36},... | collective-permute-start | bytes 6684680 | tf_op jit(solution)/shard_map/ppermute | solution.py:36
  20.0 4.2 %collective-permute-done.1 = bf16[32,16,2176]{2,1,0:T(8,128)(2,1)S(1)} collective-permute-done((bf16[32,16,2176]{2,1,0:T(8,128)(2,1)}, bf16[32,16,2176]{2,1,0:T(8,128)(2,1)S(1)}, u32[]{:S(2)}, u32[]{:S(2)}) %collective-permute-start.1) | collective-permute-done | bytes 2228256 | tf_op jit(solution)/shard_map/ppermute | solution.py:36
  24.2 2.2 %add_convert_fusion = (bf16[4,16,2176]{2,1,0:T(8,128)(2,1)S(1)}, bf16[4,16,2176]{2,1,0:T(8,128)(2,1)S(1)}, bf16[4,16,2176]{2,1,0:T(8,128)(2,1)S(1)}, bf16[4,16,2...) fusion(bf16[32,16,2176]{2,1,0:T(8,128)(2,1)S(1)} %collective-pe, ...), kind=kLoop, calls=%fused_computation.4 | loop fusion | flops 4456448 | bytes 6684672 | tf_op jit(solution)/shard_map/convert_element_type | solution.py:331
  27.8 2.4 %collective-permute-start.4 = (bf16[4,16,2176]{2,1,0:T(8,128)(2,1)S(1)}, bf16[4,16,2176]{2,1,0:T(8,128)(2,1)S(1)}, u32[]{:S(2)}, u32[]{:S(2)}) collective-permute-start(bf16[4,16,2176]{2,1,0:T(8,128)(2,1)S(1)} %get-tuple-element.59), channel_id=1, source_target_pairs={{0,96},{4,100},{8,104},{12,108},{16,112},{20,116},{24,120},{28,124... | collective-permute-start | bytes 835592 | tf_op jit(solution)/shard_map/ppermute | solution.py:36
  30.2 2.9 %collective-permute-start.5 = (bf16[4,16,2176]{2,1,0:T(8,128)(2,1)S(1)}, bf16[4,16,2176]{2,1,0:T(8,128)(2,1)S(1)}, u32[]{:S(2)}, u32[]{:S(2)}) collective-permute-start(bf16[4,16,2176]{2,1,0:T(8,128)(2,1)S(1)} %get-tuple-element.58), channel_id=1, source_target_pairs={{0,16},{4,20},{8,24},{12,28},{16,0},{20,4},{24,8},{28,12},{32,48},... | collective-permute-start | bytes 835592 | tf_op jit(solution)/shard_map/ppermute | solution.py:36
  33.5 2.4 %collective-permute-done.2 = bf16[4,16,2176]{2,1,0:T(8,128)(2,1)S(1)} collective-permute-done((bf16[4,16,2176]{2,1,0:T(8,128)(2,1)S(1)}, bf16[4,16,2176]{2,1,0:T(8,128)(2,1)S(1)}, u32[]{:S(2)}, u32[]{:S(2)}) %collective-permute-start.2) | collective-permute-done | bytes 278560 | tf_op jit(solution)/shard_map/ppermute | solution.py:36
  36.9 5.6 %collective-permute-done.3 = bf16[4,16,2176]{2,1,0:T(8,128)(2,1)S(1)} collective-permute-done((bf16[4,16,2176]{2,1,0:T(8,128)(2,1)S(1)}, bf16[4,16,2176]{2,1,0:T(8,128)(2,1)S(1)}, u32[]{:S(2)}, u32[]{:S(2)}) %collective-permute-start.3) | collective-permute-done | bytes 278560 | tf_op jit(solution)/shard_map/ppermute | solution.py:36
  42.5 3.7 %collective-permute-done.6 = bf16[4,16,2176]{2,1,0:T(8,128)(2,1)S(1)} collective-permute-done((bf16[4,16,2176]{2,1,0:T(8,128)(2,1)S(1)}, bf16[4,16,2176]{2,1,0:T(8,128)(2,1)S(1)}, u32[]{:S(2)}, u32[]{:S(2)}) %collective-permute-start.6) | collective-permute-done | bytes 278560 | tf_op jit(solution)/shard_map/ppermute | solution.py:36
  46.3 1.5 collective-permute-start.8
  48.9 1.6 collective-permute-start.10
  51.3 2.7 %collective-permute-start.13 = (bf16[16,2176]{1,0:T(8,128)(2,1)S(1)}, bf16[16,2176]{1,0:T(8,128)(2,1)S(1)}, u32[]{:S(2)}, u32[]{:S(2)}) collective-permute-start(bf16[16,2176]{1,0:T(8,128)(2,1)S(1)} %get-tuple-element.63), channel_id=1, source_target_pairs={{0,96},{4,100},{8,104},{12,108},{16,112},{20,116},{24,120},{28,124... | collective-permute-start | bytes 208904 | tf_op jit(solution)/shard_map/ppermute | solution.py:36
  54.1 1.3 collective-permute-done.11
  56.2 6.8 %collective-permute-start.14 = (f32[2,16,2176]{2,1,0:T(8,128)S(1)}, f32[2,16,2176]{2,1,0:T(8,128)S(1)}, u32[]{:S(2)}, u32[]{:S(2)}) collective-permute-start(f32[2,16,2176]{2,1,0:T(8,128)S(1)} %pad_maximum_fusion.1), channel_id=1, source_target_pairs={{0,128},{4,132},{8,136},{12,140},{16,144},{20,148},{24,152},{28,15... | collective-permute-start | bytes 835592 | tf_op jit(solution)/shard_map/ppermute | solution.py:36
  64.0 6.0 %shard_map.122 = s16[3,528,256]{2,1,0:T(8,128)(2,1)} custom-call(s32[1]{0:T(128)S(6)} %copy.14.count_ref, s32[1]{0:T(128)} %bitcast.9.mine_ref, bf16[1536,2048]{1,0:T(8,128)(2,1)} %grads_ref.5, bf16[1024,2048]{1,0:T(8,128)(2,1)} %refs_0_.3), custom_call_target="tpu_custom_call" | custom-call | tf_op jit(solution)/shard_map/pallas_call | solution.py:222
  70.0 2.5 %collective-permute-start.36 = (s16[3,528,256]{2,1,0:T(8,128)(2,1)}, s16[3,528,256]{2,1,0:T(8,128)(2,1)S(1)}, u32[]{:S(2)}, u32[]{:S(2)}) collective-permute-start(s16[3,528,256]{2,1,0:T(8,128)(2,1)} %shard_map.122), channel_id=1, source_target_pairs={{0,3},{1,0},{2,1},{3,2},{4,7},{5,4},{6,5},{7,6},{8,11},{9,8},{10,9... | collective-permute-start | bytes 2433032 | tf_op jit(solution)/shard_map/ppermute | solution.py:320
  72.6 7.5 %shard_map.121 = (s16[3,528,256]{2,1,0:T(8,128)(2,1)}, f32[1536,256]{1,0:T(8,128)}) custom-call(s32[1]{0:T(128)S(6)} %copy.14.count_ref, s32[1]{0:T(128)} %bitcast.9.mine_ref, bf16[1536,2048]{1,0:T(8,128)(2,1)} %grads_ref.5, bf16[1024,2048]{1,0:T(8,128)(2,1)} %refs_0_.3, bf16[1024,2048]{1,0:T(8,128)(2,1)} %refs_0_.3), custom_call_target="tpu_custom_call" | custom-call | tf_op jit(solution)/shard_map/pallas_call | solution.py:222
  80.2 1.6 collective-permute-done
  84.1 23.3 %collective-permute-done.35.refs_0_ = s16[3,528,256]{2,1,0:T(8,128)(2,1)S(1)} collective-permute-done((s16[3,528,256]{2,1,0:T(8,128)(2,1)}, s16[3,528,256]{2,1,0:T(8,128)(2,1)S(1)}, u32[]{:S(2)}, u32[]{:S(2)}) %collective-permute-start.35) | collective-permute-done | bytes 811040 | tf_op jit(solution)/shard_map/ppermute | solution.py:320
  107.4 3.1 %collective-permute-start.17 = (bf16[1,16,2048]{2,1,0:T(8,128)(2,1)S(1)}, bf16[1,16,2048]{2,1,0:T(8,128)(2,1)S(1)}, u32[]{:S(2)}, u32[]{:S(2)}) collective-permute-start(bf16[1,16,2048]{2,1,0:T(8,128)(2,1)S(1)} %get-tuple-element.72), channel_id=1, source_target_pairs={{0,96},{4,100},{8,104},{12,108},{16,112},{20,116},{24,120},{28,124... | collective-permute-start | bytes 196616 | tf_op jit(solution)/shard_map/ppermute | solution.py:36
  110.5 16.1 %collective-permute-done.36.refs_1_ = s16[3,528,256]{2,1,0:T(8,128)(2,1)S(1)} collective-permute-done((s16[3,528,256]{2,1,0:T(8,128)(2,1)}, s16[3,528,256]{2,1,0:T(8,128)(2,1)S(1)}, u32[]{:S(2)}, u32[]{:S(2)}) %collective-permute-start.36) | collective-permute-done | bytes 811040 | tf_op jit(solution)/shard_map/ppermute | solution.py:320
  127.1 35.8 %collective-permute-done.37.refs_2_ = s16[3,528,256]{2,1,0:T(8,128)(2,1)S(1)} collective-permute-done((s16[3,528,256]{2,1,0:T(8,128)(2,1)}, s16[3,528,256]{2,1,0:T(8,128)(2,1)S(1)}, u32[]{:S(2)}, u32[]{:S(2)}) %collective-permute-start.37) | collective-permute-done | bytes 811040 | tf_op jit(solution)/shard_map/ppermute | solution.py:320
  163.0 2.7 %collective-permute-start.20 = (bf16[1,16,2048]{2,1,0:T(8,128)(2,1)S(1)}, bf16[1,16,2048]{2,1,0:T(8,128)(2,1)S(1)}, u32[]{:S(2)}, u32[]{:S(2)}) collective-permute-start(bf16[1,16,2048]{2,1,0:T(8,128)(2,1)S(1)} %get-tuple-element.71), channel_id=1, source_target_pairs={{0,24},{4,28},{8,0},{12,4},{16,8},{20,12},{24,16},{28,20},{32,56},... | collective-permute-start | bytes 196616 | tf_op jit(solution)/shard_map/ppermute | solution.py:36
  165.7 1.6 shard_map.123
  167.7 3.8 %collective-permute-start.22 = (bf16[4,16,2048]{2,1,0:T(8,128)(2,1)S(1)}, bf16[4,16,2048]{2,1,0:T(8,128)(2,1)S(1)}, u32[]{:S(2)}, u32[]{:S(2)}) collective-permute-start(bf16[4,16,2048]{2,1,0:T(8,128)(2,1)S(1)} %pad_maximum_fusion.3.refs_0_), channel_id=1, source_target_pairs={{0,16},{4,20},{8,24},{12,28},{16,0},{20,4},{24,8},{28,12},{32,48},... | collective-permute-start | bytes 786440 | tf_op jit(solution)/shard_map/ppermute | solution.py:36
  171.5 1.7 collective-permute-start.24
  173.9 2.2 %collective-permute-start.25 = (bf16[4,16,2048]{2,1,0:T(8,128)(2,1)S(1)}, bf16[4,16,2048]{2,1,0:T(8,128)(2,1)S(1)}, u32[]{:S(2)}, u32[]{:S(2)}) collective-permute-start(bf16[4,16,2048]{2,1,0:T(8,128)(2,1)S(1)} %pad_maximum_fusion.4.refs_4_), channel_id=1, source_target_pairs={{0,64},{4,68},{8,72},{12,76},{16,80},{20,84},{24,88},{28,92},{32,9... | collective-permute-start | bytes 786440 | tf_op jit(solution)/shard_map/ppermute | solution.py:36
  176.2 1.6 collective-permute-start.26
  177.8 3.8 %collective-permute-done.22.refs_2_ = bf16[4,16,2048]{2,1,0:T(8,128)(2,1)S(1)} collective-permute-done((bf16[4,16,2048]{2,1,0:T(8,128)(2,1)S(1)}, bf16[4,16,2048]{2,1,0:T(8,128)(2,1)S(1)}, u32[]{:S(2)}, u32[]{:S(2)}) %collective-permute-start.22) | collective-permute-done | bytes 262176 | tf_op jit(solution)/shard_map/ppermute | solution.py:36
  181.6 2.8 %collective-permute-start.27 = (bf16[4,16,2048]{2,1,0:T(8,128)(2,1)S(1)}, bf16[4,16,2048]{2,1,0:T(8,128)(2,1)S(1)}, u32[]{:S(2)}, u32[]{:S(2)}) collective-permute-start(bf16[4,16,2048]{2,1,0:T(8,128)(2,1)S(1)} %pad_maximum_fusion.3.refs_0_), channel_id=1, source_target_pairs={{0,4},{4,0},{8,12},{12,8},{16,20},{20,16},{24,28},{28,24},{32,36},... | collective-permute-start | bytes 786440 | tf_op jit(solution)/shard_map/ppermute | solution.py:36
  185.6 2.8 %collective-permute-start.29 = (bf16[4,16,2048]{2,1,0:T(8,128)(2,1)S(1)}, bf16[4,16,2048]{2,1,0:T(8,128)(2,1)S(1)}, u32[]{:S(2)}, u32[]{:S(2)}) collective-permute-start(bf16[4,16,2048]{2,1,0:T(8,128)(2,1)S(1)} %collective-permute-done.22.refs_2_), channel_id=1, source_target_pairs={{0,4},{4,0},{8,12},{12,8},{16,20},{20,16},{24,28},{28,24},{32,36},... | collective-permute-start | bytes 786440 | tf_op jit(solution)/shard_map/ppermute | solution.py:36
  191.0 2.5 %shard_map.120 = bf16[64,16,2048]{2,1,0:T(8,128)(2,1)} custom-call(s32[64]{0:T(128)S(1)} %copy-done.1, s32[1]{0:T(128)} %bitcast.8.me_ref, bf16[4,16,2048]{2,1,0:T(8,128)(2,1)S(1)} %pad_maximum_fusion.3.refs_0_, bf16[4,16,2048]{2,1,0:T(8,128)(2,1)S(1)} %collective-permute-done.21.refs_1_, bf16[4,16,2048]{2,1,0:T(8,128)(2,1)S(1)} %collective-permute-done.22.refs_2_, ...), custom_call_target="tpu_custom_call" | custom-call | tf_op jit(solution)/shard_map/pallas_call | solution.py:296
  (76 shorter events, 14.7 us)
Async XLA Ops:
  16.7 7.5 %collective-permute-start.1 = (bf16[32,16,2176]{2,1,0:T(8,128)(2,1)}, bf16[32,16,2176]{2,1,0:T(8,128)(2,1)S(1)}, u32[]{:S(2)}, u32[]{:S(2)}) collective-permute-start(bf16[32,16,2176]{2,1,0:T(8,128)(2,1)} %get-tuple-element.29), channel_id=1, source_target_pairs={{0,4},{4,0},{8,12},{12,8},{16,20},{20,16},{24,28},{28,24},{32,36},... | collective-permute-start | bytes 6684680 | tf_op jit(solution)/shard_map/ppermute | solution.py:36
  26.4 9.5 %collective-permute-start.2 = (bf16[4,16,2176]{2,1,0:T(8,128)(2,1)S(1)}, bf16[4,16,2176]{2,1,0:T(8,128)(2,1)S(1)}, u32[]{:S(2)}, u32[]{:S(2)}) collective-permute-start(bf16[4,16,2176]{2,1,0:T(8,128)(2,1)S(1)} %get-tuple-element.61), channel_id=1, source_target_pairs={{0,64},{4,68},{8,72},{12,76},{16,80},{20,84},{24,88},{28,92},{32,9... | collective-permute-start | bytes 835592 | tf_op jit(solution)/shard_map/ppermute | solution.py:36
  27.5 15.0 %collective-permute-start.3 = (bf16[4,16,2176]{2,1,0:T(8,128)(2,1)S(1)}, bf16[4,16,2176]{2,1,0:T(8,128)(2,1)S(1)}, u32[]{:S(2)}, u32[]{:S(2)}) collective-permute-start(bf16[4,16,2176]{2,1,0:T(8,128)(2,1)S(1)} %get-tuple-element.60), channel_id=1, source_target_pairs={{0,32},{4,36},{8,40},{12,44},{16,48},{20,52},{24,56},{28,60},{32,6... | collective-permute-start | bytes 835592 | tf_op jit(solution)/shard_map/ppermute | solution.py:36
  27.8 14.7 %collective-permute-start.4 = (bf16[4,16,2176]{2,1,0:T(8,128)(2,1)S(1)}, bf16[4,16,2176]{2,1,0:T(8,128)(2,1)S(1)}, u32[]{:S(2)}, u32[]{:S(2)}) collective-permute-start(bf16[4,16,2176]{2,1,0:T(8,128)(2,1)S(1)} %get-tuple-element.59), channel_id=1, source_target_pairs={{0,96},{4,100},{8,104},{12,108},{16,112},{20,116},{24,120},{28,124... | collective-permute-start | bytes 835592 | tf_op jit(solution)/shard_map/ppermute | solution.py:36
  30.2 12.3 %collective-permute-start.5 = (bf16[4,16,2176]{2,1,0:T(8,128)(2,1)S(1)}, bf16[4,16,2176]{2,1,0:T(8,128)(2,1)S(1)}, u32[]{:S(2)}, u32[]{:S(2)}) collective-permute-start(bf16[4,16,2176]{2,1,0:T(8,128)(2,1)S(1)} %get-tuple-element.58), channel_id=1, source_target_pairs={{0,16},{4,20},{8,24},{12,28},{16,0},{20,4},{24,8},{28,12},{32,48},... | collective-permute-start | bytes 835592 | tf_op jit(solution)/shard_map/ppermute | solution.py:36
  33.1 13.1 %collective-permute-start.6 = (bf16[4,16,2176]{2,1,0:T(8,128)(2,1)S(1)}, bf16[4,16,2176]{2,1,0:T(8,128)(2,1)S(1)}, u32[]{:S(2)}, u32[]{:S(2)}) collective-permute-start(bf16[4,16,2176]{2,1,0:T(8,128)(2,1)S(1)} %get-tuple-element.57), channel_id=1, source_target_pairs={{0,8},{4,12},{8,16},{12,20},{16,24},{20,28},{24,0},{28,4},{32,40},... | collective-permute-start | bytes 835592 | tf_op jit(solution)/shard_map/ppermute | solution.py:36
  35.9 10.3 %collective-permute-start.7 = (bf16[4,16,2176]{2,1,0:T(8,128)(2,1)S(1)}, bf16[4,16,2176]{2,1,0:T(8,128)(2,1)S(1)}, u32[]{:S(2)}, u32[]{:S(2)}) collective-permute-start(bf16[4,16,2176]{2,1,0:T(8,128)(2,1)S(1)} %get-tuple-element.56), channel_id=1, source_target_pairs={{0,24},{4,28},{8,0},{12,4},{16,8},{20,12},{24,16},{28,20},{32,56},... | collective-permute-start | bytes 835592 | tf_op jit(solution)/shard_map/ppermute | solution.py:36
  46.3 5.0 %collective-permute-start.8 = (bf16[16,2176]{1,0:T(8,128)(2,1)S(1)}, bf16[16,2176]{1,0:T(8,128)(2,1)S(1)}, u32[]{:S(2)}, u32[]{:S(2)}) collective-permute-start(bf16[16,2176]{1,0:T(8,128)(2,1)S(1)} %get-tuple-element.68), channel_id=1, source_target_pairs={{0,16},{4,20},{8,24},{12,28},{16,0},{20,4},{24,8},{28,12},{32,48},... | collective-permute-start | bytes 208904 | tf_op jit(solution)/shard_map/ppermute | solution.py:36
  47.8 6.3 %collective-permute-start.9 = (bf16[16,2176]{1,0:T(8,128)(2,1)S(1)}, bf16[16,2176]{1,0:T(8,128)(2,1)S(1)}, u32[]{:S(2)}, u32[]{:S(2)}) collective-permute-start(bf16[16,2176]{1,0:T(8,128)(2,1)S(1)} %get-tuple-element.67), channel_id=1, source_target_pairs={{0,8},{4,12},{8,16},{12,20},{16,24},{20,28},{24,0},{28,4},{32,40},... | collective-permute-start | bytes 208904 | tf_op jit(solution)/shard_map/ppermute | solution.py:36
  48.9 5.2 %collective-permute-start.10 = (bf16[16,2176]{1,0:T(8,128)(2,1)S(1)}, bf16[16,2176]{1,0:T(8,128)(2,1)S(1)}, u32[]{:S(2)}, u32[]{:S(2)}) collective-permute-start(bf16[16,2176]{1,0:T(8,128)(2,1)S(1)} %get-tuple-element.66), channel_id=1, source_target_pairs={{0,24},{4,28},{8,0},{12,4},{16,8},{20,12},{24,16},{28,20},{32,56},... | collective-permute-start | bytes 208904 | tf_op jit(solution)/shard_map/ppermute | solution.py:36
  50.6 4.8 %collective-permute-start.11 = (bf16[16,2176]{1,0:T(8,128)(2,1)S(1)}, bf16[16,2176]{1,0:T(8,128)(2,1)S(1)}, u32[]{:S(2)}, u32[]{:S(2)}) collective-permute-start(bf16[16,2176]{1,0:T(8,128)(2,1)S(1)} %get-tuple-element.65), channel_id=1, source_target_pairs={{0,64},{4,68},{8,72},{12,76},{16,80},{20,84},{24,88},{28,92},{32,9... | collective-permute-start | bytes 208904 | tf_op jit(solution)/shard_map/ppermute | solution.py:36
  51.3 4.7 %collective-permute-start.12 = (bf16[16,2176]{1,0:T(8,128)(2,1)S(1)}, bf16[16,2176]{1,0:T(8,128)(2,1)S(1)}, u32[]{:S(2)}, u32[]{:S(2)}) collective-permute-start(bf16[16,2176]{1,0:T(8,128)(2,1)S(1)} %get-tuple-element.64), channel_id=1, source_target_pairs={{0,32},{4,36},{8,40},{12,44},{16,48},{20,52},{24,56},{28,60},{32,6... | collective-permute-start | bytes 208904 | tf_op jit(solution)/shard_map/ppermute | solution.py:36
  51.3 4.7 %collective-permute-start.13 = (bf16[16,2176]{1,0:T(8,128)(2,1)S(1)}, bf16[16,2176]{1,0:T(8,128)(2,1)S(1)}, u32[]{:S(2)}, u32[]{:S(2)}) collective-permute-start(bf16[16,2176]{1,0:T(8,128)(2,1)S(1)} %get-tuple-element.63), channel_id=1, source_target_pairs={{0,96},{4,100},{8,104},{12,108},{16,112},{20,116},{24,120},{28,124... | collective-permute-start | bytes 208904 | tf_op jit(solution)/shard_map/ppermute | solution.py:36
  56.2 23.9 %collective-permute-start.14 = (f32[2,16,2176]{2,1,0:T(8,128)S(1)}, f32[2,16,2176]{2,1,0:T(8,128)S(1)}, u32[]{:S(2)}, u32[]{:S(2)}) collective-permute-start(f32[2,16,2176]{2,1,0:T(8,128)S(1)} %pad_maximum_fusion.1), channel_id=1, source_target_pairs={{0,128},{4,132},{8,136},{12,140},{16,144},{20,148},{24,152},{28,15... | collective-permute-start | bytes 835592 | tf_op jit(solution)/shard_map/ppermute | solution.py:36
  63.1 18.8 %collective-permute-start = (f32[3,16,2048]{2,1,0:T(8,128)S(1)}, f32[3,16,2048]{2,1,0:T(8,128)S(1)}, u32[]{:S(2)}, u32[]{:S(2)}) collective-permute-start(f32[3,16,2048]{2,1,0:T(8,128)S(1)} %get-tuple-element.70), channel_id=1, source_target_pairs={{0,128},{4,132},{8,136},{12,140},{16,144},{20,148},{24,152},{28,15... | collective-permute-start | bytes 1179656 | tf_op jit(solution)/shard_map/ppermute | solution.py:36
  63.2 44.2 %collective-permute-start.35 = (s16[3,528,256]{2,1,0:T(8,128)(2,1)}, s16[3,528,256]{2,1,0:T(8,128)(2,1)S(1)}, u32[]{:S(2)}, u32[]{:S(2)}) collective-permute-start(s16[3,528,256]{2,1,0:T(8,128)(2,1)} %get-tuple-element.49), channel_id=1, source_target_pairs={{0,1},{1,2},{2,3},{3,0},{4,5},{5,6},{6,7},{7,4},{8,9},{9,10},{10,1... | collective-permute-start | bytes 2433032 | tf_op jit(solution)/shard_map/ppermute | solution.py:320
  70.0 56.5 %collective-permute-start.36 = (s16[3,528,256]{2,1,0:T(8,128)(2,1)}, s16[3,528,256]{2,1,0:T(8,128)(2,1)S(1)}, u32[]{:S(2)}, u32[]{:S(2)}) collective-permute-start(s16[3,528,256]{2,1,0:T(8,128)(2,1)} %shard_map.122), channel_id=1, source_target_pairs={{0,3},{1,0},{2,1},{3,2},{4,7},{5,4},{6,5},{7,6},{8,11},{9,8},{10,9... | collective-permute-start | bytes 2433032 | tf_op jit(solution)/shard_map/ppermute | solution.py:320
  80.1 82.9 %collective-permute-start.37 = (s16[3,528,256]{2,1,0:T(8,128)(2,1)}, s16[3,528,256]{2,1,0:T(8,128)(2,1)S(1)}, u32[]{:S(2)}, u32[]{:S(2)}) collective-permute-start(s16[3,528,256]{2,1,0:T(8,128)(2,1)} %get-tuple-element.50), channel_id=1, source_target_pairs={{0,2},{1,3},{2,0},{3,1},{4,6},{5,7},{6,4},{7,5},{8,10},{9,11},{10,... | collective-permute-start | bytes 2433032 | tf_op jit(solution)/shard_map/ppermute | solution.py:320
  82.2 80.8 %collective-permute-start.15 = (bf16[1,16,2048]{2,1,0:T(8,128)(2,1)S(1)}, bf16[1,16,2048]{2,1,0:T(8,128)(2,1)S(1)}, u32[]{:S(2)}, u32[]{:S(2)}) collective-permute-start(bf16[1,16,2048]{2,1,0:T(8,128)(2,1)S(1)} %get-tuple-element.72), channel_id=1, source_target_pairs={{0,64},{4,68},{8,72},{12,76},{16,80},{20,84},{24,88},{28,92},{32,9... | collective-permute-start | bytes 196616 | tf_op jit(solution)/shard_map/ppermute | solution.py:36
  83.3 83.9 %collective-permute-start.16 = (bf16[1,16,2048]{2,1,0:T(8,128)(2,1)S(1)}, bf16[1,16,2048]{2,1,0:T(8,128)(2,1)S(1)}, u32[]{:S(2)}, u32[]{:S(2)}) collective-permute-start(bf16[1,16,2048]{2,1,0:T(8,128)(2,1)S(1)} %get-tuple-element.72), channel_id=1, source_target_pairs={{0,32},{4,36},{8,40},{12,44},{16,48},{20,52},{24,56},{28,60},{32,6... | collective-permute-start | bytes 196616 | tf_op jit(solution)/shard_map/ppermute | solution.py:36
  107.4 59.9 %collective-permute-start.17 = (bf16[1,16,2048]{2,1,0:T(8,128)(2,1)S(1)}, bf16[1,16,2048]{2,1,0:T(8,128)(2,1)S(1)}, u32[]{:S(2)}, u32[]{:S(2)}) collective-permute-start(bf16[1,16,2048]{2,1,0:T(8,128)(2,1)S(1)} %get-tuple-element.72), channel_id=1, source_target_pairs={{0,96},{4,100},{8,104},{12,108},{16,112},{20,116},{24,120},{28,124... | collective-permute-start | bytes 196616 | tf_op jit(solution)/shard_map/ppermute | solution.py:36
  126.6 40.7 %collective-permute-start.18 = (bf16[1,16,2048]{2,1,0:T(8,128)(2,1)S(1)}, bf16[1,16,2048]{2,1,0:T(8,128)(2,1)S(1)}, u32[]{:S(2)}, u32[]{:S(2)}) collective-permute-start(bf16[1,16,2048]{2,1,0:T(8,128)(2,1)S(1)} %get-tuple-element.71), channel_id=1, source_target_pairs={{0,16},{4,20},{8,24},{12,28},{16,0},{20,4},{24,8},{28,12},{32,48},... | collective-permute-start | bytes 196616 | tf_op jit(solution)/shard_map/ppermute | solution.py:36
  167.4 8.8 %collective-permute-start.21 = (bf16[4,16,2048]{2,1,0:T(8,128)(2,1)S(1)}, bf16[4,16,2048]{2,1,0:T(8,128)(2,1)S(1)}, u32[]{:S(2)}, u32[]{:S(2)}) collective-permute-start(bf16[4,16,2048]{2,1,0:T(8,128)(2,1)S(1)} %pad_maximum_fusion.3.refs_0_), channel_id=1, source_target_pairs={{0,8},{4,12},{8,16},{12,20},{16,24},{20,28},{24,0},{28,4},{32,40},... | collective-permute-start | bytes 786440 | tf_op jit(solution)/shard_map/ppermute | solution.py:36
  167.7 13.9 %collective-permute-start.22 = (bf16[4,16,2048]{2,1,0:T(8,128)(2,1)S(1)}, bf16[4,16,2048]{2,1,0:T(8,128)(2,1)S(1)}, u32[]{:S(2)}, u32[]{:S(2)}) collective-permute-start(bf16[4,16,2048]{2,1,0:T(8,128)(2,1)S(1)} %pad_maximum_fusion.3.refs_0_), channel_id=1, source_target_pairs={{0,16},{4,20},{8,24},{12,28},{16,0},{20,4},{24,8},{28,12},{32,48},... | collective-permute-start | bytes 786440 | tf_op jit(solution)/shard_map/ppermute | solution.py:36
  171.5 12.9 %collective-permute-start.23 = (bf16[4,16,2048]{2,1,0:T(8,128)(2,1)S(1)}, bf16[4,16,2048]{2,1,0:T(8,128)(2,1)S(1)}, u32[]{:S(2)}, u32[]{:S(2)}) collective-permute-start(bf16[4,16,2048]{2,1,0:T(8,128)(2,1)S(1)} %pad_maximum_fusion.3.refs_0_), channel_id=1, source_target_pairs={{0,24},{4,28},{8,0},{12,4},{16,8},{20,12},{24,16},{28,20},{32,56},... | collective-permute-start | bytes 786440 | tf_op jit(solution)/shard_map/ppermute | solution.py:36
  171.5 12.8 %collective-permute-start.24 = (bf16[4,16,2048]{2,1,0:T(8,128)(2,1)S(1)}, bf16[4,16,2048]{2,1,0:T(8,128)(2,1)S(1)}, u32[]{:S(2)}, u32[]{:S(2)}) collective-permute-start(bf16[4,16,2048]{2,1,0:T(8,128)(2,1)S(1)} %pad_maximum_fusion.4.refs_4_), channel_id=1, source_target_pairs={{0,32},{4,36},{8,40},{12,44},{16,48},{20,52},{24,56},{28,60},{32,6... | collective-permute-start | bytes 786440 | tf_op jit(solution)/shard_map/ppermute | solution.py:36
  173.9 11.6 %collective-permute-start.25 = (bf16[4,16,2048]{2,1,0:T(8,128)(2,1)S(1)}, bf16[4,16,2048]{2,1,0:T(8,128)(2,1)S(1)}, u32[]{:S(2)}, u32[]{:S(2)}) collective-permute-start(bf16[4,16,2048]{2,1,0:T(8,128)(2,1)S(1)} %pad_maximum_fusion.4.refs_4_), channel_id=1, source_target_pairs={{0,64},{4,68},{8,72},{12,76},{16,80},{20,84},{24,88},{28,92},{32,9... | collective-permute-start | bytes 786440 | tf_op jit(solution)/shard_map/ppermute | solution.py:36
  176.2 12.2 %collective-permute-start.26 = (bf16[4,16,2048]{2,1,0:T(8,128)(2,1)S(1)}, bf16[4,16,2048]{2,1,0:T(8,128)(2,1)S(1)}, u32[]{:S(2)}, u32[]{:S(2)}) collective-permute-start(bf16[4,16,2048]{2,1,0:T(8,128)(2,1)S(1)} %pad_maximum_fusion.4.refs_4_), channel_id=1, source_target_pairs={{0,96},{4,100},{8,104},{12,108},{16,112},{20,116},{24,120},{28,124... | collective-permute-start | bytes 786440 | tf_op jit(solution)/shard_map/ppermute | solution.py:36
  181.6 6.9 %collective-permute-start.27 = (bf16[4,16,2048]{2,1,0:T(8,128)(2,1)S(1)}, bf16[4,16,2048]{2,1,0:T(8,128)(2,1)S(1)}, u32[]{:S(2)}, u32[]{:S(2)}) collective-permute-start(bf16[4,16,2048]{2,1,0:T(8,128)(2,1)S(1)} %pad_maximum_fusion.3.refs_0_), channel_id=1, source_target_pairs={{0,4},{4,0},{8,12},{12,8},{16,20},{20,16},{24,28},{28,24},{32,36},... | collective-permute-start | bytes 786440 | tf_op jit(solution)/shard_map/ppermute | solution.py:36
  184.4 4.5 %collective-permute-start.31 = (bf16[4,16,2048]{2,1,0:T(8,128)(2,1)S(1)}, bf16[4,16,2048]{2,1,0:T(8,128)(2,1)S(1)}, u32[]{:S(2)}, u32[]{:S(2)}) collective-permute-start(bf16[4,16,2048]{2,1,0:T(8,128)(2,1)S(1)} %pad_maximum_fusion.4.refs_4_), channel_id=1, source_target_pairs={{0,4},{4,0},{8,12},{12,8},{16,20},{20,16},{24,28},{28,24},{32,36},... | collective-permute-start | bytes 786440 | tf_op jit(solution)/shard_map/ppermute | solution.py:36
  184.4 4.6 %collective-permute-start.28 = (bf16[4,16,2048]{2,1,0:T(8,128)(2,1)S(1)}, bf16[4,16,2048]{2,1,0:T(8,128)(2,1)S(1)}, u32[]{:S(2)}, u32[]{:S(2)}) collective-permute-start(bf16[4,16,2048]{2,1,0:T(8,128)(2,1)S(1)} %collective-permute-done.21.refs_1_), channel_id=1, source_target_pairs={{0,4},{4,0},{8,12},{12,8},{16,20},{20,16},{24,28},{28,24},{32,36},... | collective-permute-start | bytes 786440 | tf_op jit(solution)/shard_map/ppermute | solution.py:36
  185.6 4.5 %collective-permute-start.29 = (bf16[4,16,2048]{2,1,0:T(8,128)(2,1)S(1)}, bf16[4,16,2048]{2,1,0:T(8,128)(2,1)S(1)}, u32[]{:S(2)}, u32[]{:S(2)}) collective-permute-start(bf16[4,16,2048]{2,1,0:T(8,128)(2,1)S(1)} %collective-permute-done.22.refs_2_), channel_id=1, source_target_pairs={{0,4},{4,0},{8,12},{12,8},{16,20},{20,16},{24,28},{28,24},{32,36},... | collective-permute-start | bytes 786440 | tf_op jit(solution)/shard_map/ppermute | solution.py:36
  (11 other events, 230.1 us)

commit v3 on v2

--- a/solution.py
+++ b/solution.py
@@ -324,9 +324,8 @@
     )
     arrived = to_core(send)
     shares = [pass_share(up, 1)]
-    states = jnp.stack([master, moment1, moment2.astype(f32)])
-    other_states = to_zh(states)
-
+    (down,) = input_shares(out_grads, down_weight, token_counts, my_mp, ways, (3,))
+    shares.append(pass_share(down, 3))
     pair = [
         (keep[4 * i : 4 * i + 4].astype(f32) + arrived[4 * i : 4 * i + 4].astype(f32)).astype(bf16)
         for i in range(8)
@@ -336,8 +335,6 @@
         for colour, (first, _) in enumerate(rings)
     ]
     got = lax.optimization_barrier(got)
-    (down,) = input_shares(out_grads, down_weight, token_counts, my_mp, ways, (3,))
-    shares.append(pass_share(down, 3))
     lines = [
         [
             sum((g[e].astype(f32) for g in got[colour]), pair[4 * colour][e].astype(f32)).astype(bf16)
@@ -353,33 +350,29 @@
     sums = [
         sum((g.astype(f32) for g in group), line[0].astype(f32)) for group, line in zip(got, lines)
     ]
-    sums = lax.optimization_barrier(jnp.stack(sums))
-    theirs = to_zh(sums)
+    theirs = to_zh(sums[1])
     across, own = input_shares(out_grads, down_weight, token_counts, my_mp, ways, (2, 0))
-    shares.append(pass_share(across, 2))
-
-    summed = sums + theirs[::-1]
-    digits = summed[:, :1, columns : columns + DIGITS]
-    total = jnp.sum(digits * (4.0 ** jnp.arange(DIGITS, dtype=f32)), axis=(1, 2), keepdims=True)
-    grad = summed[:, :, :columns] / total
-    old_master, old_first, old_second = jnp.stack([states, other_states], axis=1)
-    moment1_new = beta_one * old_first + (1.0 - beta_one) * grad
-    second = beta_two * old_second + (1.0 - beta_two) * grad * grad
-    master_new = old_master - learn_rate * (moment1_new / correct_one) / (
+    summed = sums[0] + theirs
+
+    digits = summed[:1, columns : columns + DIGITS]
+    total = jnp.sum(digits * (4.0 ** jnp.arange(DIGITS, dtype=f32)))
+    grad = summed[:, :columns] / total
+    moment1_new = beta_one * moment1 + (1.0 - beta_one) * grad
+    second = beta_two * moment2.astype(f32) + (1.0 - beta_two) * grad * grad
+    moment2_new = second.astype(bf16)
+    master_new = master - learn_rate * (moment1_new / correct_one) / (
         jnp.sqrt(second / correct_two) + epsilon
     )
-    weights = master_new.astype(bf16)
-    master_new, moment1_new, moment2_new = master_new[0], moment1_new[0], second[0].astype(bf16)
-
-    got = [
-        [shift(weights[colour : colour + 1], first, d) for d in (2, 1, 3)]
-        for colour, (first, _) in enumerate(rings)
-    ]
-    got = lax.optimization_barrier(got)
+
+    weights = master_new.astype(bf16)[None]
+    other = to_zh(weights)
+    shares.append(pass_share(across, 2))
+    lines = []
+    for part, (first, _) in zip((weights, other), rings):
+        two, one, three = [shift(part, first, d) for d in (2, 1, 3)]
+        lines.append(jnp.concatenate([part, one, two, three]))
     pieces = []
-    for colour, (_, second) in enumerate(rings):
-        two, one, three = got[colour]
-        line = jnp.concatenate([weights[colour : colour + 1], one, two, three])
+    for line, (_, second) in zip(lines, rings):
         two, one, three = [shift(line, second, d) for d in (2, 1, 3)]
         pieces += [line, one, two, three]
     pieces += [to_core(piece) for piece in pieces]

time: 194 us -> 187 us (0.964)
  waiting for transfers between devices: 99.5 us -> 67.7 us
  starting transfers between devices: 54.4 us -> 77.9 us
    ppermute x3, waiting for transfers between devices: 75.2 us -> 33.8 us  [pass_share(): return lax.ppermute(coded, 'mp', ring)]
    ppermute x35, starting transfers between devices: 51.1 us -> 74.5 us  [move(): return lax.ppermute(value, 'dp', pairs)]
    ppermute x35, waiting for transfers between devices: 24.3 us -> 33.9 us  [move(): return lax.ppermute(value, 'dp', pairs)]
  transfers between devices with their start and end apart: 38 -> 38, of which waited for: 14 -> 11; matrix products, arithmetic and copies ran while one was open for 1% -> 0% of each run, Pallas kernels for 8% -> 8%
where the time goes in v3:
time: 187 us; the launch traced here: 186 us
  starting transfers between devices  77.9 us (42%)
  waiting for transfers between devices  67.7 us (36%)
  Pallas kernels  33.2 us (18%)
  other arithmetic  4.6 us (2%)
    ppermute x35, starting transfers between devices, move(): return lax.ppermute(value, 'dp', pairs)  74.5 us
    ppermute x35, waiting for transfers between devices, move(): return lax.ppermute(value, 'dp', pairs)  33.9 us
    ppermute x3, waiting for transfers between devices, pass_share(): return lax.ppermute(coded, 'mp', ring)  33.8 us
    pallas_call x1, Pallas kernels, weight_partials(): pl.pallas_call(kernel, grid_spec=pltpu.PrefetchScalarGridSpec(num_scalar_...  15.4 us
    pallas_call x2, Pallas kernels, input_shares(): pl.pallas_call(kernel, grid_spec=pltpu.PrefetchScalarGridSpec(num_scalar_...  13.6 us
  transfers between devices with their start and end apart: 38, of which 11 were waited for; matrix products, arithmetic and copies ran while one was open for 0% of the time, Pallas kernels for 8%

profile of v3, /device:TPU:1, one launch (start us, length us, event | category | flops | bytes accessed | tf_op | source)
XLA Modules:
  0.0 186.4 jit_solution(9662918586397692659)
XLA Ops:
  1.3 15.4 %shard_map.119 = (bf16[32,16,2176]{2,1,0:T(8,128)(2,1)}, bf16[32,16,2176]{2,1,0:T(8,128)(2,1)}, s16[3,528,256]{2,1,0:T(8,128)(2,1)}) custom-call(s32[1]{0:T(128)S(6)} %copy.16.count_ref, s32[64]{0:T(128)} %map_ref.3, s32[1]{0:T(128)} %bitcast.me_ref, s32[1]{0:T(128)} %bitcast.1.mine_ref, bf16[1536,1024]{1,0:T(8,128)(2,1)} %acts_ref.1, ...), custom_call_target="tpu_custom_call" | custom-call | tf_op jit(solution)/shard_map/pallas_call | solution.py:162
  16.7 3.3 %collective-permute-start = (bf16[32,16,2176]{2,1,0:T(8,128)(2,1)}, bf16[32,16,2176]{2,1,0:T(8,128)(2,1)S(1)}, u32[]{:S(2)}, u32[]{:S(2)}) collective-permute-start(bf16[32,16,2176]{2,1,0:T(8,128)(2,1)} %get-tuple-element.23), channel_id=1, source_target_pairs={{0,4},{4,0},{8,12},{12,8},{16,20},{20,16},{24,28},{28,24},{32,36},... | collective-permute-start | bytes 6684680 | tf_op jit(solution)/shard_map/ppermute | solution.py:36
  20.0 4.2 %collective-permute-done = bf16[32,16,2176]{2,1,0:T(8,128)(2,1)S(1)} collective-permute-done((bf16[32,16,2176]{2,1,0:T(8,128)(2,1)}, bf16[32,16,2176]{2,1,0:T(8,128)(2,1)S(1)}, u32[]{:S(2)}, u32[]{:S(2)}) %collective-permute-start) | collective-permute-done | bytes 2228256 | tf_op jit(solution)/shard_map/ppermute | solution.py:36
  24.2 2.1 %add_convert_fusion = (bf16[4,16,2176]{2,1,0:T(8,128)(2,1)S(1)}, bf16[4,16,2176]{2,1,0:T(8,128)(2,1)S(1)}, bf16[4,16,2176]{2,1,0:T(8,128)(2,1)S(1)}, bf16[4,16,2...) fusion(bf16[32,16,2176]{2,1,0:T(8,128)(2,1)S(1)} %collective-pe, ...), kind=kLoop, calls=%fused_computation | loop fusion | flops 4456448 | bytes 6684672 | tf_op jit(solution)/shard_map/convert_element_type | solution.py:330
  29.1 2.5 %collective-permute-start.3 = (bf16[4,16,2176]{2,1,0:T(8,128)(2,1)S(1)}, bf16[4,16,2176]{2,1,0:T(8,128)(2,1)S(1)}, u32[]{:S(2)}, u32[]{:S(2)}) collective-permute-start(bf16[4,16,2176]{2,1,0:T(8,128)(2,1)S(1)} %get-tuple-element.46), channel_id=1, source_target_pairs={{0,96},{4,100},{8,104},{12,108},{16,112},{20,116},{24,120},{28,124... | collective-permute-start | bytes 835592 | tf_op jit(solution)/shard_map/ppermute | solution.py:36
  31.6 2.7 %collective-permute-done.6 = bf16[4,16,2176]{2,1,0:T(8,128)(2,1)S(1)} collective-permute-done((bf16[4,16,2176]{2,1,0:T(8,128)(2,1)S(1)}, bf16[4,16,2176]{2,1,0:T(8,128)(2,1)S(1)}, u32[]{:S(2)}, u32[]{:S(2)}) %collective-permute-start.6) | collective-permute-done | bytes 278560 | tf_op jit(solution)/shard_map/ppermute | solution.py:36
  34.3 7.4 %collective-permute-start.1 = (bf16[4,16,2176]{2,1,0:T(8,128)(2,1)S(1)}, bf16[4,16,2176]{2,1,0:T(8,128)(2,1)S(1)}, u32[]{:S(2)}, u32[]{:S(2)}) collective-permute-start(bf16[4,16,2176]{2,1,0:T(8,128)(2,1)S(1)} %get-tuple-element.48), channel_id=1, source_target_pairs={{0,64},{4,68},{8,72},{12,76},{16,80},{20,84},{24,88},{28,92},{32,9... | collective-permute-start | bytes 835592 | tf_op jit(solution)/shard_map/ppermute | solution.py:36
  41.7 5.6 %collective-permute-done.1 = bf16[4,16,2176]{2,1,0:T(8,128)(2,1)S(1)} collective-permute-done((bf16[4,16,2176]{2,1,0:T(8,128)(2,1)S(1)}, bf16[4,16,2176]{2,1,0:T(8,128)(2,1)S(1)}, u32[]{:S(2)}, u32[]{:S(2)}) %collective-permute-start.1) | collective-permute-done | bytes 278560 | tf_op jit(solution)/shard_map/ppermute | solution.py:36
  47.5 3.8 %collective-permute-start.9 = (bf16[16,2176]{1,0:T(8,128)(2,1)S(1)}, bf16[16,2176]{1,0:T(8,128)(2,1)S(1)}, u32[]{:S(2)}, u32[]{:S(2)}) collective-permute-start(bf16[16,2176]{1,0:T(8,128)(2,1)S(1)} %get-tuple-element.53), channel_id=1, source_target_pairs={{0,24},{4,28},{8,0},{12,4},{16,8},{20,12},{24,16},{28,20},{32,56},... | collective-permute-start | bytes 208904 | tf_op jit(solution)/shard_map/ppermute | solution.py:36
  52.6 2.5 %collective-permute-start.12 = (bf16[16,2176]{1,0:T(8,128)(2,1)S(1)}, bf16[16,2176]{1,0:T(8,128)(2,1)S(1)}, u32[]{:S(2)}, u32[]{:S(2)}) collective-permute-start(bf16[16,2176]{1,0:T(8,128)(2,1)S(1)} %get-tuple-element.50), channel_id=1, source_target_pairs={{0,96},{4,100},{8,104},{12,108},{16,112},{20,116},{24,120},{28,124... | collective-permute-start | bytes 208904 | tf_op jit(solution)/shard_map/ppermute | solution.py:36
  55.1 1.7 collective-permute-start.10
  56.9 3.4 %collective-permute-done.11 = bf16[16,2176]{1,0:T(8,128)(2,1)S(1)} collective-permute-done((bf16[16,2176]{1,0:T(8,128)(2,1)S(1)}, bf16[16,2176]{1,0:T(8,128)(2,1)S(1)}, u32[]{:S(2)}, u32[]{:S(2)}) %collective-permute-start.11) | collective-permute-done | bytes 69664 | tf_op jit(solution)/shard_map/ppermute | solution.py:36
  60.3 7.0 %collective-permute-start.13 = (f32[16,2176]{1,0:T(8,128)S(1)}, f32[16,2176]{1,0:T(8,128)S(1)}, u32[]{:S(2)}, u32[]{:S(2)}) collective-permute-start(f32[16,2176]{1,0:T(8,128)S(1)} %fusion.1), channel_id=1, source_target_pairs={{0,128},{4,132},{8,136},{12,140},{16,144},{20,148},{24,152},{28,15... | collective-permute-start | bytes 417800 | tf_op jit(solution)/shard_map/ppermute | solution.py:36
  67.3 2.5 %collective-permute-done.13 = f32[16,2176]{1,0:T(8,128)S(1)} collective-permute-done((f32[16,2176]{1,0:T(8,128)S(1)}, f32[16,2176]{1,0:T(8,128)S(1)}, u32[]{:S(2)}, u32[]{:S(2)}) %collective-permute-start.13) | collective-permute-done | bytes 139296 | tf_op jit(solution)/shard_map/ppermute | solution.py:36
  72.0 6.1 %collective-permute-start.20 = (bf16[1,16,2048]{2,1,0:T(8,128)(2,1)S(1)}, bf16[1,16,2048]{2,1,0:T(8,128)(2,1)S(1)}, u32[]{:S(2)}, u32[]{:S(2)}) collective-permute-start(bf16[1,16,2048]{2,1,0:T(8,128)(2,1)S(1)} %get-tuple-element.39), channel_id=1, source_target_pairs={{0,128},{4,132},{8,136},{12,140},{16,144},{20,148},{24,152},{28,15... | collective-permute-start | bytes 196616 | tf_op jit(solution)/shard_map/ppermute | solution.py:36
  78.1 6.0 %shard_map.122 = s16[3,528,256]{2,1,0:T(8,128)(2,1)} custom-call(s32[1]{0:T(128)S(6)} %copy.16.count_ref, s32[1]{0:T(128)} %bitcast.1.mine_ref, bf16[1536,2048]{1,0:T(8,128)(2,1)} %grads_ref.5, bf16[1024,2048]{1,0:T(8,128)(2,1)} %refs_0_.3), custom_call_target="tpu_custom_call" | custom-call | tf_op jit(solution)/shard_map/pallas_call | solution.py:222
  85.4 7.5 %shard_map.121 = (s16[3,528,256]{2,1,0:T(8,128)(2,1)}, f32[1536,256]{1,0:T(8,128)}) custom-call(s32[1]{0:T(128)S(6)} %copy.16.count_ref, s32[1]{0:T(128)} %bitcast.1.mine_ref, bf16[1536,2048]{1,0:T(8,128)(2,1)} %grads_ref.5, bf16[1024,2048]{1,0:T(8,128)(2,1)} %refs_0_.3, bf16[1024,2048]{1,0:T(8,128)(2,1)} %refs_0_.3), custom_call_target="tpu_custom_call" | custom-call | tf_op jit(solution)/shard_map/pallas_call | solution.py:222
  94.4 2.3 %collective-permute-start.16 = (bf16[1,16,2048]{2,1,0:T(8,128)(2,1)S(1)}, bf16[1,16,2048]{2,1,0:T(8,128)(2,1)S(1)}, u32[]{:S(2)}, u32[]{:S(2)}) collective-permute-start(bf16[1,16,2048]{2,1,0:T(8,128)(2,1)S(1)} %get-tuple-element.39), channel_id=1, source_target_pairs={{0,96},{4,100},{8,104},{12,108},{16,112},{20,116},{24,120},{28,124... | collective-permute-start | bytes 196616 | tf_op jit(solution)/shard_map/ppermute | solution.py:36
  99.2 2.2 %collective-permute-done.15 = bf16[1,16,2048]{2,1,0:T(8,128)(2,1)S(1)} collective-permute-done((bf16[1,16,2048]{2,1,0:T(8,128)(2,1)S(1)}, bf16[1,16,2048]{2,1,0:T(8,128)(2,1)S(1)}, u32[]{:S(2)}, u32[]{:S(2)}) %collective-permute-start.15) | collective-permute-done | bytes 65568 | tf_op jit(solution)/shard_map/ppermute | solution.py:36
  101.4 1.6 collective-permute-start.23
  103.7 3.9 %collective-permute-done.21 = bf16[1,16,2048]{2,1,0:T(8,128)(2,1)S(1)} collective-permute-done((bf16[1,16,2048]{2,1,0:T(8,128)(2,1)S(1)}, bf16[1,16,2048]{2,1,0:T(8,128)(2,1)S(1)}, u32[]{:S(2)}, u32[]{:S(2)}) %collective-permute-start.21) | collective-permute-done | bytes 65568 | tf_op jit(solution)/shard_map/ppermute | solution.py:36
  108.6 9.5 %collective-permute-start.27 = (bf16[4,16,2048]{2,1,0:T(8,128)(2,1)S(1)}, bf16[4,16,2048]{2,1,0:T(8,128)(2,1)S(1)}, u32[]{:S(2)}, u32[]{:S(2)}) collective-permute-start(bf16[4,16,2048]{2,1,0:T(8,128)(2,1)S(1)} %pad_maximum_fusion.refs_0_), channel_id=1, source_target_pairs={{0,4},{4,0},{8,12},{12,8},{16,20},{20,16},{24,28},{28,24},{32,36},... | collective-permute-start | bytes 786440 | tf_op jit(solution)/shard_map/ppermute | solution.py:36
  118.0 33.8 %collective-permute-done.37.refs_2_ = s16[3,528,256]{2,1,0:T(8,128)(2,1)S(1)} collective-permute-done((s16[3,528,256]{2,1,0:T(8,128)(2,1)}, s16[3,528,256]{2,1,0:T(8,128)(2,1)S(1)}, u32[]{:S(2)}, u32[]{:S(2)}) %collective-permute-start.37) | collective-permute-done | bytes 811040 | tf_op jit(solution)/shard_map/ppermute | solution.py:320
  151.9 1.9 %collective-permute-start.19 = (bf16[4,16,2048]{2,1,0:T(8,128)(2,1)S(1)}, bf16[4,16,2048]{2,1,0:T(8,128)(2,1)S(1)}, u32[]{:S(2)}, u32[]{:S(2)}) collective-permute-start(bf16[4,16,2048]{2,1,0:T(8,128)(2,1)S(1)} %pad_maximum_fusion.refs_0_), channel_id=1, source_target_pairs={{0,24},{4,28},{8,0},{12,4},{16,8},{20,12},{24,16},{28,20},{32,56},... | collective-permute-start | bytes 786440 | tf_op jit(solution)/shard_map/ppermute | solution.py:36
  153.8 1.6 collective-permute-start.18
  155.4 7.3 %collective-permute-start.31 = (bf16[4,16,2048]{2,1,0:T(8,128)(2,1)S(1)}, bf16[4,16,2048]{2,1,0:T(8,128)(2,1)S(1)}, u32[]{:S(2)}, u32[]{:S(2)}) collective-permute-start(bf16[4,16,2048]{2,1,0:T(8,128)(2,1)S(1)} %constant_dynamic-update-slice_fusion.refs_4_), channel_id=1, source_target_pairs={{0,4},{4,0},{8,12},{12,8},{16,20},{20,16},{24,28},{28,24},{32,36},... | collective-permute-start | bytes 786440 | tf_op jit(solution)/shard_map/ppermute | solution.py:36
  162.7 2.3 %collective-permute-start.26 = (bf16[4,16,2048]{2,1,0:T(8,128)(2,1)S(1)}, bf16[4,16,2048]{2,1,0:T(8,128)(2,1)S(1)}, u32[]{:S(2)}, u32[]{:S(2)}) collective-permute-start(bf16[4,16,2048]{2,1,0:T(8,128)(2,1)S(1)} %constant_dynamic-update-slice_fusion.refs_4_), channel_id=1, source_target_pairs={{0,96},{4,100},{8,104},{12,108},{16,112},{20,116},{24,120},{28,124... | collective-permute-start | bytes 786440 | tf_op jit(solution)/shard_map/ppermute | solution.py:36
  165.6 5.2 %collective-permute-start.30 = (bf16[4,16,2048]{2,1,0:T(8,128)(2,1)S(1)}, bf16[4,16,2048]{2,1,0:T(8,128)(2,1)S(1)}, u32[]{:S(2)}, u32[]{:S(2)}) collective-permute-start(bf16[4,16,2048]{2,1,0:T(8,128)(2,1)S(1)} %collective-permute-done.19.refs_3_), channel_id=1, source_target_pairs={{0,4},{4,0},{8,12},{12,8},{16,20},{20,16},{24,28},{28,24},{32,36},... | collective-permute-start | bytes 786440 | tf_op jit(solution)/shard_map/ppermute | solution.py:36
  170.8 5.2 %collective-permute-done.26.refs_7_ = bf16[4,16,2048]{2,1,0:T(8,128)(2,1)S(1)} collective-permute-done((bf16[4,16,2048]{2,1,0:T(8,128)(2,1)S(1)}, bf16[4,16,2048]{2,1,0:T(8,128)(2,1)S(1)}, u32[]{:S(2)}, u32[]{:S(2)}) %collective-permute-start.26) | collective-permute-done | bytes 262176 | tf_op jit(solution)/shard_map/ppermute | solution.py:36
  177.1 2.8 %collective-permute-done.24.refs_5_ = bf16[4,16,2048]{2,1,0:T(8,128)(2,1)S(1)} collective-permute-done((bf16[4,16,2048]{2,1,0:T(8,128)(2,1)S(1)}, bf16[4,16,2048]{2,1,0:T(8,128)(2,1)S(1)}, u32[]{:S(2)}, u32[]{:S(2)}) %collective-permute-start.24) | collective-permute-done | bytes 262176 | tf_op jit(solution)/shard_map/ppermute | solution.py:36
  182.0 1.6 shard_map.123
  183.7 2.5 %shard_map.120 = bf16[64,16,2048]{2,1,0:T(8,128)(2,1)} custom-call(s32[64]{0:T(128)S(1)} %copy-done.1, s32[1]{0:T(128)} %bitcast.me_ref, bf16[4,16,2048]{2,1,0:T(8,128)(2,1)S(1)} %pad_maximum_fusion.refs_0_, bf16[4,16,2048]{2,1,0:T(8,128)(2,1)S(1)} %collective-permute-done.17.refs_1_, bf16[4,16,2048]{2,1,0:T(8,128)(2,1)S(1)} %collective-permute-done.18.refs_2_, ...), custom_call_target="tpu_custom_call" | custom-call | tf_op jit(solution)/shard_map/pallas_call | solution.py:296
  (73 shorter events, 17.3 us)
Async XLA Ops:
  16.7 7.5 %collective-permute-start = (bf16[32,16,2176]{2,1,0:T(8,128)(2,1)}, bf16[32,16,2176]{2,1,0:T(8,128)(2,1)S(1)}, u32[]{:S(2)}, u32[]{:S(2)}) collective-permute-start(bf16[32,16,2176]{2,1,0:T(8,128)(2,1)} %get-tuple-element.23), channel_id=1, source_target_pairs={{0,4},{4,0},{8,12},{12,8},{16,20},{20,16},{24,28},{28,24},{32,36},... | collective-permute-start | bytes 6684680 | tf_op jit(solution)/shard_map/ppermute | solution.py:36
  26.4 7.9 %collective-permute-start.6 = (bf16[4,16,2176]{2,1,0:T(8,128)(2,1)S(1)}, bf16[4,16,2176]{2,1,0:T(8,128)(2,1)S(1)}, u32[]{:S(2)}, u32[]{:S(2)}) collective-permute-start(bf16[4,16,2176]{2,1,0:T(8,128)(2,1)S(1)} %get-tuple-element.43), channel_id=1, source_target_pairs={{0,24},{4,28},{8,0},{12,4},{16,8},{20,12},{24,16},{28,20},{32,56},... | collective-permute-start | bytes 835592 | tf_op jit(solution)/shard_map/ppermute | solution.py:36
  27.5 14.2 %collective-permute-start.5 = (bf16[4,16,2176]{2,1,0:T(8,128)(2,1)S(1)}, bf16[4,16,2176]{2,1,0:T(8,128)(2,1)S(1)}, u32[]{:S(2)}, u32[]{:S(2)}) collective-permute-start(bf16[4,16,2176]{2,1,0:T(8,128)(2,1)S(1)} %get-tuple-element.44), channel_id=1, source_target_pairs={{0,8},{4,12},{8,16},{12,20},{16,24},{20,28},{24,0},{28,4},{32,40},... | collective-permute-start | bytes 835592 | tf_op jit(solution)/shard_map/ppermute | solution.py:36
  27.9 13.8 %collective-permute-start.4 = (bf16[4,16,2176]{2,1,0:T(8,128)(2,1)S(1)}, bf16[4,16,2176]{2,1,0:T(8,128)(2,1)S(1)}, u32[]{:S(2)}, u32[]{:S(2)}) collective-permute-start(bf16[4,16,2176]{2,1,0:T(8,128)(2,1)S(1)} %get-tuple-element.45), channel_id=1, source_target_pairs={{0,16},{4,20},{8,24},{12,28},{16,0},{20,4},{24,8},{28,12},{32,48},... | collective-permute-start | bytes 835592 | tf_op jit(solution)/shard_map/ppermute | solution.py:36
  29.1 12.6 %collective-permute-start.3 = (bf16[4,16,2176]{2,1,0:T(8,128)(2,1)S(1)}, bf16[4,16,2176]{2,1,0:T(8,128)(2,1)S(1)}, u32[]{:S(2)}, u32[]{:S(2)}) collective-permute-start(bf16[4,16,2176]{2,1,0:T(8,128)(2,1)S(1)} %get-tuple-element.46), channel_id=1, source_target_pairs={{0,96},{4,100},{8,104},{12,108},{16,112},{20,116},{24,120},{28,124... | collective-permute-start | bytes 835592 | tf_op jit(solution)/shard_map/ppermute | solution.py:36
  31.6 10.1 %collective-permute-start.2 = (bf16[4,16,2176]{2,1,0:T(8,128)(2,1)S(1)}, bf16[4,16,2176]{2,1,0:T(8,128)(2,1)S(1)}, u32[]{:S(2)}, u32[]{:S(2)}) collective-permute-start(bf16[4,16,2176]{2,1,0:T(8,128)(2,1)S(1)} %get-tuple-element.47), channel_id=1, source_target_pairs={{0,32},{4,36},{8,40},{12,44},{16,48},{20,52},{24,56},{28,60},{32,6... | collective-permute-start | bytes 835592 | tf_op jit(solution)/shard_map/ppermute | solution.py:36
  34.3 13.1 %collective-permute-start.1 = (bf16[4,16,2176]{2,1,0:T(8,128)(2,1)S(1)}, bf16[4,16,2176]{2,1,0:T(8,128)(2,1)S(1)}, u32[]{:S(2)}, u32[]{:S(2)}) collective-permute-start(bf16[4,16,2176]{2,1,0:T(8,128)(2,1)S(1)} %get-tuple-element.48), channel_id=1, source_target_pairs={{0,64},{4,68},{8,72},{12,76},{16,80},{20,84},{24,88},{28,92},{32,9... | collective-permute-start | bytes 835592 | tf_op jit(solution)/shard_map/ppermute | solution.py:36
  47.5 7.7 %collective-permute-start.9 = (bf16[16,2176]{1,0:T(8,128)(2,1)S(1)}, bf16[16,2176]{1,0:T(8,128)(2,1)S(1)}, u32[]{:S(2)}, u32[]{:S(2)}) collective-permute-start(bf16[16,2176]{1,0:T(8,128)(2,1)S(1)} %get-tuple-element.53), channel_id=1, source_target_pairs={{0,24},{4,28},{8,0},{12,4},{16,8},{20,12},{24,16},{28,20},{32,56},... | collective-permute-start | bytes 208904 | tf_op jit(solution)/shard_map/ppermute | solution.py:36
  51.2 5.6 %collective-permute-start.8 = (bf16[16,2176]{1,0:T(8,128)(2,1)S(1)}, bf16[16,2176]{1,0:T(8,128)(2,1)S(1)}, u32[]{:S(2)}, u32[]{:S(2)}) collective-permute-start(bf16[16,2176]{1,0:T(8,128)(2,1)S(1)} %get-tuple-element.54), channel_id=1, source_target_pairs={{0,8},{4,12},{8,16},{12,20},{16,24},{20,28},{24,0},{28,4},{32,40},... | collective-permute-start | bytes 208904 | tf_op jit(solution)/shard_map/ppermute | solution.py:36
  51.2 5.6 %collective-permute-start.7 = (bf16[16,2176]{1,0:T(8,128)(2,1)S(1)}, bf16[16,2176]{1,0:T(8,128)(2,1)S(1)}, u32[]{:S(2)}, u32[]{:S(2)}) collective-permute-start(bf16[16,2176]{1,0:T(8,128)(2,1)S(1)} %get-tuple-element.55), channel_id=1, source_target_pairs={{0,16},{4,20},{8,24},{12,28},{16,0},{20,4},{24,8},{28,12},{32,48},... | collective-permute-start | bytes 208904 | tf_op jit(solution)/shard_map/ppermute | solution.py:36
  55.1 5.1 %collective-permute-start.11 = (bf16[16,2176]{1,0:T(8,128)(2,1)S(1)}, bf16[16,2176]{1,0:T(8,128)(2,1)S(1)}, u32[]{:S(2)}, u32[]{:S(2)}) collective-permute-start(bf16[16,2176]{1,0:T(8,128)(2,1)S(1)} %get-tuple-element.51), channel_id=1, source_target_pairs={{0,32},{4,36},{8,40},{12,44},{16,48},{20,52},{24,56},{28,60},{32,6... | collective-permute-start | bytes 208904 | tf_op jit(solution)/shard_map/ppermute | solution.py:36
  55.1 5.1 %collective-permute-start.10 = (bf16[16,2176]{1,0:T(8,128)(2,1)S(1)}, bf16[16,2176]{1,0:T(8,128)(2,1)S(1)}, u32[]{:S(2)}, u32[]{:S(2)}) collective-permute-start(bf16[16,2176]{1,0:T(8,128)(2,1)S(1)} %get-tuple-element.52), channel_id=1, source_target_pairs={{0,64},{4,68},{8,72},{12,76},{16,80},{20,84},{24,88},{28,92},{32,9... | collective-permute-start | bytes 208904 | tf_op jit(solution)/shard_map/ppermute | solution.py:36
  60.3 9.5 %collective-permute-start.13 = (f32[16,2176]{1,0:T(8,128)S(1)}, f32[16,2176]{1,0:T(8,128)S(1)}, u32[]{:S(2)}, u32[]{:S(2)}) collective-permute-start(f32[16,2176]{1,0:T(8,128)S(1)} %fusion.1), channel_id=1, source_target_pairs={{0,128},{4,132},{8,136},{12,140},{16,144},{20,148},{24,152},{28,15... | collective-permute-start | bytes 417800 | tf_op jit(solution)/shard_map/ppermute | solution.py:36
  72.0 24.7 %collective-permute-start.20 = (bf16[1,16,2048]{2,1,0:T(8,128)(2,1)S(1)}, bf16[1,16,2048]{2,1,0:T(8,128)(2,1)S(1)}, u32[]{:S(2)}, u32[]{:S(2)}) collective-permute-start(bf16[1,16,2048]{2,1,0:T(8,128)(2,1)S(1)} %get-tuple-element.39), channel_id=1, source_target_pairs={{0,128},{4,132},{8,136},{12,140},{16,144},{20,148},{24,152},{28,15... | collective-permute-start | bytes 196616 | tf_op jit(solution)/shard_map/ppermute | solution.py:36
  84.1 24.4 %collective-permute-start.36 = (s16[3,528,256]{2,1,0:T(8,128)(2,1)}, s16[3,528,256]{2,1,0:T(8,128)(2,1)S(1)}, u32[]{:S(2)}, u32[]{:S(2)}) collective-permute-start(s16[3,528,256]{2,1,0:T(8,128)(2,1)} %shard_map.122), channel_id=1, source_target_pairs={{0,3},{1,0},{2,1},{3,2},{4,7},{5,4},{6,5},{7,6},{8,11},{9,8},{10,9... | collective-permute-start | bytes 2433032 | tf_op jit(solution)/shard_map/ppermute | solution.py:320
  92.9 59.0 %collective-permute-start.37 = (s16[3,528,256]{2,1,0:T(8,128)(2,1)}, s16[3,528,256]{2,1,0:T(8,128)(2,1)S(1)}, u32[]{:S(2)}, u32[]{:S(2)}) collective-permute-start(s16[3,528,256]{2,1,0:T(8,128)(2,1)} %get-tuple-element.38), channel_id=1, source_target_pairs={{0,2},{1,3},{2,0},{3,1},{4,6},{5,7},{6,4},{7,5},{8,10},{9,11},{10,... | collective-permute-start | bytes 2433032 | tf_op jit(solution)/shard_map/ppermute | solution.py:320
  96.7 6.4 %collective-permute-start.14 = (bf16[1,16,2048]{2,1,0:T(8,128)(2,1)S(1)}, bf16[1,16,2048]{2,1,0:T(8,128)(2,1)S(1)}, u32[]{:S(2)}, u32[]{:S(2)}) collective-permute-start(bf16[1,16,2048]{2,1,0:T(8,128)(2,1)S(1)} %get-tuple-element.39), channel_id=1, source_target_pairs={{0,32},{4,36},{8,40},{12,44},{16,48},{20,52},{24,56},{28,60},{32,6... | collective-permute-start | bytes 196616 | tf_op jit(solution)/shard_map/ppermute | solution.py:36
  98.6 56.8 %collective-permute-start.35 = (s16[3,528,256]{2,1,0:T(8,128)(2,1)S(1)}, s16[3,528,256]{2,1,0:T(8,128)(2,1)S(1)}, u32[]{:S(2)}, u32[]{:S(2)}) collective-permute-start(s16[3,528,256]{2,1,0:T(8,128)(2,1)S(1)} %copy-done.5), channel_id=1, source_target_pairs={{0,1},{1,2},{2,3},{3,0},{4,5},{5,6},{6,7},{7,4},{8,9},{9,10},{10,1... | collective-permute-start | bytes 2433032 | tf_op jit(solution)/shard_map/ppermute | solution.py:320
  101.4 52.4 %collective-permute-start.23 = (bf16[1,16,2048]{2,1,0:T(8,128)(2,1)S(1)}, bf16[1,16,2048]{2,1,0:T(8,128)(2,1)S(1)}, u32[]{:S(2)}, u32[]{:S(2)}) collective-permute-start(bf16[1,16,2048]{2,1,0:T(8,128)(2,1)S(1)} %collective-permute-done.20), channel_id=1, source_target_pairs={{0,24},{4,28},{8,0},{12,4},{16,8},{20,12},{24,16},{28,20},{32,56},... | collective-permute-start | bytes 196616 | tf_op jit(solution)/shard_map/ppermute | solution.py:36
  107.7 47.7 %collective-permute-start.22 = (bf16[1,16,2048]{2,1,0:T(8,128)(2,1)S(1)}, bf16[1,16,2048]{2,1,0:T(8,128)(2,1)S(1)}, u32[]{:S(2)}, u32[]{:S(2)}) collective-permute-start(bf16[1,16,2048]{2,1,0:T(8,128)(2,1)S(1)} %collective-permute-done.20), channel_id=1, source_target_pairs={{0,16},{4,20},{8,24},{12,28},{16,0},{20,4},{24,8},{28,12},{32,48},... | collective-permute-start | bytes 196616 | tf_op jit(solution)/shard_map/ppermute | solution.py:36
  108.6 54.1 %collective-permute-start.27 = (bf16[4,16,2048]{2,1,0:T(8,128)(2,1)S(1)}, bf16[4,16,2048]{2,1,0:T(8,128)(2,1)S(1)}, u32[]{:S(2)}, u32[]{:S(2)}) collective-permute-start(bf16[4,16,2048]{2,1,0:T(8,128)(2,1)S(1)} %pad_maximum_fusion.refs_0_), channel_id=1, source_target_pairs={{0,4},{4,0},{8,12},{12,8},{16,20},{20,16},{24,28},{28,24},{32,36},... | collective-permute-start | bytes 786440 | tf_op jit(solution)/shard_map/ppermute | solution.py:36
  151.9 13.1 %collective-permute-start.19 = (bf16[4,16,2048]{2,1,0:T(8,128)(2,1)S(1)}, bf16[4,16,2048]{2,1,0:T(8,128)(2,1)S(1)}, u32[]{:S(2)}, u32[]{:S(2)}) collective-permute-start(bf16[4,16,2048]{2,1,0:T(8,128)(2,1)S(1)} %pad_maximum_fusion.refs_0_), channel_id=1, source_target_pairs={{0,24},{4,28},{8,0},{12,4},{16,8},{20,12},{24,16},{28,20},{32,56},... | collective-permute-start | bytes 786440 | tf_op jit(solution)/shard_map/ppermute | solution.py:36
  153.8 11.2 %collective-permute-start.18 = (bf16[4,16,2048]{2,1,0:T(8,128)(2,1)S(1)}, bf16[4,16,2048]{2,1,0:T(8,128)(2,1)S(1)}, u32[]{:S(2)}, u32[]{:S(2)}) collective-permute-start(bf16[4,16,2048]{2,1,0:T(8,128)(2,1)S(1)} %pad_maximum_fusion.refs_0_), channel_id=1, source_target_pairs={{0,16},{4,20},{8,24},{12,28},{16,0},{20,4},{24,8},{28,12},{32,48},... | collective-permute-start | bytes 786440 | tf_op jit(solution)/shard_map/ppermute | solution.py:36
  155.4 10.3 %collective-permute-start.17 = (bf16[4,16,2048]{2,1,0:T(8,128)(2,1)S(1)}, bf16[4,16,2048]{2,1,0:T(8,128)(2,1)S(1)}, u32[]{:S(2)}, u32[]{:S(2)}) collective-permute-start(bf16[4,16,2048]{2,1,0:T(8,128)(2,1)S(1)} %pad_maximum_fusion.refs_0_), channel_id=1, source_target_pairs={{0,8},{4,12},{8,16},{12,20},{16,24},{20,28},{24,0},{28,4},{32,40},... | collective-permute-start | bytes 786440 | tf_op jit(solution)/shard_map/ppermute | solution.py:36
  155.4 15.4 %collective-permute-start.31 = (bf16[4,16,2048]{2,1,0:T(8,128)(2,1)S(1)}, bf16[4,16,2048]{2,1,0:T(8,128)(2,1)S(1)}, u32[]{:S(2)}, u32[]{:S(2)}) collective-permute-start(bf16[4,16,2048]{2,1,0:T(8,128)(2,1)S(1)} %constant_dynamic-update-slice_fusion.refs_4_), channel_id=1, source_target_pairs={{0,4},{4,0},{8,12},{12,8},{16,20},{20,16},{24,28},{28,24},{32,36},... | collective-permute-start | bytes 786440 | tf_op jit(solution)/shard_map/ppermute | solution.py:36
  162.7 13.3 %collective-permute-start.26 = (bf16[4,16,2048]{2,1,0:T(8,128)(2,1)S(1)}, bf16[4,16,2048]{2,1,0:T(8,128)(2,1)S(1)}, u32[]{:S(2)}, u32[]{:S(2)}) collective-permute-start(bf16[4,16,2048]{2,1,0:T(8,128)(2,1)S(1)} %constant_dynamic-update-slice_fusion.refs_4_), channel_id=1, source_target_pairs={{0,96},{4,100},{8,104},{12,108},{16,112},{20,116},{24,120},{28,124... | collective-permute-start | bytes 786440 | tf_op jit(solution)/shard_map/ppermute | solution.py:36
  164.9 12.2 %collective-permute-start.25 = (bf16[4,16,2048]{2,1,0:T(8,128)(2,1)S(1)}, bf16[4,16,2048]{2,1,0:T(8,128)(2,1)S(1)}, u32[]{:S(2)}, u32[]{:S(2)}) collective-permute-start(bf16[4,16,2048]{2,1,0:T(8,128)(2,1)S(1)} %constant_dynamic-update-slice_fusion.refs_4_), channel_id=1, source_target_pairs={{0,64},{4,68},{8,72},{12,76},{16,80},{20,84},{24,88},{28,92},{32,9... | collective-permute-start | bytes 786440 | tf_op jit(solution)/shard_map/ppermute | solution.py:36
  165.0 14.9 %collective-permute-start.24 = (bf16[4,16,2048]{2,1,0:T(8,128)(2,1)S(1)}, bf16[4,16,2048]{2,1,0:T(8,128)(2,1)S(1)}, u32[]{:S(2)}, u32[]{:S(2)}) collective-permute-start(bf16[4,16,2048]{2,1,0:T(8,128)(2,1)S(1)} %constant_dynamic-update-slice_fusion.refs_4_), channel_id=1, source_target_pairs={{0,32},{4,36},{8,40},{12,44},{16,48},{20,52},{24,56},{28,60},{32,6... | collective-permute-start | bytes 786440 | tf_op jit(solution)/shard_map/ppermute | solution.py:36
  165.6 15.0 %collective-permute-start.30 = (bf16[4,16,2048]{2,1,0:T(8,128)(2,1)S(1)}, bf16[4,16,2048]{2,1,0:T(8,128)(2,1)S(1)}, u32[]{:S(2)}, u32[]{:S(2)}) collective-permute-start(bf16[4,16,2048]{2,1,0:T(8,128)(2,1)S(1)} %collective-permute-done.19.refs_3_), channel_id=1, source_target_pairs={{0,4},{4,0},{8,12},{12,8},{16,20},{20,16},{24,28},{28,24},{32,36},... | collective-permute-start | bytes 786440 | tf_op jit(solution)/shard_map/ppermute | solution.py:36
  170.8 12.8 %collective-permute-start.29 = (bf16[4,16,2048]{2,1,0:T(8,128)(2,1)S(1)}, bf16[4,16,2048]{2,1,0:T(8,128)(2,1)S(1)}, u32[]{:S(2)}, u32[]{:S(2)}) collective-permute-start(bf16[4,16,2048]{2,1,0:T(8,128)(2,1)S(1)} %collective-permute-done.18.refs_2_), channel_id=1, source_target_pairs={{0,4},{4,0},{8,12},{12,8},{16,20},{20,16},{24,28},{28,24},{32,36},... | collective-permute-start | bytes 786440 | tf_op jit(solution)/shard_map/ppermute | solution.py:36
  176.0 7.6 %collective-permute-start.28 = (bf16[4,16,2048]{2,1,0:T(8,128)(2,1)S(1)}, bf16[4,16,2048]{2,1,0:T(8,128)(2,1)S(1)}, u32[]{:S(2)}, u32[]{:S(2)}) collective-permute-start(bf16[4,16,2048]{2,1,0:T(8,128)(2,1)S(1)} %collective-permute-done.17.refs_1_), channel_id=1, source_target_pairs={{0,4},{4,0},{8,12},{12,8},{16,20},{20,16},{24,28},{28,24},{32,36},... | collective-permute-start | bytes 786440 | tf_op jit(solution)/shard_map/ppermute | solution.py:36
  177.1 6.5 %collective-permute-start.34 = (bf16[4,16,2048]{2,1,0:T(8,128)(2,1)S(1)}, bf16[4,16,2048]{2,1,0:T(8,128)(2,1)S(1)}, u32[]{:S(2)}, u32[]{:S(2)}) collective-permute-start(bf16[4,16,2048]{2,1,0:T(8,128)(2,1)S(1)} %collective-permute-done.26.refs_7_), channel_id=1, source_target_pairs={{0,4},{4,0},{8,12},{12,8},{16,20},{20,16},{24,28},{28,24},{32,36},... | collective-permute-start | bytes 786440 | tf_op jit(solution)/shard_map/ppermute | solution.py:36
  (12 other events, 174.8 us)

commit v4 on v3

--- a/solution.py
+++ b/solution.py
@@ -91,23 +91,20 @@
     extra = TALL // GROUP
 
     def kernel(
-        count_ref, map_ref, me_ref, mine_ref, acts_ref, grads_ref, weight_ref,
-        keep_ref, send_ref, up_ref, raw, turned, part, total, sems,
+        count_ref, map_ref, me_ref, mine_ref, acts_ref, grads_ref, up_part_ref, down_part_ref,
+        keep_ref, send_ref, up_ref, down_ref, raw, turned, part, up_sum, down_sum, sems,
     ):
         step = pl.program_id(0)
 
-        def add_up():
-            value = lax.dot_general(
-                grads_ref[...], weight_ref[...], (((1,), (1,)), ((), ())), preferred_element_type=f32
-            )
-
-            @pl.when(step == 0)
-            def _():
-                total[...] = value
-
-            @pl.when(step > 0)
-            def _():
-                total[...] += value
+        def add_shares_of(first):
+            for weight_ref, total in ((up_part_ref, up_sum), (down_part_ref, down_sum)):
+                value = lax.dot_general(
+                    grads_ref[...],
+                    weight_ref[...],
+                    (((1,), (1,)), ((), ())),
+                    preferred_element_type=f32,
+                )
+                total[...] = value if first else total[...] + value
 
         def put():
             for p in range(blocks):
@@ -137,13 +134,13 @@
                 else:
                     part[...] += value
             put()
-            add_up()
+            add_shares_of(True)
 
         @pl.when((step > 0) & (step < steps))
         def _():
             part[...] = jnp.dot(turned[...], grads_ref[...], preferred_element_type=f32)
             put()
-            add_up()
+            add_shares_of(False)
 
         @pl.when(step == steps)
         def _():
@@ -154,11 +151,22 @@
             send_ref[:, :, :EXTRA] = value
             for i in range(tokens // TALL):
                 live = lax.broadcasted_iota(jnp.int32, (TALL, width), 0) + i * TALL < count_ref[0]
-                encode(jnp.where(live, total[i * TALL : (i + 1) * TALL], 0.0), up_ref, i)
+                for total, coded_ref in ((up_sum, up_ref), (down_sum, down_ref)):
+                    encode(jnp.where(live, total[i * TALL : (i + 1) * TALL], 0.0), coded_ref, i)
 
     out = jax.ShapeDtypeStruct((near, height, columns + EXTRA), bf16)
     spec = pl.BlockSpec((near, height, wide), lambda n, *_: (0, 0, n))
     code = (tokens // TALL, TALL + extra, width)
+
+    def part_of(offset):
+        return pl.BlockSpec(
+            (width, wide),
+            lambda n, count, map, me, mine: (
+                lax.rem(mine[0] + offset, ways),
+                jnp.minimum(n, steps - 1),
+            ),
+        )
+
     return pl.pallas_call(
         kernel,
         grid_spec=pltpu.PrefetchScalarGridSpec(
@@ -167,27 +175,23 @@
             in_specs=[
                 pl.BlockSpec(memory_space=pl.ANY),
                 pl.BlockSpec((tokens, wide), lambda n, *_: (0, jnp.minimum(n, steps - 1))),
-                pl.BlockSpec(
-                    (width, wide),
-                    lambda n, count, map, me, mine: (
-                        lax.rem(mine[0] + 1, ways),
-                        jnp.minimum(n, steps - 1),
-                    ),
-                ),
+                part_of(1),
+                part_of(ways - 1),
             ],
-            out_specs=[spec, spec, pl.BlockSpec(code, lambda n, *_: (0, 0, 0))],
+            out_specs=[spec, spec] + [pl.BlockSpec(code, lambda n, *_: (0, 0, 0))] * 2,
             scratch_shapes=[
                 pltpu.VMEM((tokens, hidden), bf16),
                 pltpu.VMEM((hidden, tokens), bf16),
                 pltpu.VMEM((hidden, wide), f32),
                 pltpu.VMEM((tokens, width), f32),
+                pltpu.VMEM((tokens, width), f32),
                 pltpu.SemaphoreType.DMA((parts,)),
             ],
         ),
-        out_shape=[out, out, jax.ShapeDtypeStruct(code, i16)],
+        out_shape=[out, out] + [jax.ShapeDtypeStruct(code, i16)] * 2,
         compiler_params=pltpu.CompilerParams(vmem_limit_bytes=60 * 2**20),
         interpret=interpret,
-    )(count, owner_map, me, mine, acts, grads, weight)
+    )(count, owner_map, me, mine, acts, grads, weight, weight)
 
 
 def input_shares(grads, weight, count, mine, ways, offsets, interpret=False):
@@ -234,41 +238,40 @@
     )(count, mine, grads, *[weight] * len(offsets))
 
 
-def add_shares(own, coded, interpret=False):
+def add_shares(own, shares, interpret=False):
     tokens, width = own.shape
-    steps, padded, _ = coded[0].shape
+    places = [[(i, j) for i, piece in enumerate(share) for j in range(piece.shape[0])] for share in shares]
+    steps = len(places[0])
     tall = tokens // steps
     groups = tall // GROUP
+    pieces = [piece for share in shares for piece in share]
 
     def kernel(own_ref, *refs):
-        out = refs[-1]
-
-        def add(step, carry):
-            base = pl.multiple_of(step * tall, tall)
+        out, refs = refs[-1], list(refs[:-1])
+        held = [[refs.pop(0) for _ in share] for share in shares]
+        for step in range(steps):
+            blocks = [mine[places[k][step][0]].at[places[k][step][1]] for k, mine in enumerate(held)]
             factors = [
-                jnp.exp2(-ref[step, tall:padded, :].astype(jnp.int32).astype(f32))
-                for ref in refs[:-1]
+                jnp.exp2(-block[tall : tall + groups, :].astype(jnp.int32).astype(f32))
+                for block in blocks
             ]
             for g in range(groups):
-                rows = pl.ds(base + g * GROUP, GROUP)
+                rows = slice(step * tall + g * GROUP, step * tall + (g + 1) * GROUP)
                 value = own_ref[rows, :]
-                for ref, factor in zip(refs[:-1], factors):
-                    code = ref[step, g * GROUP : (g + 1) * GROUP, :]
+                for block, factor in zip(blocks, factors):
+                    code = block[g * GROUP : (g + 1) * GROUP, :]
                     value += code.astype(jnp.int32).astype(f32) * factor[g : g + 1]
                 out[rows, :] = value.astype(bf16)
-            return carry
-
-        lax.fori_loop(0, steps, add, 0)
 
     whole = pl.BlockSpec(memory_space=pltpu.VMEM)
     return pl.pallas_call(
         kernel,
         out_shape=jax.ShapeDtypeStruct((tokens, width), bf16),
-        in_specs=[whole] * (1 + len(coded)),
+        in_specs=[whole] * (1 + len(pieces)),
         out_specs=whole,
         compiler_params=pltpu.CompilerParams(vmem_limit_bytes=12 * 2**20),
         interpret=interpret,
-    )(own, *coded)
+    )(own, *pieces)
 
 
 def place_blocks(pieces, owner_map, me, interpret=False):
@@ -319,13 +322,12 @@
         ring = [(source, (source + offset) % ways) for source in range(ways)]
         return lax.ppermute(coded, "mp", ring)
 
-    keep, send, up = weight_partials(
+    keep, send, up, down = weight_partials(
         hidden_acts, out_grads, down_weight, token_counts, owner_map, me, my_mp, ways
     )
     arrived = to_core(send)
-    shares = [pass_share(up, 1)]
-    (down,) = input_shares(out_grads, down_weight, token_counts, my_mp, ways, (3,))
-    shares.append(pass_share(down, 3))
+    shares = [[pass_share(up, 1)], [pass_share(down, 3)]]
+    arrived, far_grads = lax.optimization_barrier((arrived, out_grads))
     pair = [
         (keep[4 * i : 4 * i + 4].astype(f32) + arrived[4 * i : 4 * i + 4].astype(f32)).astype(bf16)
         for i in range(8)
@@ -335,6 +337,8 @@
         for colour, (first, _) in enumerate(rings)
     ]
     got = lax.optimization_barrier(got)
+    across, own = input_shares(far_grads, down_weight, token_counts, my_mp, ways, (2, 0))
+    across_early = pass_share(across[:1], 2)
     lines = [
         [
             sum((g[e].astype(f32) for g in got[colour]), pair[4 * colour][e].astype(f32)).astype(bf16)
@@ -346,12 +350,11 @@
         [shift(line[d], second, d) for d in (2, 1, 3)]
         for line, (_, second) in zip(lines, rings)
     ]
-    got = lax.optimization_barrier(got)
+    got, across_rest = lax.optimization_barrier((got, across[1:]))
     sums = [
         sum((g.astype(f32) for g in group), line[0].astype(f32)) for group, line in zip(got, lines)
     ]
     theirs = to_zh(sums[1])
-    across, own = input_shares(out_grads, down_weight, token_counts, my_mp, ways, (2, 0))
     summed = sums[0] + theirs
 
     digits = summed[:1, columns : columns + DIGITS]
@@ -366,7 +369,7 @@
 
     weights = master_new.astype(bf16)[None]
     other = to_zh(weights)
-    shares.append(pass_share(across, 2))
+    shares.append([across_early, pass_share(across_rest, 2)])
     lines = []
     for part, (first, _) in zip((weights, other), rings):
         two, one, three = [shift(part, first, d) for d in (2, 1, 3)]

time: 187 us -> 171 us (0.914)
  starting transfers between devices: 77.9 us -> 63.4 us
  Pallas kernels: 33.2 us -> 29 us
  waiting for transfers between devices: 67.7 us -> 69.9 us
    ppermute x35, waiting for transfers between devices: 33.9 us -> 69.9 us  [move(): return lax.ppermute(value, 'dp', pairs)]
    ppermute x3 -> x4, waiting for transfers between devices: 33.8 us -> 0.01 us  [pass_share(): return lax.ppermute(coded, 'mp', ring)]
    ppermute x35, starting transfers between devices: 74.5 us -> 58.6 us  [move(): return lax.ppermute(value, 'dp', pairs)]
    pallas_call x2 -> x1, Pallas kernels: 13.6 us -> 7.51 us  [input_shares(): pl.pallas_call(kernel, grid_spec=pltpu.PrefetchScalarGridSpec(num_scalar_...]
    slice x0 -> x2, local copies, waits for them, and re-layouts: none -> 2.2 us  [the longest x1 1.23 us: per_device(): got, across_rest = lax.optimization_barrier((got, across[1:]))]
    pallas_call x1, Pallas kernels: 15.4 us -> 17.4 us  [weight_partials(): pl.pallas_call(kernel, grid_spec=pltpu.PrefetchScalarGridSpec(num_scalar_...]
    ppermute x3 -> x4, starting transfers between devices: 3.37 us -> 4.85 us  [pass_share(): return lax.ppermute(coded, 'mp', ring)]
  transfers between devices with their start and end apart: 38 -> 39, of which waited for: 11 -> 9; matrix products, arithmetic and copies ran while one was open for 0% -> 1% of each run, Pallas kernels for 8% -> 5%
where the time goes in v4:
time: 171 us
  waiting for transfers between devices  69.9 us (41%)
  starting transfers between devices  63.4 us (37%)
  Pallas kernels  29 us (17%)
  other arithmetic  4.6 us (3%)
  local copies, waits for them, and re-layouts  2.26 us (1%)
    ppermute x35, waiting for transfers between devices, move(): return lax.ppermute(value, 'dp', pairs)  69.9 us
    ppermute x35, starting transfers between devices, move(): return lax.ppermute(value, 'dp', pairs)  58.6 us
    pallas_call x1, Pallas kernels, weight_partials(): pl.pallas_call(kernel, grid_spec=pltpu.PrefetchScalarGridSpec(num_scalar_...  17.4 us
    pallas_call x1, Pallas kernels, input_shares(): pl.pallas_call(kernel, grid_spec=pltpu.PrefetchScalarGridSpec(num_scalar_...  7.51 us
    ppermute x4, starting transfers between devices, pass_share(): return lax.ppermute(coded, 'mp', ring)  4.85 us
  transfers between devices with their start and end apart: 39, of which 9 were waited for; matrix products, arithmetic and copies ran while one was open for 1% of the time, Pallas kernels for 5%

profile of v4, /device:TPU:1, one launch (start us, length us, event | category | flops | bytes accessed | tf_op | source)
XLA Modules:
  0.0 170.9 jit_solution(11848852674439804534)
XLA Ops:
  1.3 17.4 %shard_map.119 = (bf16[32,16,2176]{2,1,0:T(8,128)(2,1)}, bf16[32,16,2176]{2,1,0:T(8,128)(2,1)}, s16[3,528,256]{2,1,0:T(8,128)(2,1)}, s16[3,528,256]{2,1,0:T(8,128)(2,1)}) custom-call(s32[1]{0:T(128)S(6)} %copy.16.count_ref, s32[64]{0:T(128)} %map_ref.3, s32[1]{0:T(128)} %bitcast.me_ref, s32[1]{0:T(128)} %bitcast.1.mine_ref, bf16[1536,1024]{1,0:T(8,128)(2,1)} %acts_ref.1, ...), custom_call_target="tpu_custom_call" | custom-call | tf_op jit(solution)/shard_map/pallas_call | solution.py:170
  18.6 3.3 %collective-permute-start = (bf16[32,16,2176]{2,1,0:T(8,128)(2,1)}, bf16[32,16,2176]{2,1,0:T(8,128)(2,1)S(1)}, u32[]{:S(2)}, u32[]{:S(2)}) collective-permute-start(bf16[32,16,2176]{2,1,0:T(8,128)(2,1)} %get-tuple-element.27), channel_id=1, source_target_pairs={{0,4},{4,0},{8,12},{12,8},{16,20},{20,16},{24,28},{28,24},{32,36},... | collective-permute-start | bytes 6684680 | tf_op jit(solution)/shard_map/ppermute | solution.py:36
  21.9 4.2 %collective-permute-done = bf16[32,16,2176]{2,1,0:T(8,128)(2,1)S(1)} collective-permute-done((bf16[32,16,2176]{2,1,0:T(8,128)(2,1)}, bf16[32,16,2176]{2,1,0:T(8,128)(2,1)S(1)}, u32[]{:S(2)}, u32[]{:S(2)}) %collective-permute-start) | collective-permute-done | bytes 2228256 | tf_op jit(solution)/shard_map/ppermute | solution.py:36
  26.1 2.1 %add_convert_fusion = (bf16[4,16,2176]{2,1,0:T(8,128)(2,1)S(1)}, bf16[4,16,2176]{2,1,0:T(8,128)(2,1)S(1)}, bf16[4,16,2176]{2,1,0:T(8,128)(2,1)S(1)}, bf16[4,16,2...) fusion(bf16[32,16,2176]{2,1,0:T(8,128)(2,1)S(1)} %collective-pe, ...), kind=kLoop, calls=%fused_computation | loop fusion | flops 4456448 | bytes 6684672 | tf_op jit(solution)/shard_map/convert_element_type | solution.py:332
  29.7 2.4 %collective-permute-start.3 = (bf16[4,16,2176]{2,1,0:T(8,128)(2,1)S(1)}, bf16[4,16,2176]{2,1,0:T(8,128)(2,1)S(1)}, u32[]{:S(2)}, u32[]{:S(2)}) collective-permute-start(bf16[4,16,2176]{2,1,0:T(8,128)(2,1)S(1)} %get-tuple-element.54), channel_id=1, source_target_pairs={{0,96},{4,100},{8,104},{12,108},{16,112},{20,116},{24,120},{28,124... | collective-permute-start | bytes 835592 | tf_op jit(solution)/shard_map/ppermute | solution.py:36
  32.0 2.9 %collective-permute-start.4 = (bf16[4,16,2176]{2,1,0:T(8,128)(2,1)S(1)}, bf16[4,16,2176]{2,1,0:T(8,128)(2,1)S(1)}, u32[]{:S(2)}, u32[]{:S(2)}) collective-permute-start(bf16[4,16,2176]{2,1,0:T(8,128)(2,1)S(1)} %get-tuple-element.53), channel_id=1, source_target_pairs={{0,16},{4,20},{8,24},{12,28},{16,0},{20,4},{24,8},{28,12},{32,48},... | collective-permute-start | bytes 835592 | tf_op jit(solution)/shard_map/ppermute | solution.py:36
  35.4 2.4 %collective-permute-done.1 = bf16[4,16,2176]{2,1,0:T(8,128)(2,1)S(1)} collective-permute-done((bf16[4,16,2176]{2,1,0:T(8,128)(2,1)S(1)}, bf16[4,16,2176]{2,1,0:T(8,128)(2,1)S(1)}, u32[]{:S(2)}, u32[]{:S(2)}) %collective-permute-start.1) | collective-permute-done | bytes 278560 | tf_op jit(solution)/shard_map/ppermute | solution.py:36
  38.8 5.6 %collective-permute-done.2 = bf16[4,16,2176]{2,1,0:T(8,128)(2,1)S(1)} collective-permute-done((bf16[4,16,2176]{2,1,0:T(8,128)(2,1)S(1)}, bf16[4,16,2176]{2,1,0:T(8,128)(2,1)S(1)}, u32[]{:S(2)}, u32[]{:S(2)}) %collective-permute-start.2) | collective-permute-done | bytes 278560 | tf_op jit(solution)/shard_map/ppermute | solution.py:36
  44.4 3.6 %collective-permute-done.5 = bf16[4,16,2176]{2,1,0:T(8,128)(2,1)S(1)} collective-permute-done((bf16[4,16,2176]{2,1,0:T(8,128)(2,1)S(1)}, bf16[4,16,2176]{2,1,0:T(8,128)(2,1)S(1)}, u32[]{:S(2)}, u32[]{:S(2)}) %collective-permute-start.5) | collective-permute-done | bytes 278560 | tf_op jit(solution)/shard_map/ppermute | solution.py:36
  49.0 2.7 %collective-permute-start.12 = (bf16[16,2176]{1,0:T(8,128)(2,1)S(1)}, bf16[16,2176]{1,0:T(8,128)(2,1)S(1)}, u32[]{:S(2)}, u32[]{:S(2)}) collective-permute-start(bf16[16,2176]{1,0:T(8,128)(2,1)S(1)} %get-tuple-element.58), channel_id=1, source_target_pairs={{0,96},{4,100},{8,104},{12,108},{16,112},{20,116},{24,120},{28,124... | collective-permute-start | bytes 208904 | tf_op jit(solution)/shard_map/ppermute | solution.py:36
  51.8 1.4 collective-permute-start.7
  53.7 2.2 %collective-permute-start.9 = (bf16[16,2176]{1,0:T(8,128)(2,1)S(1)}, bf16[16,2176]{1,0:T(8,128)(2,1)S(1)}, u32[]{:S(2)}, u32[]{:S(2)}) collective-permute-start(bf16[16,2176]{1,0:T(8,128)(2,1)S(1)} %get-tuple-element.61), channel_id=1, source_target_pairs={{0,24},{4,28},{8,0},{12,4},{16,8},{20,12},{24,16},{28,20},{32,56},... | collective-permute-start | bytes 208904 | tf_op jit(solution)/shard_map/ppermute | solution.py:36
  55.9 7.5 %shard_map.120 = (s16[3,528,256]{2,1,0:T(8,128)(2,1)}, f32[1536,256]{1,0:T(8,128)}) custom-call(s32[1]{0:T(128)S(6)} %copy.16.count_ref, s32[1]{0:T(128)} %bitcast.1.mine_ref, bf16[1536,2048]{1,0:T(8,128)(2,1)} %grads_ref.2, bf16[1024,2048]{1,0:T(8,128)(2,1)} %refs_1_.1, bf16[1024,2048]{1,0:T(8,128)(2,1)} %refs_1_.1), custom_call_target="tpu_custom_call" | custom-call | tf_op jit(solution)/shard_map/pallas_call | solution.py:226
  64.8 6.4 %collective-permute-start.13 = (f32[16,2176]{1,0:T(8,128)S(1)}, f32[16,2176]{1,0:T(8,128)S(1)}, u32[]{:S(2)}, u32[]{:S(2)}) collective-permute-start(f32[16,2176]{1,0:T(8,128)S(1)} %fusion.1), channel_id=1, source_target_pairs={{0,128},{4,132},{8,136},{12,140},{16,144},{20,148},{24,152},{28,15... | collective-permute-start | bytes 417800 | tf_op jit(solution)/shard_map/ppermute | solution.py:36
  71.2 2.5 %collective-permute-done.13 = f32[16,2176]{1,0:T(8,128)S(1)} collective-permute-done((f32[16,2176]{1,0:T(8,128)S(1)}, f32[16,2176]{1,0:T(8,128)S(1)}, u32[]{:S(2)}, u32[]{:S(2)}) %collective-permute-start.13) | collective-permute-done | bytes 139296 | tf_op jit(solution)/shard_map/ppermute | solution.py:36
  74.5 1.5 convert_bitcast_fusion
  75.9 1.7 collective-permute-start.15
  77.6 2.1 %collective-permute-start.16 = (bf16[1,16,2048]{2,1,0:T(8,128)(2,1)S(1)}, bf16[1,16,2048]{2,1,0:T(8,128)(2,1)S(1)}, u32[]{:S(2)}, u32[]{:S(2)}) collective-permute-start(bf16[1,16,2048]{2,1,0:T(8,128)(2,1)S(1)} %get-tuple-element.47), channel_id=1, source_target_pairs={{0,96},{4,100},{8,104},{12,108},{16,112},{20,116},{24,120},{28,124... | collective-permute-start | bytes 196616 | tf_op jit(solution)/shard_map/ppermute | solution.py:36
  80.3 2.6 %collective-permute-start.36 = (s16[3,528,256]{2,1,0:T(8,128)(2,1)S(1)}, s16[3,528,256]{2,1,0:T(8,128)(2,1)S(1)}, u32[]{:S(2)}, u32[]{:S(2)}) collective-permute-start(s16[3,528,256]{2,1,0:T(8,128)(2,1)S(1)} %copy-done.5), channel_id=1, source_target_pairs={{0,3},{1,0},{2,1},{3,2},{4,7},{5,4},{6,5},{7,6},{8,11},{9,8},{10,9... | collective-permute-start | bytes 2433032 | tf_op jit(solution)/shard_map/ppermute | solution.py:323
  85.2 5.0 %collective-permute-start.20 = (bf16[1,16,2048]{2,1,0:T(8,128)(2,1)S(1)}, bf16[1,16,2048]{2,1,0:T(8,128)(2,1)S(1)}, u32[]{:S(2)}, u32[]{:S(2)}) collective-permute-start(bf16[1,16,2048]{2,1,0:T(8,128)(2,1)S(1)} %get-tuple-element.47), channel_id=1, source_target_pairs={{0,128},{4,132},{8,136},{12,140},{16,144},{20,148},{24,152},{28,15... | collective-permute-start | bytes 196616 | tf_op jit(solution)/shard_map/ppermute | solution.py:36
  90.3 35.8 %collective-permute-done.20 = bf16[1,16,2048]{2,1,0:T(8,128)(2,1)S(1)} collective-permute-done((bf16[1,16,2048]{2,1,0:T(8,128)(2,1)S(1)}, bf16[1,16,2048]{2,1,0:T(8,128)(2,1)S(1)}, u32[]{:S(2)}, u32[]{:S(2)}) %collective-permute-start.20) | collective-permute-done | bytes 65568 | tf_op jit(solution)/shard_map/ppermute | solution.py:36
  126.2 4.6 %collective-permute-done.21 = bf16[1,16,2048]{2,1,0:T(8,128)(2,1)S(1)} collective-permute-done((bf16[1,16,2048]{2,1,0:T(8,128)(2,1)S(1)}, bf16[1,16,2048]{2,1,0:T(8,128)(2,1)S(1)}, u32[]{:S(2)}, u32[]{:S(2)}) %collective-permute-start.21) | collective-permute-done | bytes 65568 | tf_op jit(solution)/shard_map/ppermute | solution.py:36
  130.8 2.1 %collective-permute-start.22 = (bf16[1,16,2048]{2,1,0:T(8,128)(2,1)S(1)}, bf16[1,16,2048]{2,1,0:T(8,128)(2,1)S(1)}, u32[]{:S(2)}, u32[]{:S(2)}) collective-permute-start(bf16[1,16,2048]{2,1,0:T(8,128)(2,1)S(1)} %collective-permute-done.20), channel_id=1, source_target_pairs={{0,16},{4,20},{8,24},{12,28},{16,0},{20,4},{24,8},{28,12},{32,48},... | collective-permute-start | bytes 196616 | tf_op jit(solution)/shard_map/ppermute | solution.py:36
  132.9 2.5 %collective-permute-done.22 = bf16[1,16,2048]{2,1,0:T(8,128)(2,1)S(1)} collective-permute-done((bf16[1,16,2048]{2,1,0:T(8,128)(2,1)S(1)}, bf16[1,16,2048]{2,1,0:T(8,128)(2,1)S(1)}, u32[]{:S(2)}, u32[]{:S(2)}) %collective-permute-start.22) | collective-permute-done | bytes 65568 | tf_op jit(solution)/shard_map/ppermute | solution.py:36
  135.4 1.4 collective-permute-start.23
  139.7 9.6 %collective-permute-start.27 = (bf16[4,16,2048]{2,1,0:T(8,128)(2,1)S(1)}, bf16[4,16,2048]{2,1,0:T(8,128)(2,1)S(1)}, u32[]{:S(2)}, u32[]{:S(2)}) collective-permute-start(bf16[4,16,2048]{2,1,0:T(8,128)(2,1)S(1)} %pad_maximum_fusion.refs_0_), channel_id=1, source_target_pairs={{0,4},{4,0},{8,12},{12,8},{16,20},{20,16},{24,28},{28,24},{32,36},... | collective-permute-start | bytes 786440 | tf_op jit(solution)/shard_map/ppermute | solution.py:36
  149.5 1.9 %collective-permute-start.25 = (bf16[4,16,2048]{2,1,0:T(8,128)(2,1)S(1)}, bf16[4,16,2048]{2,1,0:T(8,128)(2,1)S(1)}, u32[]{:S(2)}, u32[]{:S(2)}) collective-permute-start(bf16[4,16,2048]{2,1,0:T(8,128)(2,1)S(1)} %constant_dynamic-update-slice_fusion.refs_4_), channel_id=1, source_target_pairs={{0,64},{4,68},{8,72},{12,76},{16,80},{20,84},{24,88},{28,92},{32,9... | collective-permute-start | bytes 786440 | tf_op jit(solution)/shard_map/ppermute | solution.py:36
  151.3 2.0 %collective-permute-start.26 = (bf16[4,16,2048]{2,1,0:T(8,128)(2,1)S(1)}, bf16[4,16,2048]{2,1,0:T(8,128)(2,1)S(1)}, u32[]{:S(2)}, u32[]{:S(2)}) collective-permute-start(bf16[4,16,2048]{2,1,0:T(8,128)(2,1)S(1)} %constant_dynamic-update-slice_fusion.refs_4_), channel_id=1, source_target_pairs={{0,96},{4,100},{8,104},{12,108},{16,112},{20,116},{24,120},{28,124... | collective-permute-start | bytes 786440 | tf_op jit(solution)/shard_map/ppermute | solution.py:36
  153.3 2.3 %collective-permute-start.31 = (bf16[4,16,2048]{2,1,0:T(8,128)(2,1)S(1)}, bf16[4,16,2048]{2,1,0:T(8,128)(2,1)S(1)}, u32[]{:S(2)}, u32[]{:S(2)}) collective-permute-start(bf16[4,16,2048]{2,1,0:T(8,128)(2,1)S(1)} %constant_dynamic-update-slice_fusion.refs_4_), channel_id=1, source_target_pairs={{0,4},{4,0},{8,12},{12,8},{16,20},{20,16},{24,28},{28,24},{32,36},... | collective-permute-start | bytes 786440 | tf_op jit(solution)/shard_map/ppermute | solution.py:36
  155.6 8.5 %collective-permute-done.24.refs_5_ = bf16[4,16,2048]{2,1,0:T(8,128)(2,1)S(1)} collective-permute-done((bf16[4,16,2048]{2,1,0:T(8,128)(2,1)S(1)}, bf16[4,16,2048]{2,1,0:T(8,128)(2,1)S(1)}, u32[]{:S(2)}, u32[]{:S(2)}) %collective-permute-start.24) | collective-permute-done | bytes 262176 | tf_op jit(solution)/shard_map/ppermute | solution.py:36
  166.5 1.6 shard_map.122
  168.2 2.5 %shard_map.121 = bf16[64,16,2048]{2,1,0:T(8,128)(2,1)} custom-call(s32[64]{0:T(128)S(1)} %copy-done.1, s32[1]{0:T(128)} %bitcast.me_ref, bf16[4,16,2048]{2,1,0:T(8,128)(2,1)S(1)} %pad_maximum_fusion.refs_0_, bf16[4,16,2048]{2,1,0:T(8,128)(2,1)S(1)} %collective-permute-done.17.refs_1_, bf16[4,16,2048]{2,1,0:T(8,128)(2,1)S(1)} %collective-permute-done.18.refs_2_, ...), custom_call_target="tpu_custom_call" | custom-call | tf_op jit(solution)/shard_map/pallas_call | solution.py:299
  (78 shorter events, 14.9 us)
Async XLA Ops:
  18.6 7.5 %collective-permute-start = (bf16[32,16,2176]{2,1,0:T(8,128)(2,1)}, bf16[32,16,2176]{2,1,0:T(8,128)(2,1)S(1)}, u32[]{:S(2)}, u32[]{:S(2)}) collective-permute-start(bf16[32,16,2176]{2,1,0:T(8,128)(2,1)} %get-tuple-element.27), channel_id=1, source_target_pairs={{0,4},{4,0},{8,12},{12,8},{16,20},{20,16},{24,28},{28,24},{32,36},... | collective-permute-start | bytes 6684680 | tf_op jit(solution)/shard_map/ppermute | solution.py:36
  28.3 9.5 %collective-permute-start.1 = (bf16[4,16,2176]{2,1,0:T(8,128)(2,1)S(1)}, bf16[4,16,2176]{2,1,0:T(8,128)(2,1)S(1)}, u32[]{:S(2)}, u32[]{:S(2)}) collective-permute-start(bf16[4,16,2176]{2,1,0:T(8,128)(2,1)S(1)} %get-tuple-element.56), channel_id=1, source_target_pairs={{0,64},{4,68},{8,72},{12,76},{16,80},{20,84},{24,88},{28,92},{32,9... | collective-permute-start | bytes 835592 | tf_op jit(solution)/shard_map/ppermute | solution.py:36
  29.4 15.0 %collective-permute-start.2 = (bf16[4,16,2176]{2,1,0:T(8,128)(2,1)S(1)}, bf16[4,16,2176]{2,1,0:T(8,128)(2,1)S(1)}, u32[]{:S(2)}, u32[]{:S(2)}) collective-permute-start(bf16[4,16,2176]{2,1,0:T(8,128)(2,1)S(1)} %get-tuple-element.55), channel_id=1, source_target_pairs={{0,32},{4,36},{8,40},{12,44},{16,48},{20,52},{24,56},{28,60},{32,6... | collective-permute-start | bytes 835592 | tf_op jit(solution)/shard_map/ppermute | solution.py:36
  29.7 14.7 %collective-permute-start.3 = (bf16[4,16,2176]{2,1,0:T(8,128)(2,1)S(1)}, bf16[4,16,2176]{2,1,0:T(8,128)(2,1)S(1)}, u32[]{:S(2)}, u32[]{:S(2)}) collective-permute-start(bf16[4,16,2176]{2,1,0:T(8,128)(2,1)S(1)} %get-tuple-element.54), channel_id=1, source_target_pairs={{0,96},{4,100},{8,104},{12,108},{16,112},{20,116},{24,120},{28,124... | collective-permute-start | bytes 835592 | tf_op jit(solution)/shard_map/ppermute | solution.py:36
  32.0 12.4 %collective-permute-start.4 = (bf16[4,16,2176]{2,1,0:T(8,128)(2,1)S(1)}, bf16[4,16,2176]{2,1,0:T(8,128)(2,1)S(1)}, u32[]{:S(2)}, u32[]{:S(2)}) collective-permute-start(bf16[4,16,2176]{2,1,0:T(8,128)(2,1)S(1)} %get-tuple-element.53), channel_id=1, source_target_pairs={{0,16},{4,20},{8,24},{12,28},{16,0},{20,4},{24,8},{28,12},{32,48},... | collective-permute-start | bytes 835592 | tf_op jit(solution)/shard_map/ppermute | solution.py:36
  35.0 13.1 %collective-permute-start.5 = (bf16[4,16,2176]{2,1,0:T(8,128)(2,1)S(1)}, bf16[4,16,2176]{2,1,0:T(8,128)(2,1)S(1)}, u32[]{:S(2)}, u32[]{:S(2)}) collective-permute-start(bf16[4,16,2176]{2,1,0:T(8,128)(2,1)S(1)} %get-tuple-element.52), channel_id=1, source_target_pairs={{0,8},{4,12},{8,16},{12,20},{16,24},{20,28},{24,0},{28,4},{32,40},... | collective-permute-start | bytes 835592 | tf_op jit(solution)/shard_map/ppermute | solution.py:36
  37.7 10.3 %collective-permute-start.6 = (bf16[4,16,2176]{2,1,0:T(8,128)(2,1)S(1)}, bf16[4,16,2176]{2,1,0:T(8,128)(2,1)S(1)}, u32[]{:S(2)}, u32[]{:S(2)}) collective-permute-start(bf16[4,16,2176]{2,1,0:T(8,128)(2,1)S(1)} %get-tuple-element.51), channel_id=1, source_target_pairs={{0,24},{4,28},{8,0},{12,4},{16,8},{20,12},{24,16},{28,20},{32,56},... | collective-permute-start | bytes 835592 | tf_op jit(solution)/shard_map/ppermute | solution.py:36
  48.2 5.6 %collective-permute-start.10 = (bf16[16,2176]{1,0:T(8,128)(2,1)S(1)}, bf16[16,2176]{1,0:T(8,128)(2,1)S(1)}, u32[]{:S(2)}, u32[]{:S(2)}) collective-permute-start(bf16[16,2176]{1,0:T(8,128)(2,1)S(1)} %get-tuple-element.60), channel_id=1, source_target_pairs={{0,64},{4,68},{8,72},{12,76},{16,80},{20,84},{24,88},{28,92},{32,9... | collective-permute-start | bytes 208904 | tf_op jit(solution)/shard_map/ppermute | solution.py:36
  49.0 15.7 %collective-permute-start.11 = (bf16[16,2176]{1,0:T(8,128)(2,1)S(1)}, bf16[16,2176]{1,0:T(8,128)(2,1)S(1)}, u32[]{:S(2)}, u32[]{:S(2)}) collective-permute-start(bf16[16,2176]{1,0:T(8,128)(2,1)S(1)} %get-tuple-element.59), channel_id=1, source_target_pairs={{0,32},{4,36},{8,40},{12,44},{16,48},{20,52},{24,56},{28,60},{32,6... | collective-permute-start | bytes 208904 | tf_op jit(solution)/shard_map/ppermute | solution.py:36
  49.0 15.7 %collective-permute-start.12 = (bf16[16,2176]{1,0:T(8,128)(2,1)S(1)}, bf16[16,2176]{1,0:T(8,128)(2,1)S(1)}, u32[]{:S(2)}, u32[]{:S(2)}) collective-permute-start(bf16[16,2176]{1,0:T(8,128)(2,1)S(1)} %get-tuple-element.58), channel_id=1, source_target_pairs={{0,96},{4,100},{8,104},{12,108},{16,112},{20,116},{24,120},{28,124... | collective-permute-start | bytes 208904 | tf_op jit(solution)/shard_map/ppermute | solution.py:36
  51.8 12.9 %collective-permute-start.7 = (bf16[16,2176]{1,0:T(8,128)(2,1)S(1)}, bf16[16,2176]{1,0:T(8,128)(2,1)S(1)}, u32[]{:S(2)}, u32[]{:S(2)}) collective-permute-start(bf16[16,2176]{1,0:T(8,128)(2,1)S(1)} %get-tuple-element.63), channel_id=1, source_target_pairs={{0,16},{4,20},{8,24},{12,28},{16,0},{20,4},{24,8},{28,12},{32,48},... | collective-permute-start | bytes 208904 | tf_op jit(solution)/shard_map/ppermute | solution.py:36
  53.2 11.5 %collective-permute-start.8 = (bf16[16,2176]{1,0:T(8,128)(2,1)S(1)}, bf16[16,2176]{1,0:T(8,128)(2,1)S(1)}, u32[]{:S(2)}, u32[]{:S(2)}) collective-permute-start(bf16[16,2176]{1,0:T(8,128)(2,1)S(1)} %get-tuple-element.62), channel_id=1, source_target_pairs={{0,8},{4,12},{8,16},{12,20},{16,24},{20,28},{24,0},{28,4},{32,40},... | collective-permute-start | bytes 208904 | tf_op jit(solution)/shard_map/ppermute | solution.py:36
  53.7 11.0 %collective-permute-start.9 = (bf16[16,2176]{1,0:T(8,128)(2,1)S(1)}, bf16[16,2176]{1,0:T(8,128)(2,1)S(1)}, u32[]{:S(2)}, u32[]{:S(2)}) collective-permute-start(bf16[16,2176]{1,0:T(8,128)(2,1)S(1)} %get-tuple-element.61), channel_id=1, source_target_pairs={{0,24},{4,28},{8,0},{12,4},{16,8},{20,12},{24,16},{28,20},{32,56},... | collective-permute-start | bytes 208904 | tf_op jit(solution)/shard_map/ppermute | solution.py:36
  64.8 8.9 %collective-permute-start.13 = (f32[16,2176]{1,0:T(8,128)S(1)}, f32[16,2176]{1,0:T(8,128)S(1)}, u32[]{:S(2)}, u32[]{:S(2)}) collective-permute-start(f32[16,2176]{1,0:T(8,128)S(1)} %fusion.1), channel_id=1, source_target_pairs={{0,128},{4,132},{8,136},{12,140},{16,144},{20,148},{24,152},{28,15... | collective-permute-start | bytes 417800 | tf_op jit(solution)/shard_map/ppermute | solution.py:36
  75.9 8.0 %collective-permute-start.14 = (bf16[1,16,2048]{2,1,0:T(8,128)(2,1)S(1)}, bf16[1,16,2048]{2,1,0:T(8,128)(2,1)S(1)}, u32[]{:S(2)}, u32[]{:S(2)}) collective-permute-start(bf16[1,16,2048]{2,1,0:T(8,128)(2,1)S(1)} %get-tuple-element.47), channel_id=1, source_target_pairs={{0,32},{4,36},{8,40},{12,44},{16,48},{20,52},{24,56},{28,60},{32,6... | collective-permute-start | bytes 196616 | tf_op jit(solution)/shard_map/ppermute | solution.py:36
  75.9 9.3 %collective-permute-start.15 = (bf16[1,16,2048]{2,1,0:T(8,128)(2,1)S(1)}, bf16[1,16,2048]{2,1,0:T(8,128)(2,1)S(1)}, u32[]{:S(2)}, u32[]{:S(2)}) collective-permute-start(bf16[1,16,2048]{2,1,0:T(8,128)(2,1)S(1)} %get-tuple-element.47), channel_id=1, source_target_pairs={{0,64},{4,68},{8,72},{12,76},{16,80},{20,84},{24,88},{28,92},{32,9... | collective-permute-start | bytes 196616 | tf_op jit(solution)/shard_map/ppermute | solution.py:36
  77.6 12.6 %collective-permute-start.16 = (bf16[1,16,2048]{2,1,0:T(8,128)(2,1)S(1)}, bf16[1,16,2048]{2,1,0:T(8,128)(2,1)S(1)}, u32[]{:S(2)}, u32[]{:S(2)}) collective-permute-start(bf16[1,16,2048]{2,1,0:T(8,128)(2,1)S(1)} %get-tuple-element.47), channel_id=1, source_target_pairs={{0,96},{4,100},{8,104},{12,108},{16,112},{20,116},{24,120},{28,124... | collective-permute-start | bytes 196616 | tf_op jit(solution)/shard_map/ppermute | solution.py:36
  79.7 57.2 %collective-permute-start.35 = (s16[3,528,256]{2,1,0:T(8,128)(2,1)S(1)}, s16[3,528,256]{2,1,0:T(8,128)(2,1)S(1)}, u32[]{:S(2)}, u32[]{:S(2)}) collective-permute-start(s16[3,528,256]{2,1,0:T(8,128)(2,1)S(1)} %copy-done.6), channel_id=1, source_target_pairs={{0,1},{1,2},{2,3},{3,0},{4,5},{5,6},{6,7},{7,4},{8,9},{9,10},{10,1... | collective-permute-start | bytes 2433032 | tf_op jit(solution)/shard_map/ppermute | solution.py:323
  80.3 56.8 %collective-permute-start.36 = (s16[3,528,256]{2,1,0:T(8,128)(2,1)S(1)}, s16[3,528,256]{2,1,0:T(8,128)(2,1)S(1)}, u32[]{:S(2)}, u32[]{:S(2)}) collective-permute-start(s16[3,528,256]{2,1,0:T(8,128)(2,1)S(1)} %copy-done.5), channel_id=1, source_target_pairs={{0,3},{1,0},{2,1},{3,2},{4,7},{5,4},{6,5},{7,6},{8,11},{9,8},{10,9... | collective-permute-start | bytes 2433032 | tf_op jit(solution)/shard_map/ppermute | solution.py:323
  83.9 54.5 %collective-permute-start.37 = (s16[1,528,256]{2,1,0:T(8,128)(2,1)S(1)}, s16[1,528,256]{2,1,0:T(8,128)(2,1)S(1)}, u32[]{:S(2)}, u32[]{:S(2)}) collective-permute-start(s16[1,528,256]{2,1,0:T(8,128)(2,1)S(1)} %slice.207), channel_id=1, source_target_pairs={{0,2},{1,3},{2,0},{3,1},{4,6},{5,7},{6,4},{7,5},{8,10},{9,11},{10,... | collective-permute-start | bytes 811016 | tf_op jit(solution)/shard_map/ppermute | solution.py:323
  85.2 41.0 %collective-permute-start.20 = (bf16[1,16,2048]{2,1,0:T(8,128)(2,1)S(1)}, bf16[1,16,2048]{2,1,0:T(8,128)(2,1)S(1)}, u32[]{:S(2)}, u32[]{:S(2)}) collective-permute-start(bf16[1,16,2048]{2,1,0:T(8,128)(2,1)S(1)} %get-tuple-element.47), channel_id=1, source_target_pairs={{0,128},{4,132},{8,136},{12,140},{16,144},{20,148},{24,152},{28,15... | collective-permute-start | bytes 196616 | tf_op jit(solution)/shard_map/ppermute | solution.py:36
  90.2 59.1 %collective-permute-start.17 = (bf16[4,16,2048]{2,1,0:T(8,128)(2,1)S(1)}, bf16[4,16,2048]{2,1,0:T(8,128)(2,1)S(1)}, u32[]{:S(2)}, u32[]{:S(2)}) collective-permute-start(bf16[4,16,2048]{2,1,0:T(8,128)(2,1)S(1)} %pad_maximum_fusion.refs_0_), channel_id=1, source_target_pairs={{0,8},{4,12},{8,16},{12,20},{16,24},{20,28},{24,0},{28,4},{32,40},... | collective-permute-start | bytes 786440 | tf_op jit(solution)/shard_map/ppermute | solution.py:36
  126.2 4.6 %collective-permute-start.21 = (bf16[1,16,2048]{2,1,0:T(8,128)(2,1)S(1)}, bf16[1,16,2048]{2,1,0:T(8,128)(2,1)S(1)}, u32[]{:S(2)}, u32[]{:S(2)}) collective-permute-start(bf16[1,16,2048]{2,1,0:T(8,128)(2,1)S(1)} %collective-permute-done.20), channel_id=1, source_target_pairs={{0,8},{4,12},{8,16},{12,20},{16,24},{20,28},{24,0},{28,4},{32,40},... | collective-permute-start | bytes 196616 | tf_op jit(solution)/shard_map/ppermute | solution.py:36
  130.8 4.6 %collective-permute-start.22 = (bf16[1,16,2048]{2,1,0:T(8,128)(2,1)S(1)}, bf16[1,16,2048]{2,1,0:T(8,128)(2,1)S(1)}, u32[]{:S(2)}, u32[]{:S(2)}) collective-permute-start(bf16[1,16,2048]{2,1,0:T(8,128)(2,1)S(1)} %collective-permute-done.20), channel_id=1, source_target_pairs={{0,16},{4,20},{8,24},{12,28},{16,0},{20,4},{24,8},{28,12},{32,48},... | collective-permute-start | bytes 196616 | tf_op jit(solution)/shard_map/ppermute | solution.py:36
  136.8 28.8 %collective-permute-start.38 = (s16[2,528,256]{2,1,0:T(8,128)(2,1)S(1)}, s16[2,528,256]{2,1,0:T(8,128)(2,1)S(1)}, u32[]{:S(2)}, u32[]{:S(2)}) collective-permute-start(s16[2,528,256]{2,1,0:T(8,128)(2,1)S(1)} %slice.200), channel_id=1, source_target_pairs={{0,2},{1,3},{2,0},{3,1},{4,6},{5,7},{6,4},{7,5},{8,10},{9,11},{10,... | collective-permute-start | bytes 1622024 | tf_op jit(solution)/shard_map/ppermute | solution.py:323
  137.2 12.3 %collective-permute-start.18 = (bf16[4,16,2048]{2,1,0:T(8,128)(2,1)S(1)}, bf16[4,16,2048]{2,1,0:T(8,128)(2,1)S(1)}, u32[]{:S(2)}, u32[]{:S(2)}) collective-permute-start(bf16[4,16,2048]{2,1,0:T(8,128)(2,1)S(1)} %pad_maximum_fusion.refs_0_), channel_id=1, source_target_pairs={{0,16},{4,20},{8,24},{12,28},{16,0},{20,4},{24,8},{28,12},{32,48},... | collective-permute-start | bytes 786440 | tf_op jit(solution)/shard_map/ppermute | solution.py:36
  138.4 13.0 %collective-permute-start.19 = (bf16[4,16,2048]{2,1,0:T(8,128)(2,1)S(1)}, bf16[4,16,2048]{2,1,0:T(8,128)(2,1)S(1)}, u32[]{:S(2)}, u32[]{:S(2)}) collective-permute-start(bf16[4,16,2048]{2,1,0:T(8,128)(2,1)S(1)} %pad_maximum_fusion.refs_0_), channel_id=1, source_target_pairs={{0,24},{4,28},{8,0},{12,4},{16,8},{20,12},{24,16},{28,20},{32,56},... | collective-permute-start | bytes 786440 | tf_op jit(solution)/shard_map/ppermute | solution.py:36
  139.7 13.6 %collective-permute-start.27 = (bf16[4,16,2048]{2,1,0:T(8,128)(2,1)S(1)}, bf16[4,16,2048]{2,1,0:T(8,128)(2,1)S(1)}, u32[]{:S(2)}, u32[]{:S(2)}) collective-permute-start(bf16[4,16,2048]{2,1,0:T(8,128)(2,1)S(1)} %pad_maximum_fusion.refs_0_), channel_id=1, source_target_pairs={{0,4},{4,0},{8,12},{12,8},{16,20},{20,16},{24,28},{28,24},{32,36},... | collective-permute-start | bytes 786440 | tf_op jit(solution)/shard_map/ppermute | solution.py:36
  149.4 14.8 %collective-permute-start.24 = (bf16[4,16,2048]{2,1,0:T(8,128)(2,1)S(1)}, bf16[4,16,2048]{2,1,0:T(8,128)(2,1)S(1)}, u32[]{:S(2)}, u32[]{:S(2)}) collective-permute-start(bf16[4,16,2048]{2,1,0:T(8,128)(2,1)S(1)} %constant_dynamic-update-slice_fusion.refs_4_), channel_id=1, source_target_pairs={{0,32},{4,36},{8,40},{12,44},{16,48},{20,52},{24,56},{28,60},{32,6... | collective-permute-start | bytes 786440 | tf_op jit(solution)/shard_map/ppermute | solution.py:36
  149.5 15.5 %collective-permute-start.25 = (bf16[4,16,2048]{2,1,0:T(8,128)(2,1)S(1)}, bf16[4,16,2048]{2,1,0:T(8,128)(2,1)S(1)}, u32[]{:S(2)}, u32[]{:S(2)}) collective-permute-start(bf16[4,16,2048]{2,1,0:T(8,128)(2,1)S(1)} %constant_dynamic-update-slice_fusion.refs_4_), channel_id=1, source_target_pairs={{0,64},{4,68},{8,72},{12,76},{16,80},{20,84},{24,88},{28,92},{32,9... | collective-permute-start | bytes 786440 | tf_op jit(solution)/shard_map/ppermute | solution.py:36
  151.3 13.7 %collective-permute-start.26 = (bf16[4,16,2048]{2,1,0:T(8,128)(2,1)S(1)}, bf16[4,16,2048]{2,1,0:T(8,128)(2,1)S(1)}, u32[]{:S(2)}, u32[]{:S(2)}) collective-permute-start(bf16[4,16,2048]{2,1,0:T(8,128)(2,1)S(1)} %constant_dynamic-update-slice_fusion.refs_4_), channel_id=1, source_target_pairs={{0,96},{4,100},{8,104},{12,108},{16,112},{20,116},{24,120},{28,124... | collective-permute-start | bytes 786440 | tf_op jit(solution)/shard_map/ppermute | solution.py:36
  153.3 12.3 %collective-permute-start.31 = (bf16[4,16,2048]{2,1,0:T(8,128)(2,1)S(1)}, bf16[4,16,2048]{2,1,0:T(8,128)(2,1)S(1)}, u32[]{:S(2)}, u32[]{:S(2)}) collective-permute-start(bf16[4,16,2048]{2,1,0:T(8,128)(2,1)S(1)} %constant_dynamic-update-slice_fusion.refs_4_), channel_id=1, source_target_pairs={{0,4},{4,0},{8,12},{12,8},{16,20},{20,16},{24,28},{28,24},{32,36},... | collective-permute-start | bytes 786440 | tf_op jit(solution)/shard_map/ppermute | solution.py:36
  (14 other events, 190.6 us)

commit v5 on v4

--- a/solution.py
+++ b/solution.py
@@ -338,7 +338,6 @@
     ]
     got = lax.optimization_barrier(got)
     across, own = input_shares(far_grads, down_weight, token_counts, my_mp, ways, (2, 0))
-    across_early = pass_share(across[:1], 2)
     lines = [
         [
             sum((g[e].astype(f32) for g in got[colour]), pair[4 * colour][e].astype(f32)).astype(bf16)
@@ -346,14 +345,10 @@
         ]
         for colour in range(2)
     ]
-    got = [
-        [shift(line[d], second, d) for d in (2, 1, 3)]
-        for line, (_, second) in zip(lines, rings)
-    ]
-    got, across_rest = lax.optimization_barrier((got, across[1:]))
-    sums = [
-        sum((g.astype(f32) for g in group), line[0].astype(f32)) for group, line in zip(got, lines)
-    ]
+    sums = []
+    for line, (_, second) in zip(lines, rings):
+        got = lax.optimization_barrier([shift(line[d], second, d) for d in (2, 1, 3)])
+        sums.append(sum((g.astype(f32) for g in got), line[0].astype(f32)))
     theirs = to_zh(sums[1])
     summed = sums[0] + theirs
 
@@ -369,7 +364,7 @@
 
     weights = master_new.astype(bf16)[None]
     other = to_zh(weights)
-    shares.append([across_early, pass_share(across_rest, 2)])
+    shares.append([pass_share(across, 2)])
     lines = []
     for part, (first, _) in zip((weights, other), rings):
         two, one, three = [shift(part, first, d) for d in (2, 1, 3)]

time: 171 us -> 176 us (1.029)
  waiting for transfers between devices: 69.9 us -> 79.5 us
  starting transfers between devices: 63.4 us -> 59.6 us
    ppermute x4 -> x3, waiting for transfers between devices: 0.01 us -> 41.1 us  [pass_share(): return lax.ppermute(coded, 'mp', ring)]
    ppermute x35, waiting for transfers between devices: 69.9 us -> 38.4 us  [move(): return lax.ppermute(value, 'dp', pairs)]
    ppermute x35, starting transfers between devices: 58.6 us -> 55 us  [move(): return lax.ppermute(value, 'dp', pairs)]
    slice x2 -> x0, local copies, waits for them, and re-layouts: 2.2 us -> none  [the longest x1 1.23 us: per_device(): got, across_rest = lax.optimization_barrier((got, across[1:]))]
    ppermute x4 -> x3, starting transfers between devices: 4.85 us -> 4.54 us  [pass_share(): return lax.ppermute(coded, 'mp', ring)]
  transfers between devices with their start and end apart: 39 -> 38, of which waited for: 9 -> 12; matrix products, arithmetic and copies ran while one was open for 1% -> 0% of each run, Pallas kernels for 5% -> 5%
where the time goes in v5:
time: 176 us
  waiting for transfers between devices  79.5 us (45%)
  starting transfers between devices  59.6 us (34%)
  Pallas kernels  29 us (16%)
  other arithmetic  4.6 us (3%)
    ppermute x35, starting transfers between devices, move(): return lax.ppermute(value, 'dp', pairs)  55 us
    ppermute x3, waiting for transfers between devices, pass_share(): return lax.ppermute(coded, 'mp', ring)  41.1 us
    ppermute x35, waiting for transfers between devices, move(): return lax.ppermute(value, 'dp', pairs)  38.4 us
    pallas_call x1, Pallas kernels, weight_partials(): pl.pallas_call(kernel, grid_spec=pltpu.PrefetchScalarGridSpec(num_scalar_...  17.4 us
    pallas_call x1, Pallas kernels, input_shares(): pl.pallas_call(kernel, grid_spec=pltpu.PrefetchScalarGridSpec(num_scalar_...  7.52 us
    ppermute x3, starting transfers between devices, pass_share(): return lax.ppermute(coded, 'mp', ring)  4.54 us
  transfers between devices with their start and end apart: 38, of which 12 were waited for; matrix products, arithmetic and copies ran while one was open for 0% of the time, Pallas kernels for 5%

profile of v5, /device:TPU:1, one launch (start us, length us, event | category | flops | bytes accessed | tf_op | source)
XLA Modules:
  0.0 175.8 jit_solution(6772076414139401736)
XLA Ops:
  1.3 17.4 %shard_map.119 = (bf16[32,16,2176]{2,1,0:T(8,128)(2,1)}, bf16[32,16,2176]{2,1,0:T(8,128)(2,1)}, s16[3,528,256]{2,1,0:T(8,128)(2,1)}, s16[3,528,256]{2,1,0:T(8,128)(2,1)}) custom-call(s32[1]{0:T(128)S(6)} %copy.16.count_ref, s32[64]{0:T(128)} %map_ref.3, s32[1]{0:T(128)} %bitcast.me_ref, s32[1]{0:T(128)} %bitcast.1.mine_ref, bf16[1536,1024]{1,0:T(8,128)(2,1)} %acts_ref.1, ...), custom_call_target="tpu_custom_call" | custom-call | tf_op jit(solution)/shard_map/pallas_call | solution.py:170
  18.6 3.3 %collective-permute-start = (bf16[32,16,2176]{2,1,0:T(8,128)(2,1)}, bf16[32,16,2176]{2,1,0:T(8,128)(2,1)S(1)}, u32[]{:S(2)}, u32[]{:S(2)}) collective-permute-start(bf16[32,16,2176]{2,1,0:T(8,128)(2,1)} %get-tuple-element.26), channel_id=1, source_target_pairs={{0,4},{4,0},{8,12},{12,8},{16,20},{20,16},{24,28},{28,24},{32,36},... | collective-permute-start | bytes 6684680 | tf_op jit(solution)/shard_map/ppermute | solution.py:36
  21.9 4.2 %collective-permute-done = bf16[32,16,2176]{2,1,0:T(8,128)(2,1)S(1)} collective-permute-done((bf16[32,16,2176]{2,1,0:T(8,128)(2,1)}, bf16[32,16,2176]{2,1,0:T(8,128)(2,1)S(1)}, u32[]{:S(2)}, u32[]{:S(2)}) %collective-permute-start) | collective-permute-done | bytes 2228256 | tf_op jit(solution)/shard_map/ppermute | solution.py:36
  26.1 2.1 %add_convert_fusion.7 = (bf16[4,16,2176]{2,1,0:T(8,128)(2,1)S(1)}, bf16[4,16,2176]{2,1,0:T(8,128)(2,1)S(1)}, bf16[4,16,2176]{2,1,0:T(8,128)(2,1)S(1)}, bf16[4,16...) fusion(bf16[32,16,2176]{2,1,0:T(8,128)(2,1)S(1)} %collective-pe, ...), kind=kLoop, calls=%fused_computation.7 | loop fusion | flops 4456448 | bytes 6684672 | tf_op jit(solution)/shard_map/convert_element_type | solution.py:332
  31.1 2.5 %collective-permute-start.3 = (bf16[4,16,2176]{2,1,0:T(8,128)(2,1)S(1)}, bf16[4,16,2176]{2,1,0:T(8,128)(2,1)S(1)}, u32[]{:S(2)}, u32[]{:S(2)}) collective-permute-start(bf16[4,16,2176]{2,1,0:T(8,128)(2,1)S(1)} %get-tuple-element.53), channel_id=1, source_target_pairs={{0,96},{4,100},{8,104},{12,108},{16,112},{20,116},{24,120},{28,124... | collective-permute-start | bytes 835592 | tf_op jit(solution)/shard_map/ppermute | solution.py:36
  33.5 2.7 %collective-permute-done.6 = bf16[4,16,2176]{2,1,0:T(8,128)(2,1)S(1)} collective-permute-done((bf16[4,16,2176]{2,1,0:T(8,128)(2,1)S(1)}, bf16[4,16,2176]{2,1,0:T(8,128)(2,1)S(1)}, u32[]{:S(2)}, u32[]{:S(2)}) %collective-permute-start.6) | collective-permute-done | bytes 278560 | tf_op jit(solution)/shard_map/ppermute | solution.py:36
  36.2 7.4 %collective-permute-start.1 = (bf16[4,16,2176]{2,1,0:T(8,128)(2,1)S(1)}, bf16[4,16,2176]{2,1,0:T(8,128)(2,1)S(1)}, u32[]{:S(2)}, u32[]{:S(2)}) collective-permute-start(bf16[4,16,2176]{2,1,0:T(8,128)(2,1)S(1)} %get-tuple-element.55), channel_id=1, source_target_pairs={{0,64},{4,68},{8,72},{12,76},{16,80},{20,84},{24,88},{28,92},{32,9... | collective-permute-start | bytes 835592 | tf_op jit(solution)/shard_map/ppermute | solution.py:36
  43.6 5.6 %collective-permute-done.1 = bf16[4,16,2176]{2,1,0:T(8,128)(2,1)S(1)} collective-permute-done((bf16[4,16,2176]{2,1,0:T(8,128)(2,1)S(1)}, bf16[4,16,2176]{2,1,0:T(8,128)(2,1)S(1)}, u32[]{:S(2)}, u32[]{:S(2)}) %collective-permute-start.1) | collective-permute-done | bytes 278560 | tf_op jit(solution)/shard_map/ppermute | solution.py:36
  49.4 2.5 %collective-permute-start.12 = (bf16[16,2176]{1,0:T(8,128)(2,1)S(1)}, bf16[16,2176]{1,0:T(8,128)(2,1)S(1)}, u32[]{:S(2)}, u32[]{:S(2)}) collective-permute-start(bf16[16,2176]{1,0:T(8,128)(2,1)S(1)} %get-tuple-element.59), channel_id=1, source_target_pairs={{0,96},{4,100},{8,104},{12,108},{16,112},{20,116},{24,120},{28,124... | collective-permute-start | bytes 208904 | tf_op jit(solution)/shard_map/ppermute | solution.py:36
  51.9 1.7 collective-permute-start.10
  53.6 3.4 %collective-permute-done.11 = bf16[16,2176]{1,0:T(8,128)(2,1)S(1)} collective-permute-done((bf16[16,2176]{1,0:T(8,128)(2,1)S(1)}, bf16[16,2176]{1,0:T(8,128)(2,1)S(1)}, u32[]{:S(2)}, u32[]{:S(2)}) %collective-permute-start.11) | collective-permute-done | bytes 69664 | tf_op jit(solution)/shard_map/ppermute | solution.py:36
  57.1 7.0 %collective-permute-start.13 = (f32[16,2176]{1,0:T(8,128)S(1)}, f32[16,2176]{1,0:T(8,128)S(1)}, u32[]{:S(2)}, u32[]{:S(2)}) collective-permute-start(f32[16,2176]{1,0:T(8,128)S(1)} %fusion.1), channel_id=1, source_target_pairs={{0,128},{4,132},{8,136},{12,140},{16,144},{20,148},{24,152},{28,15... | collective-permute-start | bytes 417800 | tf_op jit(solution)/shard_map/ppermute | solution.py:36
  64.2 3.8 %collective-permute-start.9 = (bf16[16,2176]{1,0:T(8,128)(2,1)S(1)}, bf16[16,2176]{1,0:T(8,128)(2,1)S(1)}, u32[]{:S(2)}, u32[]{:S(2)}) collective-permute-start(bf16[16,2176]{1,0:T(8,128)(2,1)S(1)} %get-tuple-element.56), channel_id=1, source_target_pairs={{0,24},{4,28},{8,0},{12,4},{16,8},{20,12},{24,16},{28,20},{32,56},... | collective-permute-start | bytes 208904 | tf_op jit(solution)/shard_map/ppermute | solution.py:36
  69.3 3.7 %collective-permute-done.8 = bf16[16,2176]{1,0:T(8,128)(2,1)S(1)} collective-permute-done((bf16[16,2176]{1,0:T(8,128)(2,1)S(1)}, bf16[16,2176]{1,0:T(8,128)(2,1)S(1)}, u32[]{:S(2)}, u32[]{:S(2)}) %collective-permute-start.8) | collective-permute-done | bytes 69664 | tf_op jit(solution)/shard_map/ppermute | solution.py:36
  73.8 1.5 convert_bitcast_fusion
  76.3 2.2 %collective-permute-start.36 = (s16[3,528,256]{2,1,0:T(8,128)(2,1)S(1)}, s16[3,528,256]{2,1,0:T(8,128)(2,1)S(1)}, u32[]{:S(2)}, u32[]{:S(2)}) collective-permute-start(s16[3,528,256]{2,1,0:T(8,128)(2,1)S(1)} %copy-done.5), channel_id=1, source_target_pairs={{0,3},{1,0},{2,1},{3,2},{4,7},{5,4},{6,5},{7,6},{8,11},{9,8},{10,9... | collective-permute-start | bytes 2433032 | tf_op jit(solution)/shard_map/ppermute | solution.py:323
  78.5 2.3 %collective-permute-start.16 = (bf16[1,16,2048]{2,1,0:T(8,128)(2,1)S(1)}, bf16[1,16,2048]{2,1,0:T(8,128)(2,1)S(1)}, u32[]{:S(2)}, u32[]{:S(2)}) collective-permute-start(bf16[1,16,2048]{2,1,0:T(8,128)(2,1)S(1)} %get-tuple-element.45), channel_id=1, source_target_pairs={{0,96},{4,100},{8,104},{12,108},{16,112},{20,116},{24,120},{28,124... | collective-permute-start | bytes 196616 | tf_op jit(solution)/shard_map/ppermute | solution.py:36
  80.9 1.5 collective-permute-done.20
  82.5 7.5 %shard_map.121 = (s16[3,528,256]{2,1,0:T(8,128)(2,1)}, f32[1536,256]{1,0:T(8,128)}) custom-call(s32[1]{0:T(128)S(6)} %copy.16.count_ref, s32[1]{0:T(128)} %bitcast.1.mine_ref, bf16[1536,2048]{1,0:T(8,128)(2,1)} %grads_ref.2, bf16[1024,2048]{1,0:T(8,128)(2,1)} %refs_1_.1, bf16[1024,2048]{1,0:T(8,128)(2,1)} %refs_1_.1), custom_call_target="tpu_custom_call" | custom-call | tf_op jit(solution)/shard_map/pallas_call | solution.py:226
  90.1 1.3 collective-permute-start.37
  91.3 3.0 %collective-permute-start.23 = (bf16[1,16,2048]{2,1,0:T(8,128)(2,1)S(1)}, bf16[1,16,2048]{2,1,0:T(8,128)(2,1)S(1)}, u32[]{:S(2)}, u32[]{:S(2)}) collective-permute-start(bf16[1,16,2048]{2,1,0:T(8,128)(2,1)S(1)} %collective-permute-done.20), channel_id=1, source_target_pairs={{0,24},{4,28},{8,0},{12,4},{16,8},{20,12},{24,16},{28,20},{32,56},... | collective-permute-start | bytes 196616 | tf_op jit(solution)/shard_map/ppermute | solution.py:36
  94.4 4.6 %collective-permute-done.21 = bf16[1,16,2048]{2,1,0:T(8,128)(2,1)S(1)} collective-permute-done((bf16[1,16,2048]{2,1,0:T(8,128)(2,1)S(1)}, bf16[1,16,2048]{2,1,0:T(8,128)(2,1)S(1)}, u32[]{:S(2)}, u32[]{:S(2)}) %collective-permute-start.21) | collective-permute-done | bytes 65568 | tf_op jit(solution)/shard_map/ppermute | solution.py:36
  99.0 8.3 %collective-permute-start.27 = (bf16[4,16,2048]{2,1,0:T(8,128)(2,1)S(1)}, bf16[4,16,2048]{2,1,0:T(8,128)(2,1)S(1)}, u32[]{:S(2)}, u32[]{:S(2)}) collective-permute-start(bf16[4,16,2048]{2,1,0:T(8,128)(2,1)S(1)} %pad_maximum_fusion.refs_0_), channel_id=1, source_target_pairs={{0,4},{4,0},{8,12},{12,8},{16,20},{20,16},{24,28},{28,24},{32,36},... | collective-permute-start | bytes 786440 | tf_op jit(solution)/shard_map/ppermute | solution.py:36
  107.4 7.1 %collective-permute-done.36.refs_1_ = s16[3,528,256]{2,1,0:T(8,128)(2,1)S(1)} collective-permute-done((s16[3,528,256]{2,1,0:T(8,128)(2,1)S(1)}, s16[3,528,256]{2,1,0:T(8,128)(2,1)S(1)}, u32[]{:S(2)}, u32[]{:S(2)}) %collective-permute-start.36) | collective-permute-done | bytes 811040 | tf_op jit(solution)/shard_map/ppermute | solution.py:323
  114.5 2.4 %collective-permute-start.19 = (bf16[4,16,2048]{2,1,0:T(8,128)(2,1)S(1)}, bf16[4,16,2048]{2,1,0:T(8,128)(2,1)S(1)}, u32[]{:S(2)}, u32[]{:S(2)}) collective-permute-start(bf16[4,16,2048]{2,1,0:T(8,128)(2,1)S(1)} %pad_maximum_fusion.refs_0_), channel_id=1, source_target_pairs={{0,24},{4,28},{8,0},{12,4},{16,8},{20,12},{24,16},{28,20},{32,56},... | collective-permute-start | bytes 786440 | tf_op jit(solution)/shard_map/ppermute | solution.py:36
  117.5 34.0 %collective-permute-done.37.refs_2_ = s16[3,528,256]{2,1,0:T(8,128)(2,1)S(1)} collective-permute-done((s16[3,528,256]{2,1,0:T(8,128)(2,1)}, s16[3,528,256]{2,1,0:T(8,128)(2,1)S(1)}, u32[]{:S(2)}, u32[]{:S(2)}) %collective-permute-start.37) | collective-permute-done | bytes 811040 | tf_op jit(solution)/shard_map/ppermute | solution.py:323
  152.0 2.3 %collective-permute-start.26 = (bf16[4,16,2048]{2,1,0:T(8,128)(2,1)S(1)}, bf16[4,16,2048]{2,1,0:T(8,128)(2,1)S(1)}, u32[]{:S(2)}, u32[]{:S(2)}) collective-permute-start(bf16[4,16,2048]{2,1,0:T(8,128)(2,1)S(1)} %constant_dynamic-update-slice_fusion.refs_4_), channel_id=1, source_target_pairs={{0,96},{4,100},{8,104},{12,108},{16,112},{20,116},{24,120},{28,124... | collective-permute-start | bytes 786440 | tf_op jit(solution)/shard_map/ppermute | solution.py:36
  155.7 9.8 %collective-permute-done.26.refs_7_ = bf16[4,16,2048]{2,1,0:T(8,128)(2,1)S(1)} collective-permute-done((bf16[4,16,2048]{2,1,0:T(8,128)(2,1)S(1)}, bf16[4,16,2048]{2,1,0:T(8,128)(2,1)S(1)}, u32[]{:S(2)}, u32[]{:S(2)}) %collective-permute-start.26) | collective-permute-done | bytes 262176 | tf_op jit(solution)/shard_map/ppermute | solution.py:36
  166.5 2.8 %collective-permute-done.24.refs_5_ = bf16[4,16,2048]{2,1,0:T(8,128)(2,1)S(1)} collective-permute-done((bf16[4,16,2048]{2,1,0:T(8,128)(2,1)S(1)}, bf16[4,16,2048]{2,1,0:T(8,128)(2,1)S(1)}, u32[]{:S(2)}, u32[]{:S(2)}) %collective-permute-start.24) | collective-permute-done | bytes 262176 | tf_op jit(solution)/shard_map/ppermute | solution.py:36
  170.0 1.4 copy-done
  171.4 1.6 shard_map.122
  173.0 2.5 %shard_map.120 = bf16[64,16,2048]{2,1,0:T(8,128)(2,1)} custom-call(s32[64]{0:T(128)S(1)} %copy-done.1, s32[1]{0:T(128)} %bitcast.me_ref, bf16[4,16,2048]{2,1,0:T(8,128)(2,1)S(1)} %pad_maximum_fusion.refs_0_, bf16[4,16,2048]{2,1,0:T(8,128)(2,1)S(1)} %collective-permute-done.17.refs_1_, bf16[4,16,2048]{2,1,0:T(8,128)(2,1)S(1)} %collective-permute-done.18.refs_2_, ...), custom_call_target="tpu_custom_call" | custom-call | tf_op jit(solution)/shard_map/pallas_call | solution.py:299
  (74 shorter events, 10.7 us)
Async XLA Ops:
  18.6 7.5 %collective-permute-start = (bf16[32,16,2176]{2,1,0:T(8,128)(2,1)}, bf16[32,16,2176]{2,1,0:T(8,128)(2,1)S(1)}, u32[]{:S(2)}, u32[]{:S(2)}) collective-permute-start(bf16[32,16,2176]{2,1,0:T(8,128)(2,1)} %get-tuple-element.26), channel_id=1, source_target_pairs={{0,4},{4,0},{8,12},{12,8},{16,20},{20,16},{24,28},{28,24},{32,36},... | collective-permute-start | bytes 6684680 | tf_op jit(solution)/shard_map/ppermute | solution.py:36
  28.3 7.9 %collective-permute-start.6 = (bf16[4,16,2176]{2,1,0:T(8,128)(2,1)S(1)}, bf16[4,16,2176]{2,1,0:T(8,128)(2,1)S(1)}, u32[]{:S(2)}, u32[]{:S(2)}) collective-permute-start(bf16[4,16,2176]{2,1,0:T(8,128)(2,1)S(1)} %get-tuple-element.50), channel_id=1, source_target_pairs={{0,24},{4,28},{8,0},{12,4},{16,8},{20,12},{24,16},{28,20},{32,56},... | collective-permute-start | bytes 835592 | tf_op jit(solution)/shard_map/ppermute | solution.py:36
  29.4 14.2 %collective-permute-start.5 = (bf16[4,16,2176]{2,1,0:T(8,128)(2,1)S(1)}, bf16[4,16,2176]{2,1,0:T(8,128)(2,1)S(1)}, u32[]{:S(2)}, u32[]{:S(2)}) collective-permute-start(bf16[4,16,2176]{2,1,0:T(8,128)(2,1)S(1)} %get-tuple-element.51), channel_id=1, source_target_pairs={{0,8},{4,12},{8,16},{12,20},{16,24},{20,28},{24,0},{28,4},{32,40},... | collective-permute-start | bytes 835592 | tf_op jit(solution)/shard_map/ppermute | solution.py:36
  29.8 13.8 %collective-permute-start.4 = (bf16[4,16,2176]{2,1,0:T(8,128)(2,1)S(1)}, bf16[4,16,2176]{2,1,0:T(8,128)(2,1)S(1)}, u32[]{:S(2)}, u32[]{:S(2)}) collective-permute-start(bf16[4,16,2176]{2,1,0:T(8,128)(2,1)S(1)} %get-tuple-element.52), channel_id=1, source_target_pairs={{0,16},{4,20},{8,24},{12,28},{16,0},{20,4},{24,8},{28,12},{32,48},... | collective-permute-start | bytes 835592 | tf_op jit(solution)/shard_map/ppermute | solution.py:36
  31.1 12.6 %collective-permute-start.3 = (bf16[4,16,2176]{2,1,0:T(8,128)(2,1)S(1)}, bf16[4,16,2176]{2,1,0:T(8,128)(2,1)S(1)}, u32[]{:S(2)}, u32[]{:S(2)}) collective-permute-start(bf16[4,16,2176]{2,1,0:T(8,128)(2,1)S(1)} %get-tuple-element.53), channel_id=1, source_target_pairs={{0,96},{4,100},{8,104},{12,108},{16,112},{20,116},{24,120},{28,124... | collective-permute-start | bytes 835592 | tf_op jit(solution)/shard_map/ppermute | solution.py:36
  33.5 10.1 %collective-permute-start.2 = (bf16[4,16,2176]{2,1,0:T(8,128)(2,1)S(1)}, bf16[4,16,2176]{2,1,0:T(8,128)(2,1)S(1)}, u32[]{:S(2)}, u32[]{:S(2)}) collective-permute-start(bf16[4,16,2176]{2,1,0:T(8,128)(2,1)S(1)} %get-tuple-element.54), channel_id=1, source_target_pairs={{0,32},{4,36},{8,40},{12,44},{16,48},{20,52},{24,56},{28,60},{32,6... | collective-permute-start | bytes 835592 | tf_op jit(solution)/shard_map/ppermute | solution.py:36
  36.2 13.1 %collective-permute-start.1 = (bf16[4,16,2176]{2,1,0:T(8,128)(2,1)S(1)}, bf16[4,16,2176]{2,1,0:T(8,128)(2,1)S(1)}, u32[]{:S(2)}, u32[]{:S(2)}) collective-permute-start(bf16[4,16,2176]{2,1,0:T(8,128)(2,1)S(1)} %get-tuple-element.55), channel_id=1, source_target_pairs={{0,64},{4,68},{8,72},{12,76},{16,80},{20,84},{24,88},{28,92},{32,9... | collective-permute-start | bytes 835592 | tf_op jit(solution)/shard_map/ppermute | solution.py:36
  51.9 5.1 %collective-permute-start.11 = (bf16[16,2176]{1,0:T(8,128)(2,1)S(1)}, bf16[16,2176]{1,0:T(8,128)(2,1)S(1)}, u32[]{:S(2)}, u32[]{:S(2)}) collective-permute-start(bf16[16,2176]{1,0:T(8,128)(2,1)S(1)} %get-tuple-element.60), channel_id=1, source_target_pairs={{0,32},{4,36},{8,40},{12,44},{16,48},{20,52},{24,56},{28,60},{32,6... | collective-permute-start | bytes 208904 | tf_op jit(solution)/shard_map/ppermute | solution.py:36
  51.9 5.1 %collective-permute-start.10 = (bf16[16,2176]{1,0:T(8,128)(2,1)S(1)}, bf16[16,2176]{1,0:T(8,128)(2,1)S(1)}, u32[]{:S(2)}, u32[]{:S(2)}) collective-permute-start(bf16[16,2176]{1,0:T(8,128)(2,1)S(1)} %get-tuple-element.61), channel_id=1, source_target_pairs={{0,64},{4,68},{8,72},{12,76},{16,80},{20,84},{24,88},{28,92},{32,9... | collective-permute-start | bytes 208904 | tf_op jit(solution)/shard_map/ppermute | solution.py:36
  57.1 16.0 %collective-permute-start.13 = (f32[16,2176]{1,0:T(8,128)S(1)}, f32[16,2176]{1,0:T(8,128)S(1)}, u32[]{:S(2)}, u32[]{:S(2)}) collective-permute-start(f32[16,2176]{1,0:T(8,128)S(1)} %fusion.1), channel_id=1, source_target_pairs={{0,128},{4,132},{8,136},{12,140},{16,144},{20,148},{24,152},{28,15... | collective-permute-start | bytes 417800 | tf_op jit(solution)/shard_map/ppermute | solution.py:36
  64.2 5.1 %collective-permute-start.9 = (bf16[16,2176]{1,0:T(8,128)(2,1)S(1)}, bf16[16,2176]{1,0:T(8,128)(2,1)S(1)}, u32[]{:S(2)}, u32[]{:S(2)}) collective-permute-start(bf16[16,2176]{1,0:T(8,128)(2,1)S(1)} %get-tuple-element.56), channel_id=1, source_target_pairs={{0,24},{4,28},{8,0},{12,4},{16,8},{20,12},{24,16},{28,20},{32,56},... | collective-permute-start | bytes 208904 | tf_op jit(solution)/shard_map/ppermute | solution.py:36
  68.0 5.1 %collective-permute-start.8 = (bf16[16,2176]{1,0:T(8,128)(2,1)S(1)}, bf16[16,2176]{1,0:T(8,128)(2,1)S(1)}, u32[]{:S(2)}, u32[]{:S(2)}) collective-permute-start(bf16[16,2176]{1,0:T(8,128)(2,1)S(1)} %get-tuple-element.57), channel_id=1, source_target_pairs={{0,8},{4,12},{8,16},{12,20},{16,24},{20,28},{24,0},{28,4},{32,40},... | collective-permute-start | bytes 208904 | tf_op jit(solution)/shard_map/ppermute | solution.py:36
  75.3 7.1 %collective-permute-start.20 = (bf16[1,16,2048]{2,1,0:T(8,128)(2,1)S(1)}, bf16[1,16,2048]{2,1,0:T(8,128)(2,1)S(1)}, u32[]{:S(2)}, u32[]{:S(2)}) collective-permute-start(bf16[1,16,2048]{2,1,0:T(8,128)(2,1)S(1)} %get-tuple-element.45), channel_id=1, source_target_pairs={{0,128},{4,132},{8,136},{12,140},{16,144},{20,148},{24,152},{28,15... | collective-permute-start | bytes 196616 | tf_op jit(solution)/shard_map/ppermute | solution.py:36
  75.3 23.7 %collective-permute-start.35 = (s16[3,528,256]{2,1,0:T(8,128)(2,1)S(1)}, s16[3,528,256]{2,1,0:T(8,128)(2,1)S(1)}, u32[]{:S(2)}, u32[]{:S(2)}) collective-permute-start(s16[3,528,256]{2,1,0:T(8,128)(2,1)S(1)} %copy-done.6), channel_id=1, source_target_pairs={{0,1},{1,2},{2,3},{3,0},{4,5},{5,6},{6,7},{7,4},{8,9},{9,10},{10,1... | collective-permute-start | bytes 2433032 | tf_op jit(solution)/shard_map/ppermute | solution.py:323
  76.3 38.2 %collective-permute-start.36 = (s16[3,528,256]{2,1,0:T(8,128)(2,1)S(1)}, s16[3,528,256]{2,1,0:T(8,128)(2,1)S(1)}, u32[]{:S(2)}, u32[]{:S(2)}) collective-permute-start(s16[3,528,256]{2,1,0:T(8,128)(2,1)S(1)} %copy-done.5), channel_id=1, source_target_pairs={{0,3},{1,0},{2,1},{3,2},{4,7},{5,4},{6,5},{7,6},{8,11},{9,8},{10,9... | collective-permute-start | bytes 2433032 | tf_op jit(solution)/shard_map/ppermute | solution.py:323
  78.5 11.5 %collective-permute-start.16 = (bf16[1,16,2048]{2,1,0:T(8,128)(2,1)S(1)}, bf16[1,16,2048]{2,1,0:T(8,128)(2,1)S(1)}, u32[]{:S(2)}, u32[]{:S(2)}) collective-permute-start(bf16[1,16,2048]{2,1,0:T(8,128)(2,1)S(1)} %get-tuple-element.45), channel_id=1, source_target_pairs={{0,96},{4,100},{8,104},{12,108},{16,112},{20,116},{24,120},{28,124... | collective-permute-start | bytes 196616 | tf_op jit(solution)/shard_map/ppermute | solution.py:36
  80.9 10.5 %collective-permute-start.15 = (bf16[1,16,2048]{2,1,0:T(8,128)(2,1)S(1)}, bf16[1,16,2048]{2,1,0:T(8,128)(2,1)S(1)}, u32[]{:S(2)}, u32[]{:S(2)}) collective-permute-start(bf16[1,16,2048]{2,1,0:T(8,128)(2,1)S(1)} %get-tuple-element.45), channel_id=1, source_target_pairs={{0,64},{4,68},{8,72},{12,76},{16,80},{20,84},{24,88},{28,92},{32,9... | collective-permute-start | bytes 196616 | tf_op jit(solution)/shard_map/ppermute | solution.py:36
  82.4 12.0 %collective-permute-start.14 = (bf16[1,16,2048]{2,1,0:T(8,128)(2,1)S(1)}, bf16[1,16,2048]{2,1,0:T(8,128)(2,1)S(1)}, u32[]{:S(2)}, u32[]{:S(2)}) collective-permute-start(bf16[1,16,2048]{2,1,0:T(8,128)(2,1)S(1)} %get-tuple-element.45), channel_id=1, source_target_pairs={{0,32},{4,36},{8,40},{12,44},{16,48},{20,52},{24,56},{28,60},{32,6... | collective-permute-start | bytes 196616 | tf_op jit(solution)/shard_map/ppermute | solution.py:36
  90.1 61.4 %collective-permute-start.37 = (s16[3,528,256]{2,1,0:T(8,128)(2,1)}, s16[3,528,256]{2,1,0:T(8,128)(2,1)S(1)}, u32[]{:S(2)}, u32[]{:S(2)}) collective-permute-start(s16[3,528,256]{2,1,0:T(8,128)(2,1)} %get-tuple-element.44), channel_id=1, source_target_pairs={{0,2},{1,3},{2,0},{3,1},{4,6},{5,7},{6,4},{7,5},{8,10},{9,11},{10,... | collective-permute-start | bytes 2433032 | tf_op jit(solution)/shard_map/ppermute | solution.py:323
  91.3 25.6 %collective-permute-start.23 = (bf16[1,16,2048]{2,1,0:T(8,128)(2,1)S(1)}, bf16[1,16,2048]{2,1,0:T(8,128)(2,1)S(1)}, u32[]{:S(2)}, u32[]{:S(2)}) collective-permute-start(bf16[1,16,2048]{2,1,0:T(8,128)(2,1)S(1)} %collective-permute-done.20), channel_id=1, source_target_pairs={{0,24},{4,28},{8,0},{12,4},{16,8},{20,12},{24,16},{28,20},{32,56},... | collective-permute-start | bytes 196616 | tf_op jit(solution)/shard_map/ppermute | solution.py:36
  99.0 17.9 %collective-permute-start.22 = (bf16[1,16,2048]{2,1,0:T(8,128)(2,1)S(1)}, bf16[1,16,2048]{2,1,0:T(8,128)(2,1)S(1)}, u32[]{:S(2)}, u32[]{:S(2)}) collective-permute-start(bf16[1,16,2048]{2,1,0:T(8,128)(2,1)S(1)} %collective-permute-done.20), channel_id=1, source_target_pairs={{0,16},{4,20},{8,24},{12,28},{16,0},{20,4},{24,8},{28,12},{32,48},... | collective-permute-start | bytes 196616 | tf_op jit(solution)/shard_map/ppermute | solution.py:36
  99.0 53.0 %collective-permute-start.27 = (bf16[4,16,2048]{2,1,0:T(8,128)(2,1)S(1)}, bf16[4,16,2048]{2,1,0:T(8,128)(2,1)S(1)}, u32[]{:S(2)}, u32[]{:S(2)}) collective-permute-start(bf16[4,16,2048]{2,1,0:T(8,128)(2,1)S(1)} %pad_maximum_fusion.refs_0_), channel_id=1, source_target_pairs={{0,4},{4,0},{8,12},{12,8},{16,20},{20,16},{24,28},{28,24},{32,36},... | collective-permute-start | bytes 786440 | tf_op jit(solution)/shard_map/ppermute | solution.py:36
  114.5 39.9 %collective-permute-start.19 = (bf16[4,16,2048]{2,1,0:T(8,128)(2,1)S(1)}, bf16[4,16,2048]{2,1,0:T(8,128)(2,1)S(1)}, u32[]{:S(2)}, u32[]{:S(2)}) collective-permute-start(bf16[4,16,2048]{2,1,0:T(8,128)(2,1)S(1)} %pad_maximum_fusion.refs_0_), channel_id=1, source_target_pairs={{0,24},{4,28},{8,0},{12,4},{16,8},{20,12},{24,16},{28,20},{32,56},... | collective-permute-start | bytes 786440 | tf_op jit(solution)/shard_map/ppermute | solution.py:36
  116.9 37.5 %collective-permute-start.18 = (bf16[4,16,2048]{2,1,0:T(8,128)(2,1)S(1)}, bf16[4,16,2048]{2,1,0:T(8,128)(2,1)S(1)}, u32[]{:S(2)}, u32[]{:S(2)}) collective-permute-start(bf16[4,16,2048]{2,1,0:T(8,128)(2,1)S(1)} %pad_maximum_fusion.refs_0_), channel_id=1, source_target_pairs={{0,16},{4,20},{8,24},{12,28},{16,0},{20,4},{24,8},{28,12},{32,48},... | collective-permute-start | bytes 786440 | tf_op jit(solution)/shard_map/ppermute | solution.py:36
  116.9 38.1 %collective-permute-start.17 = (bf16[4,16,2048]{2,1,0:T(8,128)(2,1)S(1)}, bf16[4,16,2048]{2,1,0:T(8,128)(2,1)S(1)}, u32[]{:S(2)}, u32[]{:S(2)}) collective-permute-start(bf16[4,16,2048]{2,1,0:T(8,128)(2,1)S(1)} %pad_maximum_fusion.refs_0_), channel_id=1, source_target_pairs={{0,8},{4,12},{8,16},{12,20},{16,24},{20,28},{24,0},{28,4},{32,40},... | collective-permute-start | bytes 786440 | tf_op jit(solution)/shard_map/ppermute | solution.py:36
  152.0 13.5 %collective-permute-start.26 = (bf16[4,16,2048]{2,1,0:T(8,128)(2,1)S(1)}, bf16[4,16,2048]{2,1,0:T(8,128)(2,1)S(1)}, u32[]{:S(2)}, u32[]{:S(2)}) collective-permute-start(bf16[4,16,2048]{2,1,0:T(8,128)(2,1)S(1)} %constant_dynamic-update-slice_fusion.refs_4_), channel_id=1, source_target_pairs={{0,96},{4,100},{8,104},{12,108},{16,112},{20,116},{24,120},{28,124... | collective-permute-start | bytes 786440 | tf_op jit(solution)/shard_map/ppermute | solution.py:36
  154.4 12.2 %collective-permute-start.25 = (bf16[4,16,2048]{2,1,0:T(8,128)(2,1)S(1)}, bf16[4,16,2048]{2,1,0:T(8,128)(2,1)S(1)}, u32[]{:S(2)}, u32[]{:S(2)}) collective-permute-start(bf16[4,16,2048]{2,1,0:T(8,128)(2,1)S(1)} %constant_dynamic-update-slice_fusion.refs_4_), channel_id=1, source_target_pairs={{0,64},{4,68},{8,72},{12,76},{16,80},{20,84},{24,88},{28,92},{32,9... | collective-permute-start | bytes 786440 | tf_op jit(solution)/shard_map/ppermute | solution.py:36
  154.4 14.9 %collective-permute-start.24 = (bf16[4,16,2048]{2,1,0:T(8,128)(2,1)S(1)}, bf16[4,16,2048]{2,1,0:T(8,128)(2,1)S(1)}, u32[]{:S(2)}, u32[]{:S(2)}) collective-permute-start(bf16[4,16,2048]{2,1,0:T(8,128)(2,1)S(1)} %constant_dynamic-update-slice_fusion.refs_4_), channel_id=1, source_target_pairs={{0,32},{4,36},{8,40},{12,44},{16,48},{20,52},{24,56},{28,60},{32,6... | collective-permute-start | bytes 786440 | tf_op jit(solution)/shard_map/ppermute | solution.py:36
  155.0 15.0 %collective-permute-start.30 = (bf16[4,16,2048]{2,1,0:T(8,128)(2,1)S(1)}, bf16[4,16,2048]{2,1,0:T(8,128)(2,1)S(1)}, u32[]{:S(2)}, u32[]{:S(2)}) collective-permute-start(bf16[4,16,2048]{2,1,0:T(8,128)(2,1)S(1)} %collective-permute-done.19.refs_3_), channel_id=1, source_target_pairs={{0,4},{4,0},{8,12},{12,8},{16,20},{20,16},{24,28},{28,24},{32,36},... | collective-permute-start | bytes 786440 | tf_op jit(solution)/shard_map/ppermute | solution.py:36
  155.6 17.4 %collective-permute-start.29 = (bf16[4,16,2048]{2,1,0:T(8,128)(2,1)S(1)}, bf16[4,16,2048]{2,1,0:T(8,128)(2,1)S(1)}, u32[]{:S(2)}, u32[]{:S(2)}) collective-permute-start(bf16[4,16,2048]{2,1,0:T(8,128)(2,1)S(1)} %collective-permute-done.18.refs_2_), channel_id=1, source_target_pairs={{0,4},{4,0},{8,12},{12,8},{16,20},{20,16},{24,28},{28,24},{32,36},... | collective-permute-start | bytes 786440 | tf_op jit(solution)/shard_map/ppermute | solution.py:36
  165.5 7.5 %collective-permute-start.28 = (bf16[4,16,2048]{2,1,0:T(8,128)(2,1)S(1)}, bf16[4,16,2048]{2,1,0:T(8,128)(2,1)S(1)}, u32[]{:S(2)}, u32[]{:S(2)}) collective-permute-start(bf16[4,16,2048]{2,1,0:T(8,128)(2,1)S(1)} %collective-permute-done.17.refs_1_), channel_id=1, source_target_pairs={{0,4},{4,0},{8,12},{12,8},{16,20},{20,16},{24,28},{28,24},{32,36},... | collective-permute-start | bytes 786440 | tf_op jit(solution)/shard_map/ppermute | solution.py:36
  166.5 6.5 %collective-permute-start.34 = (bf16[4,16,2048]{2,1,0:T(8,128)(2,1)S(1)}, bf16[4,16,2048]{2,1,0:T(8,128)(2,1)S(1)}, u32[]{:S(2)}, u32[]{:S(2)}) collective-permute-start(bf16[4,16,2048]{2,1,0:T(8,128)(2,1)S(1)} %collective-permute-done.26.refs_7_), channel_id=1, source_target_pairs={{0,4},{4,0},{8,12},{12,8},{16,20},{20,16},{24,28},{28,24},{32,36},... | collective-permute-start | bytes 786440 | tf_op jit(solution)/shard_map/ppermute | solution.py:36
  (13 other events, 259.5 us)

commit v6 on v5

--- a/solution.py
+++ b/solution.py
@@ -194,48 +194,59 @@
     )(count, owner_map, me, mine, acts, grads, weight, weight)
 
 
-def input_shares(grads, weight, count, mine, ways, offsets, interpret=False):
+def far_shares(grads, weight, count, mine, ways, interpret=False):
     tokens, columns = grads.shape
     hidden = weight.shape[0]
     width = hidden // ways
-    tall = TALL
-    extra = tall // GROUP
-
-    def kernel(count_ref, mine_ref, grads_ref, *refs):
+    extra = TALL // GROUP
+    steps = tokens // TALL
+
+    def kernel(count_ref, mine_ref, grads_ref, far_ref, near_ref, first_out, rest_out, own_out):
         step = pl.program_id(0)
-        live = lax.broadcasted_iota(jnp.int32, (tall, width), 0) + step * tall < count_ref[0]
-        for offset, part, out in zip(offsets, refs[: len(offsets)], refs[len(offsets) :]):
+        live = lax.broadcasted_iota(jnp.int32, (TALL, width), 0) + step * TALL < count_ref[0]
+
+        def share_of(part):
             share = lax.dot_general(
                 grads_ref[...], part[...], (((1,), (1,)), ((), ())), preferred_element_type=f32
             )
-            share = jnp.where(live, share, 0.0)
-            if offset == 0:
-                out[...] = share
-                continue
-            encode(share, out, 0)
+            return jnp.where(live, share, 0.0)
+
+        @pl.when(step == 0)
+        def _():
+            encode(share_of(far_ref), first_out, 0)
+
+        @pl.when(step > 0)
+        def _():
+            encode(share_of(far_ref), rest_out, 0)
+
+        own_out[...] = share_of(near_ref)
 
     def part_of(offset):
         return pl.BlockSpec(
             (width, columns), lambda n, count, mine: (lax.rem(mine[0] + offset, ways), 0)
         )
 
-    own = jax.ShapeDtypeStruct((tokens, width), f32)
-    code = jax.ShapeDtypeStruct((tokens // tall, tall + extra, width), i16)
-    own_spec = pl.BlockSpec((tall, width), lambda n, *_: (n, 0))
-    code_spec = pl.BlockSpec((1, tall + extra, width), lambda n, *_: (n, 0, 0))
+    block = (1, TALL + extra, width)
     return pl.pallas_call(
         kernel,
         grid_spec=pltpu.PrefetchScalarGridSpec(
             num_scalar_prefetch=2,
-            grid=(tokens // tall,),
-            in_specs=[pl.BlockSpec((tall, columns), lambda n, *_: (n, 0))]
-            + [part_of(offset) for offset in offsets],
-            out_specs=[own_spec if offset == 0 else code_spec for offset in offsets],
+            grid=(steps,),
+            in_specs=[pl.BlockSpec((TALL, columns), lambda n, *_: (n, 0)), part_of(2), part_of(0)],
+            out_specs=[
+                pl.BlockSpec(block, lambda n, *_: (0, 0, 0)),
+                pl.BlockSpec(block, lambda n, *_: (jnp.maximum(n - 1, 0), 0, 0)),
+                pl.BlockSpec((TALL, width), lambda n, *_: (n, 0)),
+            ],
         ),
-        out_shape=[own if offset == 0 else code for offset in offsets],
+        out_shape=[
+            jax.ShapeDtypeStruct(block, i16),
+            jax.ShapeDtypeStruct((steps - 1, *block[1:]), i16),
+            jax.ShapeDtypeStruct((tokens, width), f32),
+        ],
         compiler_params=pltpu.CompilerParams(vmem_limit_bytes=60 * 2**20),
         interpret=interpret,
-    )(count, mine, grads, *[weight] * len(offsets))
+    )(count, mine, grads, weight, weight)
 
 
 def add_shares(own, shares, interpret=False):
@@ -337,7 +348,10 @@
         for colour, (first, _) in enumerate(rings)
     ]
     got = lax.optimization_barrier(got)
-    across, own = input_shares(far_grads, down_weight, token_counts, my_mp, ways, (2, 0))
+    across_first, across_rest, own = far_shares(
+        far_grads, down_weight, token_counts, my_mp, ways
+    )
+    across_early = pass_share(across_first, 2)
     lines = [
         [
             sum((g[e].astype(f32) for g in got[colour]), pair[4 * colour][e].astype(f32)).astype(bf16)
@@ -364,7 +378,7 @@
 
     weights = master_new.astype(bf16)[None]
     other = to_zh(weights)
-    shares.append([pass_share(across, 2)])
+    shares.append([across_early, pass_share(across_rest, 2)])
     lines = []
     for part, (first, _) in zip((weights, other), rings):
         two, one, three = [shift(part, first, d) for d in (2, 1, 3)]
@@ -374,8 +388,9 @@
         two, one, three = [shift(line, second, d) for d in (2, 1, 3)]
         pieces += [line, one, two, three]
     pieces += [to_core(piece) for piece in pieces]
+    weights_new = place_blocks(pieces, owner_map, me).reshape(hidden, columns)
+    weights_new, own = lax.optimization_barrier((weights_new, own))
     input_grads = add_shares(own, shares)
-    weights_new = place_blocks(pieces, owner_map, me).reshape(hidden, columns)
     return (master_new, moment1_new, moment2_new, weights_new, input_grads)
 
 

time: 176 us -> 196 us (1.11)
  waiting for transfers between devices: 79.5 us -> 94 us
  starting transfers between devices: 59.6 us -> 64 us
    ppermute x35, waiting for transfers between devices: 38.4 us -> 54 us  [move(): return lax.ppermute(value, 'dp', pairs)]
    ppermute x35, starting transfers between devices: 55 us -> 58.3 us  [move(): return lax.ppermute(value, 'dp', pairs)]
    ppermute x3 -> x4, starting transfers between devices: 4.54 us -> 5.63 us  [pass_share(): return lax.ppermute(coded, 'mp', ring)]
    ppermute x3 -> x4, waiting for transfers between devices: 41.1 us -> 40 us  [pass_share(): return lax.ppermute(coded, 'mp', ring)]
  transfers between devices with their start and end apart: 38 -> 39, of which waited for: 12 -> 19; matrix products, arithmetic and copies ran while one was open for 0% -> 0% of each run, Pallas kernels for 5% -> 6%
where the time goes in v6:
time: 196 us
  waiting for transfers between devices  94 us (48%)
  starting transfers between devices  64 us (33%)
  Pallas kernels  30.2 us (15%)
  other arithmetic  4.6 us (2%)
    ppermute x35, starting transfers between devices, move(): return lax.ppermute(value, 'dp', pairs)  58.3 us
    ppermute x35, waiting for transfers between devices, move(): return lax.ppermute(value, 'dp', pairs)  54 us
    ppermute x4, waiting for transfers between devices, pass_share(): return lax.ppermute(coded, 'mp', ring)  40 us
    pallas_call x1, Pallas kernels, weight_partials(): pl.pallas_call(kernel, grid_spec=pltpu.PrefetchScalarGridSpec(num_scalar_...  17.4 us
    pallas_call x1, Pallas kernels, far_shares(): pl.pallas_call(kernel, grid_spec=pltpu.PrefetchScalarGridSpec(num_scalar_...  8.08 us
    ppermute x4, starting transfers between devices, pass_share(): return lax.ppermute(coded, 'mp', ring)  5.63 us
  transfers between devices with their start and end apart: 39, of which 19 were waited for; matrix products, arithmetic and copies ran while one was open for 0% of the time, Pallas kernels for 6%

profile of v6, /device:TPU:1, one launch (start us, length us, event | category | flops | bytes accessed | tf_op | source)
XLA Modules:
  0.0 195.8 jit_solution(9734276704740942855)
XLA Ops:
  1.3 17.4 %shard_map.119 = (bf16[32,16,2176]{2,1,0:T(8,128)(2,1)}, bf16[32,16,2176]{2,1,0:T(8,128)(2,1)}, s16[3,528,256]{2,1,0:T(8,128)(2,1)}, s16[3,528,256]{2,1,0:T(8,128)(2,1)}) custom-call(s32[1]{0:T(128)S(6)} %copy.16.count_ref, s32[64]{0:T(128)} %map_ref.3, s32[1]{0:T(128)} %bitcast.me_ref, s32[1]{0:T(128)} %bitcast.1.mine_ref, bf16[1536,1024]{1,0:T(8,128)(2,1)} %acts_ref.1, ...), custom_call_target="tpu_custom_call" | custom-call | tf_op jit(solution)/shard_map/pallas_call | solution.py:170
  18.7 3.3 %collective-permute-start = (bf16[32,16,2176]{2,1,0:T(8,128)(2,1)}, bf16[32,16,2176]{2,1,0:T(8,128)(2,1)S(1)}, u32[]{:S(2)}, u32[]{:S(2)}) collective-permute-start(bf16[32,16,2176]{2,1,0:T(8,128)(2,1)} %get-tuple-element.29), channel_id=1, source_target_pairs={{0,4},{4,0},{8,12},{12,8},{16,20},{20,16},{24,28},{28,24},{32,36},... | collective-permute-start | bytes 6684680 | tf_op jit(solution)/shard_map/ppermute | solution.py:36
  22.0 4.2 %collective-permute-done = bf16[32,16,2176]{2,1,0:T(8,128)(2,1)S(1)} collective-permute-done((bf16[32,16,2176]{2,1,0:T(8,128)(2,1)}, bf16[32,16,2176]{2,1,0:T(8,128)(2,1)S(1)}, u32[]{:S(2)}, u32[]{:S(2)}) %collective-permute-start) | collective-permute-done | bytes 2228256 | tf_op jit(solution)/shard_map/ppermute | solution.py:36
  26.1 2.1 %add_convert_fusion.7 = (bf16[4,16,2176]{2,1,0:T(8,128)(2,1)S(1)}, bf16[4,16,2176]{2,1,0:T(8,128)(2,1)S(1)}, bf16[4,16,2176]{2,1,0:T(8,128)(2,1)S(1)}, bf16[4,16...) fusion(bf16[32,16,2176]{2,1,0:T(8,128)(2,1)S(1)} %collective-pe, ...), kind=kLoop, calls=%fused_computation.7 | loop fusion | flops 4456448 | bytes 6684672 | tf_op jit(solution)/shard_map/convert_element_type | solution.py:343
  31.1 2.5 %collective-permute-start.3 = (bf16[4,16,2176]{2,1,0:T(8,128)(2,1)S(1)}, bf16[4,16,2176]{2,1,0:T(8,128)(2,1)S(1)}, u32[]{:S(2)}, u32[]{:S(2)}) collective-permute-start(bf16[4,16,2176]{2,1,0:T(8,128)(2,1)S(1)} %get-tuple-element.59), channel_id=1, source_target_pairs={{0,96},{4,100},{8,104},{12,108},{16,112},{20,116},{24,120},{28,124... | collective-permute-start | bytes 835592 | tf_op jit(solution)/shard_map/ppermute | solution.py:36
  33.5 2.7 %collective-permute-done.6 = bf16[4,16,2176]{2,1,0:T(8,128)(2,1)S(1)} collective-permute-done((bf16[4,16,2176]{2,1,0:T(8,128)(2,1)S(1)}, bf16[4,16,2176]{2,1,0:T(8,128)(2,1)S(1)}, u32[]{:S(2)}, u32[]{:S(2)}) %collective-permute-start.6) | collective-permute-done | bytes 278560 | tf_op jit(solution)/shard_map/ppermute | solution.py:36
  36.2 7.4 %collective-permute-start.1 = (bf16[4,16,2176]{2,1,0:T(8,128)(2,1)S(1)}, bf16[4,16,2176]{2,1,0:T(8,128)(2,1)S(1)}, u32[]{:S(2)}, u32[]{:S(2)}) collective-permute-start(bf16[4,16,2176]{2,1,0:T(8,128)(2,1)S(1)} %get-tuple-element.61), channel_id=1, source_target_pairs={{0,64},{4,68},{8,72},{12,76},{16,80},{20,84},{24,88},{28,92},{32,9... | collective-permute-start | bytes 835592 | tf_op jit(solution)/shard_map/ppermute | solution.py:36
  43.7 5.6 %collective-permute-done.1 = bf16[4,16,2176]{2,1,0:T(8,128)(2,1)S(1)} collective-permute-done((bf16[4,16,2176]{2,1,0:T(8,128)(2,1)S(1)}, bf16[4,16,2176]{2,1,0:T(8,128)(2,1)S(1)}, u32[]{:S(2)}, u32[]{:S(2)}) %collective-permute-start.1) | collective-permute-done | bytes 278560 | tf_op jit(solution)/shard_map/ppermute | solution.py:36
  49.4 2.5 %collective-permute-start.12 = (bf16[16,2176]{1,0:T(8,128)(2,1)S(1)}, bf16[16,2176]{1,0:T(8,128)(2,1)S(1)}, u32[]{:S(2)}, u32[]{:S(2)}) collective-permute-start(bf16[16,2176]{1,0:T(8,128)(2,1)S(1)} %get-tuple-element.65), channel_id=1, source_target_pairs={{0,96},{4,100},{8,104},{12,108},{16,112},{20,116},{24,120},{28,124... | collective-permute-start | bytes 208904 | tf_op jit(solution)/shard_map/ppermute | solution.py:36
  51.9 1.7 collective-permute-start.10
  53.6 3.4 %collective-permute-done.11 = bf16[16,2176]{1,0:T(8,128)(2,1)S(1)} collective-permute-done((bf16[16,2176]{1,0:T(8,128)(2,1)S(1)}, bf16[16,2176]{1,0:T(8,128)(2,1)S(1)}, u32[]{:S(2)}, u32[]{:S(2)}) %collective-permute-start.11) | collective-permute-done | bytes 69664 | tf_op jit(solution)/shard_map/ppermute | solution.py:36
  57.1 7.0 %collective-permute-start.13 = (f32[16,2176]{1,0:T(8,128)S(1)}, f32[16,2176]{1,0:T(8,128)S(1)}, u32[]{:S(2)}, u32[]{:S(2)}) collective-permute-start(f32[16,2176]{1,0:T(8,128)S(1)} %fusion.1), channel_id=1, source_target_pairs={{0,128},{4,132},{8,136},{12,140},{16,144},{20,148},{24,152},{28,15... | collective-permute-start | bytes 417800 | tf_op jit(solution)/shard_map/ppermute | solution.py:36
  64.2 3.8 %collective-permute-start.9 = (bf16[16,2176]{1,0:T(8,128)(2,1)S(1)}, bf16[16,2176]{1,0:T(8,128)(2,1)S(1)}, u32[]{:S(2)}, u32[]{:S(2)}) collective-permute-start(bf16[16,2176]{1,0:T(8,128)(2,1)S(1)} %get-tuple-element.62), channel_id=1, source_target_pairs={{0,24},{4,28},{8,0},{12,4},{16,8},{20,12},{24,16},{28,20},{32,56},... | collective-permute-start | bytes 208904 | tf_op jit(solution)/shard_map/ppermute | solution.py:36
  69.3 3.7 %collective-permute-done.8 = bf16[16,2176]{1,0:T(8,128)(2,1)S(1)} collective-permute-done((bf16[16,2176]{1,0:T(8,128)(2,1)S(1)}, bf16[16,2176]{1,0:T(8,128)(2,1)S(1)}, u32[]{:S(2)}, u32[]{:S(2)}) %collective-permute-start.8) | collective-permute-done | bytes 69664 | tf_op jit(solution)/shard_map/ppermute | solution.py:36
  75.3 2.3 %collective-permute-start.16 = (bf16[1,16,2048]{2,1,0:T(8,128)(2,1)S(1)}, bf16[1,16,2048]{2,1,0:T(8,128)(2,1)S(1)}, u32[]{:S(2)}, u32[]{:S(2)}) collective-permute-start(bf16[1,16,2048]{2,1,0:T(8,128)(2,1)S(1)} %get-tuple-element.51), channel_id=1, source_target_pairs={{0,96},{4,100},{8,104},{12,108},{16,112},{20,116},{24,120},{28,124... | collective-permute-start | bytes 196616 | tf_op jit(solution)/shard_map/ppermute | solution.py:36
  79.5 2.8 %collective-permute-done.15 = bf16[1,16,2048]{2,1,0:T(8,128)(2,1)S(1)} collective-permute-done((bf16[1,16,2048]{2,1,0:T(8,128)(2,1)S(1)}, bf16[1,16,2048]{2,1,0:T(8,128)(2,1)S(1)}, u32[]{:S(2)}, u32[]{:S(2)}) %collective-permute-start.15) | collective-permute-done | bytes 65568 | tf_op jit(solution)/shard_map/ppermute | solution.py:36
  82.6 6.9 %collective-permute-start.27 = (bf16[4,16,2048]{2,1,0:T(8,128)(2,1)S(1)}, bf16[4,16,2048]{2,1,0:T(8,128)(2,1)S(1)}, u32[]{:S(2)}, u32[]{:S(2)}) collective-permute-start(bf16[4,16,2048]{2,1,0:T(8,128)(2,1)S(1)} %pad_maximum_fusion.refs_0_), channel_id=1, source_target_pairs={{0,4},{4,0},{8,12},{12,8},{16,20},{20,16},{24,28},{28,24},{32,36},... | collective-permute-start | bytes 786440 | tf_op jit(solution)/shard_map/ppermute | solution.py:36
  89.6 2.5 %collective-permute-start.19 = (bf16[4,16,2048]{2,1,0:T(8,128)(2,1)S(1)}, bf16[4,16,2048]{2,1,0:T(8,128)(2,1)S(1)}, u32[]{:S(2)}, u32[]{:S(2)}) collective-permute-start(bf16[4,16,2048]{2,1,0:T(8,128)(2,1)S(1)} %pad_maximum_fusion.refs_0_), channel_id=1, source_target_pairs={{0,24},{4,28},{8,0},{12,4},{16,8},{20,12},{24,16},{28,20},{32,56},... | collective-permute-start | bytes 786440 | tf_op jit(solution)/shard_map/ppermute | solution.py:36
  92.7 2.1 %collective-permute-start.21 = (bf16[1,16,2048]{2,1,0:T(8,128)(2,1)S(1)}, bf16[1,16,2048]{2,1,0:T(8,128)(2,1)S(1)}, u32[]{:S(2)}, u32[]{:S(2)}) collective-permute-start(bf16[1,16,2048]{2,1,0:T(8,128)(2,1)S(1)} %collective-permute-done.20), channel_id=1, source_target_pairs={{0,8},{4,12},{8,16},{12,20},{16,24},{20,28},{24,0},{28,4},{32,40},... | collective-permute-start | bytes 196616 | tf_op jit(solution)/shard_map/ppermute | solution.py:36
  94.7 13.5 %collective-permute-done.21 = bf16[1,16,2048]{2,1,0:T(8,128)(2,1)S(1)} collective-permute-done((bf16[1,16,2048]{2,1,0:T(8,128)(2,1)S(1)}, bf16[1,16,2048]{2,1,0:T(8,128)(2,1)S(1)}, u32[]{:S(2)}, u32[]{:S(2)}) %collective-permute-start.21) | collective-permute-done | bytes 65568 | tf_op jit(solution)/shard_map/ppermute | solution.py:36
  108.8 4.0 %collective-permute-done.22 = bf16[1,16,2048]{2,1,0:T(8,128)(2,1)S(1)} collective-permute-done((bf16[1,16,2048]{2,1,0:T(8,128)(2,1)S(1)}, bf16[1,16,2048]{2,1,0:T(8,128)(2,1)S(1)}, u32[]{:S(2)}, u32[]{:S(2)}) %collective-permute-start.22) | collective-permute-done | bytes 65568 | tf_op jit(solution)/shard_map/ppermute | solution.py:36
  113.0 2.9 %collective-permute-done.23 = bf16[1,16,2048]{2,1,0:T(8,128)(2,1)S(1)} collective-permute-done((bf16[1,16,2048]{2,1,0:T(8,128)(2,1)S(1)}, bf16[1,16,2048]{2,1,0:T(8,128)(2,1)S(1)}, u32[]{:S(2)}, u32[]{:S(2)}) %collective-permute-start.23) | collective-permute-done | bytes 65568 | tf_op jit(solution)/shard_map/ppermute | solution.py:36
  116.0 3.1 %collective-permute-start.31 = (bf16[4,16,2048]{2,1,0:T(8,128)(2,1)S(1)}, bf16[4,16,2048]{2,1,0:T(8,128)(2,1)S(1)}, u32[]{:S(2)}, u32[]{:S(2)}) collective-permute-start(bf16[4,16,2048]{2,1,0:T(8,128)(2,1)S(1)} %constant_dynamic-update-slice_fusion.refs_4_), channel_id=1, source_target_pairs={{0,4},{4,0},{8,12},{12,8},{16,20},{20,16},{24,28},{28,24},{32,36},... | collective-permute-start | bytes 786440 | tf_op jit(solution)/shard_map/ppermute | solution.py:36
  122.0 2.5 %collective-permute-start.36 = (s16[3,528,256]{2,1,0:T(8,128)(2,1)}, s16[3,528,256]{2,1,0:T(8,128)(2,1)S(1)}, u32[]{:S(2)}, u32[]{:S(2)}) collective-permute-start(s16[3,528,256]{2,1,0:T(8,128)(2,1)} %get-tuple-element.48), channel_id=1, source_target_pairs={{0,3},{1,0},{2,1},{3,2},{4,7},{5,4},{6,5},{7,6},{8,11},{9,8},{10,9... | collective-permute-start | bytes 2433032 | tf_op jit(solution)/shard_map/ppermute | solution.py:334
  124.6 2.3 %collective-permute-done.26.refs_7_ = bf16[4,16,2048]{2,1,0:T(8,128)(2,1)S(1)} collective-permute-done((bf16[4,16,2048]{2,1,0:T(8,128)(2,1)S(1)}, bf16[4,16,2048]{2,1,0:T(8,128)(2,1)S(1)}, u32[]{:S(2)}, u32[]{:S(2)}) %collective-permute-start.26) | collective-permute-done | bytes 262176 | tf_op jit(solution)/shard_map/ppermute | solution.py:36
  128.7 2.1 %collective-permute-start.29 = (bf16[4,16,2048]{2,1,0:T(8,128)(2,1)S(1)}, bf16[4,16,2048]{2,1,0:T(8,128)(2,1)}, u32[]{:S(2)}, u32[]{:S(2)}) collective-permute-start(bf16[4,16,2048]{2,1,0:T(8,128)(2,1)S(1)} %collective-permute-done.18.refs_2_), channel_id=1, source_target_pairs={{0,4},{4,0},{8,12},{12,8},{16,20},{20,16},{24,28},{28,24},{32,36},... | collective-permute-start | bytes 786440 | tf_op jit(solution)/shard_map/ppermute | solution.py:36
  130.8 4.3 %collective-permute-done.24.refs_5_ = bf16[4,16,2048]{2,1,0:T(8,128)(2,1)S(1)} collective-permute-done((bf16[4,16,2048]{2,1,0:T(8,128)(2,1)S(1)}, bf16[4,16,2048]{2,1,0:T(8,128)(2,1)S(1)}, u32[]{:S(2)}, u32[]{:S(2)}) %collective-permute-start.24) | collective-permute-done | bytes 262176 | tf_op jit(solution)/shard_map/ppermute | solution.py:36
  136.2 8.1 %shard_map.121 = (s16[1,528,256]{2,1,0:T(8,128)(2,1)}, s16[2,528,256]{2,1,0:T(8,128)(2,1)}, f32[1536,256]{1,0:T(8,128)}) custom-call(s32[1]{0:T(128)S(6)} %copy.16.count_ref, s32[1]{0:T(128)} %bitcast.1.mine_ref, bf16[1536,2048]{1,0:T(8,128)(2,1)} %grads_ref.2, bf16[1024,2048]{1,0:T(8,128)(2,1)} %near_ref.1, bf16[1024,2048]{1,0:T(8,128)(2,1)} %near_ref.1), custom_call_target="tpu_custom_call" | custom-call | tf_op jit(solution)/shard_map/pallas_call | solution.py:230
  151.1 3.1 %shard_map.120 = bf16[64,16,2048]{2,1,0:T(8,128)(2,1)} custom-call(s32[64]{0:T(128)S(1)} %copy-done.3, s32[1]{0:T(128)} %bitcast.me_ref, bf16[4,16,2048]{2,1,0:T(8,128)(2,1)S(1)} %pad_maximum_fusion.refs_0_, bf16[4,16,2048]{2,1,0:T(8,128)(2,1)S(1)} %collective-permute-done.17.refs_1_, bf16[4,16,2048]{2,1,0:T(8,128)(2,1)S(1)} %collective-permute-done.18.refs_2_, ...), custom_call_target="tpu_custom_call" | custom-call | tf_op jit(solution)/shard_map/pallas_call | solution.py:310
  154.2 4.3 %collective-permute-done.36.refs_1_ = s16[3,528,256]{2,1,0:T(8,128)(2,1)S(1)} collective-permute-done((s16[3,528,256]{2,1,0:T(8,128)(2,1)}, s16[3,528,256]{2,1,0:T(8,128)(2,1)S(1)}, u32[]{:S(2)}, u32[]{:S(2)}) %collective-permute-start.36) | collective-permute-done | bytes 811040 | tf_op jit(solution)/shard_map/ppermute | solution.py:334
  158.5 35.7 %collective-permute-done.37.refs_2_ = s16[1,528,256]{2,1,0:T(8,128)(2,1)S(1)} collective-permute-done((s16[1,528,256]{2,1,0:T(8,128)(2,1)}, s16[1,528,256]{2,1,0:T(8,128)(2,1)S(1)}, u32[]{:S(2)}, u32[]{:S(2)}) %collective-permute-start.37) | collective-permute-done | bytes 270368 | tf_op jit(solution)/shard_map/ppermute | solution.py:334
  194.2 1.6 shard_map.122
  (76 shorter events, 23.0 us)
Async XLA Ops:
  18.7 7.5 %collective-permute-start = (bf16[32,16,2176]{2,1,0:T(8,128)(2,1)}, bf16[32,16,2176]{2,1,0:T(8,128)(2,1)S(1)}, u32[]{:S(2)}, u32[]{:S(2)}) collective-permute-start(bf16[32,16,2176]{2,1,0:T(8,128)(2,1)} %get-tuple-element.29), channel_id=1, source_target_pairs={{0,4},{4,0},{8,12},{12,8},{16,20},{20,16},{24,28},{28,24},{32,36},... | collective-permute-start | bytes 6684680 | tf_op jit(solution)/shard_map/ppermute | solution.py:36
  28.3 7.9 %collective-permute-start.6 = (bf16[4,16,2176]{2,1,0:T(8,128)(2,1)S(1)}, bf16[4,16,2176]{2,1,0:T(8,128)(2,1)S(1)}, u32[]{:S(2)}, u32[]{:S(2)}) collective-permute-start(bf16[4,16,2176]{2,1,0:T(8,128)(2,1)S(1)} %get-tuple-element.56), channel_id=1, source_target_pairs={{0,24},{4,28},{8,0},{12,4},{16,8},{20,12},{24,16},{28,20},{32,56},... | collective-permute-start | bytes 835592 | tf_op jit(solution)/shard_map/ppermute | solution.py:36
  29.4 14.2 %collective-permute-start.5 = (bf16[4,16,2176]{2,1,0:T(8,128)(2,1)S(1)}, bf16[4,16,2176]{2,1,0:T(8,128)(2,1)S(1)}, u32[]{:S(2)}, u32[]{:S(2)}) collective-permute-start(bf16[4,16,2176]{2,1,0:T(8,128)(2,1)S(1)} %get-tuple-element.57), channel_id=1, source_target_pairs={{0,8},{4,12},{8,16},{12,20},{16,24},{20,28},{24,0},{28,4},{32,40},... | collective-permute-start | bytes 835592 | tf_op jit(solution)/shard_map/ppermute | solution.py:36
  29.9 13.8 %collective-permute-start.4 = (bf16[4,16,2176]{2,1,0:T(8,128)(2,1)S(1)}, bf16[4,16,2176]{2,1,0:T(8,128)(2,1)S(1)}, u32[]{:S(2)}, u32[]{:S(2)}) collective-permute-start(bf16[4,16,2176]{2,1,0:T(8,128)(2,1)S(1)} %get-tuple-element.58), channel_id=1, source_target_pairs={{0,16},{4,20},{8,24},{12,28},{16,0},{20,4},{24,8},{28,12},{32,48},... | collective-permute-start | bytes 835592 | tf_op jit(solution)/shard_map/ppermute | solution.py:36
  31.1 12.6 %collective-permute-start.3 = (bf16[4,16,2176]{2,1,0:T(8,128)(2,1)S(1)}, bf16[4,16,2176]{2,1,0:T(8,128)(2,1)S(1)}, u32[]{:S(2)}, u32[]{:S(2)}) collective-permute-start(bf16[4,16,2176]{2,1,0:T(8,128)(2,1)S(1)} %get-tuple-element.59), channel_id=1, source_target_pairs={{0,96},{4,100},{8,104},{12,108},{16,112},{20,116},{24,120},{28,124... | collective-permute-start | bytes 835592 | tf_op jit(solution)/shard_map/ppermute | solution.py:36
  33.5 10.1 %collective-permute-start.2 = (bf16[4,16,2176]{2,1,0:T(8,128)(2,1)S(1)}, bf16[4,16,2176]{2,1,0:T(8,128)(2,1)S(1)}, u32[]{:S(2)}, u32[]{:S(2)}) collective-permute-start(bf16[4,16,2176]{2,1,0:T(8,128)(2,1)S(1)} %get-tuple-element.60), channel_id=1, source_target_pairs={{0,32},{4,36},{8,40},{12,44},{16,48},{20,52},{24,56},{28,60},{32,6... | collective-permute-start | bytes 835592 | tf_op jit(solution)/shard_map/ppermute | solution.py:36
  36.2 13.1 %collective-permute-start.1 = (bf16[4,16,2176]{2,1,0:T(8,128)(2,1)S(1)}, bf16[4,16,2176]{2,1,0:T(8,128)(2,1)S(1)}, u32[]{:S(2)}, u32[]{:S(2)}) collective-permute-start(bf16[4,16,2176]{2,1,0:T(8,128)(2,1)S(1)} %get-tuple-element.61), channel_id=1, source_target_pairs={{0,64},{4,68},{8,72},{12,76},{16,80},{20,84},{24,88},{28,92},{32,9... | collective-permute-start | bytes 835592 | tf_op jit(solution)/shard_map/ppermute | solution.py:36
  51.9 5.1 %collective-permute-start.11 = (bf16[16,2176]{1,0:T(8,128)(2,1)S(1)}, bf16[16,2176]{1,0:T(8,128)(2,1)S(1)}, u32[]{:S(2)}, u32[]{:S(2)}) collective-permute-start(bf16[16,2176]{1,0:T(8,128)(2,1)S(1)} %get-tuple-element.66), channel_id=1, source_target_pairs={{0,32},{4,36},{8,40},{12,44},{16,48},{20,52},{24,56},{28,60},{32,6... | collective-permute-start | bytes 208904 | tf_op jit(solution)/shard_map/ppermute | solution.py:36
  51.9 5.1 %collective-permute-start.10 = (bf16[16,2176]{1,0:T(8,128)(2,1)S(1)}, bf16[16,2176]{1,0:T(8,128)(2,1)S(1)}, u32[]{:S(2)}, u32[]{:S(2)}) collective-permute-start(bf16[16,2176]{1,0:T(8,128)(2,1)S(1)} %get-tuple-element.67), channel_id=1, source_target_pairs={{0,64},{4,68},{8,72},{12,76},{16,80},{20,84},{24,88},{28,92},{32,9... | collective-permute-start | bytes 208904 | tf_op jit(solution)/shard_map/ppermute | solution.py:36
  57.1 16.0 %collective-permute-start.13 = (f32[16,2176]{1,0:T(8,128)S(1)}, f32[16,2176]{1,0:T(8,128)S(1)}, u32[]{:S(2)}, u32[]{:S(2)}) collective-permute-start(f32[16,2176]{1,0:T(8,128)S(1)} %fusion.1), channel_id=1, source_target_pairs={{0,128},{4,132},{8,136},{12,140},{16,144},{20,148},{24,152},{28,15... | collective-permute-start | bytes 417800 | tf_op jit(solution)/shard_map/ppermute | solution.py:36
  64.2 5.1 %collective-permute-start.9 = (bf16[16,2176]{1,0:T(8,128)(2,1)S(1)}, bf16[16,2176]{1,0:T(8,128)(2,1)S(1)}, u32[]{:S(2)}, u32[]{:S(2)}) collective-permute-start(bf16[16,2176]{1,0:T(8,128)(2,1)S(1)} %get-tuple-element.62), channel_id=1, source_target_pairs={{0,24},{4,28},{8,0},{12,4},{16,8},{20,12},{24,16},{28,20},{32,56},... | collective-permute-start | bytes 208904 | tf_op jit(solution)/shard_map/ppermute | solution.py:36
  68.0 5.1 %collective-permute-start.8 = (bf16[16,2176]{1,0:T(8,128)(2,1)S(1)}, bf16[16,2176]{1,0:T(8,128)(2,1)S(1)}, u32[]{:S(2)}, u32[]{:S(2)}) collective-permute-start(bf16[16,2176]{1,0:T(8,128)(2,1)S(1)} %get-tuple-element.63), channel_id=1, source_target_pairs={{0,8},{4,12},{8,16},{12,20},{16,24},{20,28},{24,0},{28,4},{32,40},... | collective-permute-start | bytes 208904 | tf_op jit(solution)/shard_map/ppermute | solution.py:36
  68.0 5.1 %collective-permute-start.7 = (bf16[16,2176]{1,0:T(8,128)(2,1)S(1)}, bf16[16,2176]{1,0:T(8,128)(2,1)S(1)}, u32[]{:S(2)}, u32[]{:S(2)}) collective-permute-start(bf16[16,2176]{1,0:T(8,128)(2,1)S(1)} %get-tuple-element.64), channel_id=1, source_target_pairs={{0,16},{4,20},{8,24},{12,28},{16,0},{20,4},{24,8},{28,12},{32,48},... | collective-permute-start | bytes 208904 | tf_op jit(solution)/shard_map/ppermute | solution.py:36
  77.6 4.7 %collective-permute-start.15 = (bf16[1,16,2048]{2,1,0:T(8,128)(2,1)S(1)}, bf16[1,16,2048]{2,1,0:T(8,128)(2,1)S(1)}, u32[]{:S(2)}, u32[]{:S(2)}) collective-permute-start(bf16[1,16,2048]{2,1,0:T(8,128)(2,1)S(1)} %get-tuple-element.51), channel_id=1, source_target_pairs={{0,64},{4,68},{8,72},{12,76},{16,80},{20,84},{24,88},{28,92},{32,9... | collective-permute-start | bytes 196616 | tf_op jit(solution)/shard_map/ppermute | solution.py:36
  77.6 5.0 %collective-permute-start.14 = (bf16[1,16,2048]{2,1,0:T(8,128)(2,1)S(1)}, bf16[1,16,2048]{2,1,0:T(8,128)(2,1)S(1)}, u32[]{:S(2)}, u32[]{:S(2)}) collective-permute-start(bf16[1,16,2048]{2,1,0:T(8,128)(2,1)S(1)} %get-tuple-element.51), channel_id=1, source_target_pairs={{0,32},{4,36},{8,40},{12,44},{16,48},{20,52},{24,56},{28,60},{32,6... | collective-permute-start | bytes 196616 | tf_op jit(solution)/shard_map/ppermute | solution.py:36
  78.2 14.5 %collective-permute-start.20 = (bf16[1,16,2048]{2,1,0:T(8,128)(2,1)S(1)}, bf16[1,16,2048]{2,1,0:T(8,128)(2,1)S(1)}, u32[]{:S(2)}, u32[]{:S(2)}) collective-permute-start(bf16[1,16,2048]{2,1,0:T(8,128)(2,1)S(1)} %get-tuple-element.51), channel_id=1, source_target_pairs={{0,128},{4,132},{8,136},{12,140},{16,144},{20,148},{24,152},{28,15... | collective-permute-start | bytes 196616 | tf_op jit(solution)/shard_map/ppermute | solution.py:36
  82.6 36.4 %collective-permute-start.27 = (bf16[4,16,2048]{2,1,0:T(8,128)(2,1)S(1)}, bf16[4,16,2048]{2,1,0:T(8,128)(2,1)S(1)}, u32[]{:S(2)}, u32[]{:S(2)}) collective-permute-start(bf16[4,16,2048]{2,1,0:T(8,128)(2,1)S(1)} %pad_maximum_fusion.refs_0_), channel_id=1, source_target_pairs={{0,4},{4,0},{8,12},{12,8},{16,20},{20,16},{24,28},{28,24},{32,36},... | collective-permute-start | bytes 786440 | tf_op jit(solution)/shard_map/ppermute | solution.py:36
  89.6 30.1 %collective-permute-start.19 = (bf16[4,16,2048]{2,1,0:T(8,128)(2,1)S(1)}, bf16[4,16,2048]{2,1,0:T(8,128)(2,1)S(1)}, u32[]{:S(2)}, u32[]{:S(2)}) collective-permute-start(bf16[4,16,2048]{2,1,0:T(8,128)(2,1)S(1)} %pad_maximum_fusion.refs_0_), channel_id=1, source_target_pairs={{0,24},{4,28},{8,0},{12,4},{16,8},{20,12},{24,16},{28,20},{32,56},... | collective-permute-start | bytes 786440 | tf_op jit(solution)/shard_map/ppermute | solution.py:36
  92.1 28.7 %collective-permute-start.18 = (bf16[4,16,2048]{2,1,0:T(8,128)(2,1)S(1)}, bf16[4,16,2048]{2,1,0:T(8,128)(2,1)S(1)}, u32[]{:S(2)}, u32[]{:S(2)}) collective-permute-start(bf16[4,16,2048]{2,1,0:T(8,128)(2,1)S(1)} %pad_maximum_fusion.refs_0_), channel_id=1, source_target_pairs={{0,16},{4,20},{8,24},{12,28},{16,0},{20,4},{24,8},{28,12},{32,48},... | collective-permute-start | bytes 786440 | tf_op jit(solution)/shard_map/ppermute | solution.py:36
  92.1 29.2 %collective-permute-start.17 = (bf16[4,16,2048]{2,1,0:T(8,128)(2,1)S(1)}, bf16[4,16,2048]{2,1,0:T(8,128)(2,1)S(1)}, u32[]{:S(2)}, u32[]{:S(2)}) collective-permute-start(bf16[4,16,2048]{2,1,0:T(8,128)(2,1)S(1)} %pad_maximum_fusion.refs_0_), channel_id=1, source_target_pairs={{0,8},{4,12},{8,16},{12,20},{16,24},{20,28},{24,0},{28,4},{32,40},... | collective-permute-start | bytes 786440 | tf_op jit(solution)/shard_map/ppermute | solution.py:36
  92.7 15.6 %collective-permute-start.21 = (bf16[1,16,2048]{2,1,0:T(8,128)(2,1)S(1)}, bf16[1,16,2048]{2,1,0:T(8,128)(2,1)S(1)}, u32[]{:S(2)}, u32[]{:S(2)}) collective-permute-start(bf16[1,16,2048]{2,1,0:T(8,128)(2,1)S(1)} %collective-permute-done.20), channel_id=1, source_target_pairs={{0,8},{4,12},{8,16},{12,20},{16,24},{20,28},{24,0},{28,4},{32,40},... | collective-permute-start | bytes 196616 | tf_op jit(solution)/shard_map/ppermute | solution.py:36
  116.0 6.0 %collective-permute-start.31 = (bf16[4,16,2048]{2,1,0:T(8,128)(2,1)S(1)}, bf16[4,16,2048]{2,1,0:T(8,128)(2,1)S(1)}, u32[]{:S(2)}, u32[]{:S(2)}) collective-permute-start(bf16[4,16,2048]{2,1,0:T(8,128)(2,1)S(1)} %constant_dynamic-update-slice_fusion.refs_4_), channel_id=1, source_target_pairs={{0,4},{4,0},{8,12},{12,8},{16,20},{20,16},{24,28},{28,24},{32,36},... | collective-permute-start | bytes 786440 | tf_op jit(solution)/shard_map/ppermute | solution.py:36
  119.1 7.8 %collective-permute-start.26 = (bf16[4,16,2048]{2,1,0:T(8,128)(2,1)S(1)}, bf16[4,16,2048]{2,1,0:T(8,128)(2,1)S(1)}, u32[]{:S(2)}, u32[]{:S(2)}) collective-permute-start(bf16[4,16,2048]{2,1,0:T(8,128)(2,1)S(1)} %constant_dynamic-update-slice_fusion.refs_4_), channel_id=1, source_target_pairs={{0,96},{4,100},{8,104},{12,108},{16,112},{20,116},{24,120},{28,124... | collective-permute-start | bytes 786440 | tf_op jit(solution)/shard_map/ppermute | solution.py:36
  119.7 9.0 %collective-permute-start.25 = (bf16[4,16,2048]{2,1,0:T(8,128)(2,1)S(1)}, bf16[4,16,2048]{2,1,0:T(8,128)(2,1)S(1)}, u32[]{:S(2)}, u32[]{:S(2)}) collective-permute-start(bf16[4,16,2048]{2,1,0:T(8,128)(2,1)S(1)} %constant_dynamic-update-slice_fusion.refs_4_), channel_id=1, source_target_pairs={{0,64},{4,68},{8,72},{12,76},{16,80},{20,84},{24,88},{28,92},{32,9... | collective-permute-start | bytes 786440 | tf_op jit(solution)/shard_map/ppermute | solution.py:36
  120.7 14.3 %collective-permute-start.24 = (bf16[4,16,2048]{2,1,0:T(8,128)(2,1)S(1)}, bf16[4,16,2048]{2,1,0:T(8,128)(2,1)S(1)}, u32[]{:S(2)}, u32[]{:S(2)}) collective-permute-start(bf16[4,16,2048]{2,1,0:T(8,128)(2,1)S(1)} %constant_dynamic-update-slice_fusion.refs_4_), channel_id=1, source_target_pairs={{0,32},{4,36},{8,40},{12,44},{16,48},{20,52},{24,56},{28,60},{32,6... | collective-permute-start | bytes 786440 | tf_op jit(solution)/shard_map/ppermute | solution.py:36
  121.3 32.9 %collective-permute-start.35 = (s16[3,528,256]{2,1,0:T(8,128)(2,1)}, s16[3,528,256]{2,1,0:T(8,128)(2,1)S(1)}, u32[]{:S(2)}, u32[]{:S(2)}) collective-permute-start(s16[3,528,256]{2,1,0:T(8,128)(2,1)} %get-tuple-element.47), channel_id=1, source_target_pairs={{0,1},{1,2},{2,3},{3,0},{4,5},{5,6},{6,7},{7,4},{8,9},{9,10},{10,1... | collective-permute-start | bytes 2433032 | tf_op jit(solution)/shard_map/ppermute | solution.py:334
  122.0 36.5 %collective-permute-start.36 = (s16[3,528,256]{2,1,0:T(8,128)(2,1)}, s16[3,528,256]{2,1,0:T(8,128)(2,1)S(1)}, u32[]{:S(2)}, u32[]{:S(2)}) collective-permute-start(s16[3,528,256]{2,1,0:T(8,128)(2,1)} %get-tuple-element.48), channel_id=1, source_target_pairs={{0,3},{1,0},{2,1},{3,2},{4,7},{5,4},{6,5},{7,6},{8,11},{9,8},{10,9... | collective-permute-start | bytes 2433032 | tf_op jit(solution)/shard_map/ppermute | solution.py:334
  126.8 17.4 %collective-permute-start.30 = (bf16[4,16,2048]{2,1,0:T(8,128)(2,1)S(1)}, bf16[4,16,2048]{2,1,0:T(8,128)(2,1)}, u32[]{:S(2)}, u32[]{:S(2)}) collective-permute-start(bf16[4,16,2048]{2,1,0:T(8,128)(2,1)S(1)} %collective-permute-done.19.refs_3_), channel_id=1, source_target_pairs={{0,4},{4,0},{8,12},{12,8},{16,20},{20,16},{24,28},{28,24},{32,36},... | collective-permute-start | bytes 786440 | tf_op jit(solution)/shard_map/ppermute | solution.py:36
  128.7 16.8 %collective-permute-start.29 = (bf16[4,16,2048]{2,1,0:T(8,128)(2,1)S(1)}, bf16[4,16,2048]{2,1,0:T(8,128)(2,1)}, u32[]{:S(2)}, u32[]{:S(2)}) collective-permute-start(bf16[4,16,2048]{2,1,0:T(8,128)(2,1)S(1)} %collective-permute-done.18.refs_2_), channel_id=1, source_target_pairs={{0,4},{4,0},{8,12},{12,8},{16,20},{20,16},{24,28},{28,24},{32,36},... | collective-permute-start | bytes 786440 | tf_op jit(solution)/shard_map/ppermute | solution.py:36
  135.7 10.1 %collective-permute-start.28 = (bf16[4,16,2048]{2,1,0:T(8,128)(2,1)S(1)}, bf16[4,16,2048]{2,1,0:T(8,128)(2,1)}, u32[]{:S(2)}, u32[]{:S(2)}) collective-permute-start(bf16[4,16,2048]{2,1,0:T(8,128)(2,1)S(1)} %collective-permute-done.17.refs_1_), channel_id=1, source_target_pairs={{0,4},{4,0},{8,12},{12,8},{16,20},{20,16},{24,28},{28,24},{32,36},... | collective-permute-start | bytes 786440 | tf_op jit(solution)/shard_map/ppermute | solution.py:36
  144.3 49.9 %collective-permute-start.38 = (s16[2,528,256]{2,1,0:T(8,128)(2,1)}, s16[2,528,256]{2,1,0:T(8,128)(2,1)S(1)}, u32[]{:S(2)}, u32[]{:S(2)}) collective-permute-start(s16[2,528,256]{2,1,0:T(8,128)(2,1)} %get-tuple-element.50), channel_id=1, source_target_pairs={{0,2},{1,3},{2,0},{3,1},{4,6},{5,7},{6,4},{7,5},{8,10},{9,11},{10,... | collective-permute-start | bytes 1622024 | tf_op jit(solution)/shard_map/ppermute | solution.py:334
  147.0 47.2 %collective-permute-start.37 = (s16[1,528,256]{2,1,0:T(8,128)(2,1)}, s16[1,528,256]{2,1,0:T(8,128)(2,1)S(1)}, u32[]{:S(2)}, u32[]{:S(2)}) collective-permute-start(s16[1,528,256]{2,1,0:T(8,128)(2,1)} %get-tuple-element.49), channel_id=1, source_target_pairs={{0,2},{1,3},{2,0},{3,1},{4,6},{5,7},{6,4},{7,5},{8,10},{9,11},{10,... | collective-permute-start | bytes 811016 | tf_op jit(solution)/shard_map/ppermute | solution.py:334
  (14 other events, 235.6 us)
